TPU v7x, 32 devices: a whole 2x2x4 slice. The times are simulated.
32 devices in a mesh: wide: 4 (over y, x), seq: 8 (over z, core).
Axes of the slice: x: 2, y: 2, z: 4, core: 2. Of those that a mesh axis runs over, the one named last changes fastest.
Arguments:
- inputs: bfloat16 [2, 4, 512, 2048], P(None, 'wide', 'seq'), may hold values from -6 to 6
- documents: int32 [2, 4, 512], P(None, 'wide'), may hold values from 0 to 10, as said below
- cotangent: bfloat16 [2, 4, 512, 2048], P(None, 'wide', 'seq'), may hold values from -6 to 6
- query_weight: bfloat16 [2048, 2048], P(('wide', 'seq')), may hold values from -0.125 to 0.125
- key_weight: bfloat16 [2048, 2048], P(('wide', 'seq')), may hold values from -0.125 to 0.125
- value_weight: bfloat16 [2048, 2048], P(('wide', 'seq')), may hold values from -0.125 to 0.125
- output_weight: bfloat16 [2048, 2048], P(('wide', 'seq')), may hold values from -0.125 to 0.125
- query_gain: bfloat16 [2048], P(('wide', 'seq')), may hold values from 0.25 to 1.75
- key_gain: bfloat16 [2048], P(('wide', 'seq')), may hold values from 0.25 to 1.75
- attention_gain: bfloat16 [2048], P(('wide', 'seq')), may hold values from 0.25 to 1.75
- gate_weight: bfloat16 [2048, 8192], P(('wide', 'seq')), may hold values from -0.125 to 0.125
- up_weight: bfloat16 [2048, 8192], P(('wide', 'seq')), may hold values from -0.125 to 0.125
- down_weight: bfloat16 [8192, 2048], P(('wide', 'seq')), may hold values from -0.0625 to 0.0625
- feed_gain: bfloat16 [2048], P(('wide', 'seq')), may hold values from 0.25 to 1.75
Outputs:
- layer_out: bfloat16 [2, 4, 512, 2048], P(None, 'wide', 'seq')
- input_grad: float32 [2, 4, 512, 2048], P(None, 'wide', 'seq')
- query_weight_grad: float32 [2048, 2048], P(('wide', 'seq'))
- key_weight_grad: float32 [2048, 2048], P(('wide', 'seq'))
- value_weight_grad: float32 [2048, 2048], P(('wide', 'seq'))
- output_weight_grad: float32 [2048, 2048], P(('wide', 'seq'))
- query_gain_grad: float32 [2048], P(('wide', 'seq'))
- key_gain_grad: float32 [2048], P(('wide', 'seq'))
- attention_gain_grad: float32 [2048], P(('wide', 'seq'))
- gate_weight_grad: float32 [2048, 8192], P(('wide', 'seq'))
- up_weight_grad: float32 [2048, 8192], P(('wide', 'seq'))
- down_weight_grad: float32 [8192, 2048], P(('wide', 'seq'))
- feed_gain_grad: float32 [2048], P(('wide', 'seq'))
Inputs may be any that keep to these rules, and one draw needn't show every extreme that they name: Along each row the numbers start at 0 and rise by 0 or 1 from one position to the next; every row holds exactly 11 documents, and one document covers positions 63 to 448.
All inputs are finite; a program needn't handle non-finite values.
Results may differ from a plain program's by a relative error of at most 0.019.
Values may be sent and summed in bfloat16 or wider, within the bound.
A program may use at most 640 MiB of HBM per device.

v0:
```python
import jax
import jax.numpy as jnp
from jax import lax
from jax.sharding import PartitionSpec as P

HEADS = 16
HEAD_DIM = 128


eps_norm = 1e-06
rope_base = 500000.0
masked_value = -1e30


def normalize(values, gain_vec):
    inverse = lax.rsqrt(jnp.mean(values * values, axis=-1, keepdims=True) + eps_norm)
    normed = values * inverse
    return (normed * gain_vec, normed, inverse)


def normalize_back(grad_out, normed, inverse, gain_vec):
    scaled = grad_out * gain_vec
    grad_in = inverse * (scaled - normed * jnp.mean(scaled * normed, axis=-1, keepdims=True))
    return (grad_in, jnp.sum(grad_out * normed, axis=0))


def rotation_tables(positions, head_dim):
    half_dim = head_dim // 2
    frequency = rope_base ** (-jnp.arange(half_dim, dtype=jnp.float32) * 2.0 / head_dim)
    angles = positions.astype(jnp.float32)[:, None] * frequency[None, :]
    return (jnp.cos(angles)[:, None, :], jnp.sin(angles)[:, None, :])


def rotate(values, cosine, sine_table):
    half_dim = values.shape[-1] // 2
    first_half = values[..., :half_dim]
    second_half = values[..., half_dim:]
    return jnp.concatenate(
        [
            first_half * cosine - second_half * sine_table,
            second_half * cosine + first_half * sine_table,
        ],
        axis=-1,
    )


def forward_fold(left, products, pieces):
    updated = []
    for member in range(len(pieces)):
        if member < products:
            updated.append(jnp.dot(left, pieces[member], preferred_element_type=jnp.float32))
        else:
            updated.append(pieces[member])
    return tuple(updated)


def backward_fold(grad_rows, pieces):
    contrib = lax.dot_general(
        grad_rows[0], pieces[0], (((1,), (1,)), ((), ())), preferred_element_type=jnp.float32
    )
    for member in range(1, len(pieces)):
        contrib = contrib + lax.dot_general(
            grad_rows[member],
            pieces[member],
            (((1,), (1,)), ((), ())),
            preferred_element_type=jnp.float32,
        )
    return contrib


def weight_terms(left_rows, right_rows):
    blocks = []
    for member in range(len(left_rows)):
        columns = left_rows[member]
        blocks.append(
            lax.dot_general(
                columns,
                right_rows[member],
                (((0,), (0,)), ((), ())),
                preferred_element_type=jnp.float32,
            )
        )
    return jnp.concatenate(blocks, axis=1)


def block_scores(queries, key_rows, query_pos, query_docs, key_docs, key_start, score_scale):
    raw_scores = (
        jnp.einsum("qhd,khd->hqk", queries, key_rows, preferred_element_type=jnp.float32)
        * score_scale
    )
    key_pos = key_start + jnp.arange(key_rows.shape[0], dtype=jnp.int32)
    allowed = (key_pos[None, :] <= query_pos[:, None]) & (key_docs[None, :] == query_docs[:, None])
    return jnp.where(allowed[None], raw_scores, masked_value)


def key_block(key_all, value_all, doc_all, number, block_len):
    begin_row = number * block_len
    return (
        lax.dynamic_slice_in_dim(key_all, begin_row, block_len, 0),
        lax.dynamic_slice_in_dim(value_all, begin_row, block_len, 0),
        lax.dynamic_slice_in_dim(doc_all, begin_row, block_len, 0),
        begin_row,
    )


def attend_forward(
    queries, key_all, value_all, query_pos, query_docs, doc_all, block_len, score_scale
):
    head_count = queries.shape[1]
    query_count = queries.shape[0]
    numbers = jnp.arange(key_all.shape[0] // block_len, dtype=jnp.int32)

    def first_pass(carried, number):
        maxima, totals = carried
        key_rows, value_rows, key_docs, begin_row = key_block(
            key_all, value_all, doc_all, number, block_len
        )
        scores = block_scores(
            queries, key_rows, query_pos, query_docs, key_docs, begin_row, score_scale
        )
        new_max = jnp.maximum(maxima, jnp.max(scores, axis=-1))
        totals = totals * jnp.exp(maxima - new_max) + jnp.sum(
            jnp.exp(scores - new_max[..., None]), axis=-1
        )
        return ((new_max, totals), None)

    initial = (
        jnp.full((head_count, query_count), masked_value, jnp.float32),
        jnp.zeros((head_count, query_count), jnp.float32),
    )
    (maxima, totals), unused = lax.scan(first_pass, initial, numbers)
    logsum = maxima + jnp.log(totals)

    def second_pass(accum_out, number):
        key_rows, value_rows, key_docs, begin_row = key_block(
            key_all, value_all, doc_all, number, block_len
        )
        scores = block_scores(
            queries, key_rows, query_pos, query_docs, key_docs, begin_row, score_scale
        )
        probability = jnp.exp(scores - logsum[..., None]).astype(jnp.bfloat16)
        return (
            accum_out
            + jnp.einsum(
                "hqk,khd->qhd", probability, value_rows, preferred_element_type=jnp.float32
            ),
            None,
        )

    accum_out, unused = lax.scan(
        second_pass, jnp.zeros((query_count, head_count, queries.shape[2]), jnp.float32), numbers
    )
    return (accum_out, logsum)


def attend_backward(
    queries,
    key_all,
    value_all,
    query_pos,
    query_docs,
    doc_all,
    block_len,
    score_scale,
    d_out,
    logsum,
    delta_row,
):
    numbers = jnp.arange(key_all.shape[0] // block_len, dtype=jnp.int32)

    def advance(grad_query, number):
        key_rows, value_rows, key_docs, begin_row = key_block(
            key_all, value_all, doc_all, number, block_len
        )
        probability = jnp.exp(
            block_scores(queries, key_rows, query_pos, query_docs, key_docs, begin_row, score_scale)
            - logsum[..., None]
        )
        d_probs = jnp.einsum("qhd,khd->hqk", d_out, value_rows, preferred_element_type=jnp.float32)
        d_scores = (probability * (d_probs - delta_row[..., None])).astype(jnp.bfloat16)
        grad_query = grad_query + jnp.einsum(
            "hqk,khd->qhd", d_scores, key_rows, preferred_element_type=jnp.float32
        )
        grad_key = jnp.einsum("hqk,qhd->khd", d_scores, queries, preferred_element_type=jnp.float32)
        grad_value = jnp.einsum(
            "hqk,qhd->khd",
            probability.astype(jnp.bfloat16),
            d_out,
            preferred_element_type=jnp.float32,
        )
        return (grad_query, (grad_key, grad_value))

    grad_query, (key_terms, value_terms) = lax.scan(
        advance, jnp.zeros(queries.shape, jnp.float32), numbers
    )
    return (grad_query, key_terms.reshape(key_all.shape), value_terms.reshape(value_all.shape))


def on_device(
    inputs,
    documents,
    cotangent,
    query_weight,
    key_weight,
    value_weight,
    output_weight,
    query_gain,
    key_gain,
    attention_gain,
    gate_weight,
    up_weight,
    down_weight,
    feed_gain,
):
    micro_count, unused, local_len, model_width = inputs.shape
    head_count = HEADS
    head_dim = HEAD_DIM
    feed_width = gate_weight.shape[1]
    total_rows = micro_count * local_len
    score_scale = head_dim ** (-0.5)
    block_len = min(512, documents.shape[2])
    flat_rows = inputs.reshape(total_rows, model_width)
    offset = lax.axis_index("seq") * local_len
    query_pos = offset + jnp.arange(local_len, dtype=jnp.int32)
    doc_rows = documents[:, 0, :]
    query_docs = lax.dynamic_slice_in_dim(doc_rows, offset, local_len, 1)
    cosine, sine_table = rotation_tables(query_pos, head_dim)
    folded_in = forward_fold(
        flat_rows,
        3,
        (
            lax.all_gather(query_weight, ("wide", "seq"), axis=0, tiled=True),
            lax.all_gather(key_weight, ("wide", "seq"), axis=0, tiled=True),
            lax.all_gather(value_weight, ("wide", "seq"), axis=0, tiled=True),
            lax.all_gather(query_gain, ("wide", "seq"), axis=0, tiled=True),
            lax.all_gather(key_gain, ("wide", "seq"), axis=0, tiled=True),
        ),
    )
    query_lin, key_lin, value_lin = (folded_in[0], folded_in[1], folded_in[2])
    gain_query = folded_in[3].astype(jnp.float32)
    gain_key = folded_in[4].astype(jnp.float32)
    query_out, query_normed, query_inverse = normalize(query_lin, gain_query)
    key_out, key_normed, key_inverse = normalize(key_lin, gain_key)
    queries = rotate(
        query_out.reshape(micro_count, local_len, head_count, head_dim), cosine, sine_table
    ).astype(jnp.bfloat16)
    key_local = rotate(
        key_out.reshape(micro_count, local_len, head_count, head_dim), cosine, sine_table
    ).astype(jnp.bfloat16)
    value_local = value_lin.astype(jnp.bfloat16).reshape(
        micro_count, local_len, head_count, head_dim
    )
    key_all, value_all = (
        lax.all_gather(key_local, "seq", axis=1, tiled=True),
        lax.all_gather(value_local, "seq", axis=1, tiled=True),
    )
    attended_parts = []
    logsums = []
    for member in range(micro_count):
        accum_out, logsum = attend_forward(
            queries[member],
            key_all[member],
            value_all[member],
            query_pos,
            query_docs[member],
            doc_rows[member],
            block_len,
            score_scale,
        )
        attended_parts.append(accum_out)
        logsums.append(logsum)
    attended = jnp.stack(attended_parts).reshape(total_rows, model_width).astype(jnp.bfloat16)
    folded_out = forward_fold(
        attended,
        1,
        (
            lax.all_gather(output_weight, ("wide", "seq"), axis=0, tiled=True),
            lax.all_gather(attention_gain, ("wide", "seq"), axis=0, tiled=True),
        ),
    )
    mixed_lin = folded_out[0]
    gain_attention = folded_out[1].astype(jnp.float32)
    mixed_out, mixed_normed, mixed_inverse = normalize(mixed_lin, gain_attention)
    hidden = flat_rows.astype(jnp.float32) + mixed_out
    hidden_low = hidden.astype(jnp.bfloat16)
    folded_feed = forward_fold(
        hidden_low,
        2,
        (
            lax.all_gather(gate_weight, ("wide", "seq"), axis=0, tiled=True),
            lax.all_gather(up_weight, ("wide", "seq"), axis=0, tiled=True),
            lax.all_gather(feed_gain, ("wide", "seq"), axis=0, tiled=True),
        ),
    )
    gate_lin, upward = (folded_feed[0], folded_feed[1])
    gain_feed = folded_feed[2].astype(jnp.float32)
    sigma = jax.nn.sigmoid(gate_lin)
    silu_gate = gate_lin * sigma
    active = (silu_gate * upward).astype(jnp.bfloat16)
    folded_down = forward_fold(
        active, 1, (lax.all_gather(down_weight, ("wide", "seq"), axis=0, tiled=True),)
    )
    down_lin = folded_down[0]
    down_out, down_normed, down_inverse = normalize(down_lin, gain_feed)
    layer_out = (
        (hidden + down_out).astype(jnp.bfloat16).reshape(micro_count, 1, local_len, model_width)
    )
    grad_out = cotangent.reshape(total_rows, model_width).astype(jnp.float32)
    d_down_float, feed_term = normalize_back(grad_out, down_normed, down_inverse, gain_feed)
    d_down = d_down_float.astype(jnp.bfloat16)
    down_grad = lax.psum_scatter(
        weight_terms((active,), (d_down,)), ("wide", "seq"), scatter_dimension=0, tiled=True
    )
    d_active = backward_fold(
        (d_down,), (lax.all_gather(down_weight, ("wide", "seq"), axis=0, tiled=True),)
    )
    d_gate = (d_active * upward * sigma * (1.0 + gate_lin * (1.0 - sigma))).astype(jnp.bfloat16)
    d_up = (d_active * silu_gate).astype(jnp.bfloat16)
    mlp_grad = lax.psum_scatter(
        weight_terms((hidden_low,), (jnp.concatenate([d_gate, d_up], axis=1),)),
        ("wide", "seq"),
        scatter_dimension=0,
        tiled=True,
    )
    feed_back = backward_fold(
        (d_gate, d_up),
        (
            lax.all_gather(gate_weight, ("wide", "seq"), axis=0, tiled=True),
            lax.all_gather(up_weight, ("wide", "seq"), axis=0, tiled=True),
        ),
    )
    d_hidden = grad_out + feed_back
    d_mixed_float, attention_term = normalize_back(
        d_hidden, mixed_normed, mixed_inverse, gain_attention
    )
    d_mixed = d_mixed_float.astype(jnp.bfloat16)
    d_attended_float = backward_fold(
        (d_mixed,), (lax.all_gather(output_weight, ("wide", "seq"), axis=0, tiled=True),)
    )
    d_attended = d_attended_float.astype(jnp.bfloat16).reshape(
        micro_count, local_len, head_count, head_dim
    )
    query_grads = []
    key_grads = []
    value_grads = []
    for member in range(micro_count):
        delta_row = jnp.einsum(
            "qhd,qhd->hq", d_attended[member].astype(jnp.float32), attended_parts[member]
        )
        grad_query, grad_key, grad_value = attend_backward(
            queries[member],
            key_all[member],
            value_all[member],
            query_pos,
            query_docs[member],
            doc_rows[member],
            block_len,
            score_scale,
            d_attended[member],
            logsums[member],
            delta_row,
        )
        query_grads.append(grad_query)
        key_grads.append(grad_key)
        value_grads.append(grad_value)
    key_sum, value_sum = (
        lax.psum_scatter(
            jnp.stack(key_grads).astype(jnp.bfloat16), "seq", scatter_dimension=1, tiled=True
        ).astype(jnp.float32),
        lax.psum_scatter(
            jnp.stack(value_grads).astype(jnp.bfloat16), "seq", scatter_dimension=1, tiled=True
        ).astype(jnp.float32),
    )
    d_queries = rotate(jnp.stack(query_grads) * score_scale, cosine, -sine_table).reshape(
        total_rows, model_width
    )
    d_keys = rotate(key_sum * score_scale, cosine, -sine_table).reshape(total_rows, model_width)
    d_query_float, query_term = normalize_back(d_queries, query_normed, query_inverse, gain_query)
    d_key_float, key_term = normalize_back(d_keys, key_normed, key_inverse, gain_key)
    d_query_lin = d_query_float.astype(jnp.bfloat16)
    d_key_lin = d_key_float.astype(jnp.bfloat16)
    d_value_lin = value_sum.reshape(total_rows, model_width).astype(jnp.bfloat16)
    stacked_lin = jnp.concatenate([d_query_lin, d_key_lin, d_value_lin], axis=1)
    attn_grad = lax.psum_scatter(
        weight_terms((flat_rows, attended), (stacked_lin, d_mixed)),
        ("wide", "seq"),
        scatter_dimension=0,
        tiled=True,
    )
    input_back = backward_fold(
        (d_query_lin, d_key_lin, d_value_lin),
        (
            lax.all_gather(query_weight, ("wide", "seq"), axis=0, tiled=True),
            lax.all_gather(key_weight, ("wide", "seq"), axis=0, tiled=True),
            lax.all_gather(value_weight, ("wide", "seq"), axis=0, tiled=True),
        ),
    )
    input_grad = (d_hidden + input_back).reshape(micro_count, 1, local_len, model_width)
    gain_grads = lax.psum_scatter(
        jnp.stack([query_term, key_term, attention_term, feed_term]),
        ("wide", "seq"),
        scatter_dimension=1,
        tiled=True,
    )
    return (
        layer_out,
        input_grad,
        attn_grad[:, :model_width],
        attn_grad[:, model_width : 2 * model_width],
        attn_grad[:, 2 * model_width : 3 * model_width],
        attn_grad[:, 3 * model_width :],
        gain_grads[0],
        gain_grads[1],
        gain_grads[2],
        mlp_grad[:, :feed_width],
        mlp_grad[:, feed_width:],
        down_grad,
        gain_grads[3],
    )


def solution(mesh):
    in_specs = (
        P(None, "wide", "seq", None),
        P(None, "wide", None),
        P(None, "wide", "seq", None),
        P(("wide", "seq"), None),
        P(("wide", "seq"), None),
        P(("wide", "seq"), None),
        P(("wide", "seq"), None),
        P(("wide", "seq")),
        P(("wide", "seq")),
        P(("wide", "seq")),
        P(("wide", "seq"), None),
        P(("wide", "seq"), None),
        P(("wide", "seq"), None),
        P(("wide", "seq")),
    )
    out_specs = (
        P(None, "wide", "seq", None),
        P(None, "wide", "seq", None),
        P(("wide", "seq"), None),
        P(("wide", "seq"), None),
        P(("wide", "seq"), None),
        P(("wide", "seq"), None),
        P(("wide", "seq")),
        P(("wide", "seq")),
        P(("wide", "seq")),
        P(("wide", "seq"), None),
        P(("wide", "seq"), None),
        P(("wide", "seq"), None),
        P(("wide", "seq")),
    )
    return jax.shard_map(
        on_device, mesh=mesh, in_specs=in_specs, out_specs=out_specs, check_vma=False
    )
```

profile of v0, /device:TPU:9, one launch (start us, length us, event | category | flops | bytes accessed | tf_op | source)
XLA Modules:
  0.0 4640.7 jit_solution(18250322991258031083)
XLA Ops:
  12.9 41.0 all-reduce.5
  54.1 36.4 all-gather.16.cloned.1.call-done
  90.5 4.9 multiply_reduce_fusion.6
  96.8 72.6 %all-gather.14.cloned.1.call-done = bf16[2048,2048]{1,0:T(8,128)(2,1)} async-done(((bf16[64,2048]{1,0:T(8,128)(2,1)}), bf16[2048,2048]{1,0:T(8,128)(2,1)}) %all-gather.14.cloned.1.call-update) | async-done | bytes 8388624 | tf_op jit(solution)/shard_map/all_gather | solution.py:232
  169.4 4.7 multiply_reduce_fusion.7
  176.2 1.4 subtract_convert_fusion
  178.7 69.7 %all-gather.10.cloned.1.call-done = bf16[2048,2048]{1,0:T(8,128)(2,1)} async-done(((bf16[64,2048]{1,0:T(8,128)(2,1)}), bf16[2048,2048]{1,0:T(8,128)(2,1)}) %all-gather.10.cloned.1.call-update) | async-done | bytes 8388624 | tf_op jit(solution)/shard_map/all_gather | solution.py:234
  248.4 4.6 fusion.26
  258.3 36.4 all-gather.18.cloned.1.call-done
  294.6 2.7 fusion.73
  301.2 41.4 all-gather.12.cloned.1.call-done
  342.5 2.3 fusion.16
  345.7 2.2 fusion.12
  350.0 73.1 %all-gather.20.cloned.1.call-done = bf16[2048,2048]{1,0:T(8,128)(2,1)} async-done(((bf16[64,2048]{1,0:T(8,128)(2,1)}), bf16[2048,2048]{1,0:T(8,128)(2,1)}) %all-gather.20.cloned.1.call-update) | async-done | bytes 8388624 | tf_op jit(solution)/shard_map/all_gather | solution.py:277
  423.1 4.9 multiply_reduce_fusion.5
  430.0 187.6 %all-gather.22.cloned.1.call-done = bf16[2048,8192]{1,0:T(8,128)(2,1)} async-done(((bf16[64,8192]{1,0:T(8,128)(2,1)}), bf16[2048,8192]{1,0:T(8,128)(2,1)}) %all-gather.22.cloned.1.call-update) | async-done | bytes 33554448 | tf_op jit(solution)/shard_map/all_gather | solution.py:290
  617.6 17.2 fusion.75
  634.8 178.8 %all-gather.24.cloned.1.call-done = bf16[2048,8192]{1,0:T(8,128)(2,1)} async-done(((bf16[64,8192]{1,0:T(8,128)(2,1)}), bf16[2048,8192]{1,0:T(8,128)(2,1)}) %all-gather.24.cloned.1.call-update) | async-done | bytes 33554448 | tf_op jit(solution)/shard_map/all_gather | solution.py:291
  813.6 20.6 multiply_convert_fusion.2
  834.1 175.4 %all-gather.26.cloned.1.call-done = bf16[8192,2048]{1,0:T(8,128)(2,1)} async-done(((bf16[256,2048]{1,0:T(8,128)(2,1)}), bf16[8192,2048]{1,0:T(8,128)(2,1)}) %all-gather.26.cloned.1.call-update) | async-done | bytes 33554448 | tf_op jit(solution)/shard_map/all_gather | solution.py:301
  1009.6 13.6 multiply_reduce_fusion.4
  1025.2 19.9 multiply_convert_fusion
  1045.2 17.4 fusion.76
  1062.6 18.1 multiply_reduce_fusion
  1080.7 2.9 multiply_convert_fusion.7
  1083.6 6.5 convolution_convert_fusion
  1097.6 2.3 pad_maximum_fusion.1
  1103.3 2.4 pad_maximum_fusion.2
  1105.7 8.0 copy.82
  1114.9 2.1 fusion.24
  1117.0 2.1 fusion.25
  1119.3 29.0 reduce-scatter.10.cloned.1.call-done
  1154.9 47.1 %fusion = f32[2048,16384]{1,0:T(8,128)} fusion(bf16[128,2048]{1,0:T(8,128)(2,1)S(1)} %copy-done.27, bf16[128,8192]{1,0:T(8,128)(2,1)} %get-tuple-element.246, bf16[128,8192]{1,0:T(8,128)(2,1)} %get-tuple-element.247), kind=kOutput, calls=%fused_computation.4 | convolution fusion | flops 8598323200 | bytes 138936320 | tf_op jit(solution)/shard_map/dot_general | solution.py:76
  1203.0 9.2 fusion.34
  1215.1 2.4 multiply_convert_fusion.5
  1218.0 20.7 convolution_bitcast_fusion
  1238.6 44.4 pad_maximum_fusion
  1283.0 61.3 %copy.104 = f32[2048,8192]{1,0:T(8,128)} copy(f32[2048,8192]{0,1:T(8,128)} %pad_maximum_fusion) | data formatting | bytes 134217728
  1344.7 1.7 copy-done.14
  1346.7 24.6 fusion.78
  1371.3 6.5 fusion.77
  1377.8 6.5 convolution_add_fusion.2
  1384.4 3.8 fusion.5
  1391.6 1824.6 %all-reduce.8.cloned.1.call-done = f32[2048,16384]{1,0:T(8,128)} async-done(((f32[2048,16384]{1,0:T(8,128)}), f32[2048,16384]{1,0:T(8,128)}) %all-reduce.8.cloned.1.call-update) | async-done | bytes 134217744
  3216.3 4.9 fusion.67
  3221.2 703.7 %reduce-scatter.16.cloned.1.call-done = f32[64,8192]{1,0:T(8,128)} async-done(((f32[2048,8192]{1,0:T(8,128)}), f32[64,8192]{1,0:T(8,128)}) %reduce-scatter.16.cloned.1.call-update) | async-done | bytes 2097168
  3924.8 2.9 fusion.68
  3927.7 705.9 %reduce-scatter.14.cloned.1.call-done = f32[256,2048]{1,0:T(8,128)} async-done(((f32[8192,2048]{1,0:T(8,128)}), f32[256,2048]{1,0:T(8,128)}) %reduce-scatter.14.cloned.1.call-update) | async-done | bytes 2097168 | tf_op jit(solution)/shard_map/reduce_scatter | solution.py:311
  (213 shorter events, 52.9 us)
Async XLA Ops:
  7.2 83.3 %all-gather.16.cloned.1.call-start = ((), (), s32[]{:S(2)}) async-start(), calls=%async_computation.8 | async-start | bytes 8650752 | tf_op jit(solution)/shard_map/all_gather | solution.py:233
  7.9 161.5 %all-gather.14.cloned.1.call-start = ((), (), s32[]{:S(2)}) async-start(), calls=%async_computation.7 | async-start | bytes 8650752 | tf_op jit(solution)/shard_map/all_gather | solution.py:232
  8.7 239.8 %all-gather.10.cloned.1.call-start = ((), (), s32[]{:S(2)}) async-start(), calls=%async_computation.5 | async-start | bytes 8650752 | tf_op jit(solution)/shard_map/all_gather | solution.py:234
  9.4 285.2 %all-gather.18.cloned.1.call-start = ((), (), s32[]{:S(2)}) async-start(), calls=%async_computation.9 | async-start | bytes 4718592 | tf_op jit(solution)/shard_map/all_gather | solution.py:254
  95.4 74.0 %copy-start.4 = (bf16[2,1,64,2048]{3,2,1,0:T(8,128)(2,1)S(1)}, bf16[2,1,64,2048]{3,2,1,0:T(8,128)(2,1)}, u32[]{:S(2)}) copy-start(bf16[2,1,64,2048]{3,2,1,0:T(8,128)(2,1)} %param.14) | copy-start | bytes 1572868
  95.5 78.7 %copy-start.44 = (f32[128]{0:T(128)}, f32[128]{0:T(128)S(1)}, u32[]{:S(2)}) copy-start(f32[128]{0:T(128)S(1)} %add_rsqrt_fusion.2) | copy-start | bytes 1540
  174.2 2.0 copy-start.46
  177.6 80.5 %copy-start.23 = (bf16[2,64,16,64]{3,1,2,0:T(8,128)(2,1)}, bf16[2,64,16,64]{3,1,2,0:T(8,128)(2,1)S(1)}, u32[]{:S(2)}) copy-start(bf16[2,64,16,64]{3,1,2,0:T(8,128)(2,1)S(1)} %get-tuple-element.273) | copy-start | bytes 786436
  178.7 163.8 %all-gather.12.cloned.1.call-start = ((), (), s32[]{:S(2)}) async-start(), calls=%async_computation.6 | async-start | bytes 4718592 | tf_op jit(solution)/shard_map/all_gather | solution.py:255
  253.1 4.2 copy-start.43
  254.2 168.9 %all-gather.20.cloned.1.call-start = ((), (), s32[]{:S(2)}) async-start(), calls=%async_computation.10 | async-start | bytes 8650752 | tf_op jit(solution)/shard_map/all_gather | solution.py:277
  254.7 362.8 %all-gather.22.cloned.1.call-start = ((), (), s32[]{:S(2)}) async-start(), calls=%async_computation.11 | async-start | bytes 34603008 | tf_op jit(solution)/shard_map/all_gather | solution.py:290
  255.5 558.1 %all-gather.24.cloned.1.call-start = ((), (), s32[]{:S(2)}) async-start(), calls=%async_computation.12 | async-start | bytes 34603008 | tf_op jit(solution)/shard_map/all_gather | solution.py:291
  256.2 753.3 %all-gather.26.cloned.1.call-start = ((), (), s32[]{:S(2)}) async-start(), calls=%async_computation.13 | async-start | bytes 34603008 | tf_op jit(solution)/shard_map/all_gather | solution.py:301
  257.0 891.3 %reduce-scatter.10.cloned.1.call-start = ((), (), s32[]{:S(2)}) async-start(), calls=%async_computation.14 | async-start | bytes 4718592 | tf_op jit(solution)/shard_map/reduce_scatter | solution.py:367
  294.6 3.4 copy-start.5
  294.6 3.4 copy-start.24
  342.5 3.2 copy-start.1
  1009.6 13.7 copy-start.28
  1045.2 17.4 copy-start.11
  1045.2 17.4 copy-start.29
  1083.6 6.5 copy-start.37
  1083.6 6.8 copy-start.34
  1083.6 7.2 copy-start.32
  1090.1 1.8 copy-start.2
  1090.1 3.0 copy-start.12
  1090.3 3.7 copy-start.38
  1090.3 4.6 copy-start.40
  1090.7 3.3 copy-start.25
  1094.0 1.9 copy-start.21
  1100.0 1.7 copy-start.39
  1100.0 112.2 %reduce-scatter.12.cloned.1.call-start = ((), (), s32[]{:S(2)}) async-start(), calls=%async_computation.15 | async-start | bytes 4718592 | tf_op jit(solution)/shard_map/reduce_scatter | solution.py:370
  1113.7 3.3 copy-start.22
  1113.7 274.5 %reduce-scatter.18.cloned.1.call-start = ((), (), s32[]{:S(2)}) async-start(), calls=%async_computation.18 | async-start | bytes 1081344
  1151.2 2.2 copy-start.16
  1151.2 1.7 copy-start.9
  1151.6 3.3 copy-start.27
  1154.8 2061.4 %all-reduce.8.cloned.1.call-start = ((), (), s32[]{:S(2)}) async-start(), calls=%async_computation.19 | async-start | bytes 268435456
  1202.0 2722.8 %reduce-scatter.16.cloned.1.call-start = ((), (), s32[]{:S(2)}) async-start(), calls=%async_computation.17 | async-start | bytes 69206016
  1212.2 5.3 copy-start.18
  1344.3 2.1 copy-start.14
  1344.3 2.3 copy-start.42
  1344.4 3289.3 %reduce-scatter.14.cloned.1.call-start = ((), (), s32[]{:S(2)}) async-start(), calls=%async_computation.16 | async-start | bytes 69206016 | tf_op jit(solution)/shard_map/reduce_scatter | solution.py:311
  1371.3 6.5 copy-start.30
  1371.3 13.1 slice-start
  1377.8 6.6 slice-start.1
  1377.8 6.6 copy-start.15
  1377.8 6.6 copy-start.36
  (17 other events, 19.7 us)
Sparse Core Ops, SparseCore 0:
  11.0 79.4 all-gather.15
  93.5 75.8 all-gather.13
  172.4 75.9 all-gather.9
  250.4 44.1 all-gather.17
  296.6 45.8 all-gather.11
  345.4 77.6 all-gather.19
  426.0 191.4 all-gather.21
  620.6 192.9 all-gather.23
  816.5 192.9 all-gather.25
  1100.1 48.0 reduce-scatter.9
  1150.6 48.1 reduce-scatter.11
  1200.8 123.8 reduce-scatter.17
  1332.3 1883.8 all-reduce.7
  3218.6 706.1 reduce-scatter.15
  3927.7 705.8 reduce-scatter.13
where the time goes:
time: 4650 us; the launch traced here: 4640 us
  waiting for transfers between devices  4140 us (89%)
  matrix products  268 us (6%)
  local copies, waits for them, and re-layouts  108 us (2%)
  other arithmetic  67.3 us (1%)
    unnamed x18, waiting for transfers between devices  2530 us
    reduce_scatter x1, waiting for transfers between devices, on_device(): lax.psum_scatter(weight_terms((active,), (d_down,)), ('wide', 'seq'), sca...  706 us
    all_gather x1, waiting for transfers between devices, on_device(): lax.all_gather(gate_weight, ('wide', 'seq'), axis=0, tiled=True)  188 us
    all_gather x1, waiting for transfers between devices, on_device(): lax.all_gather(up_weight, ('wide', 'seq'), axis=0, tiled=True)  179 us
    all_gather x1, waiting for transfers between devices, on_device(): lax.all_gather(down_weight, ('wide', 'seq'), axis=0, tiled=True)  175 us
    dot_general x4, matrix products, weight_terms(): lax.dot_general(columns, right_rows[member], (((0,), (0,)), ((), ())), pr...  102 us
  transfers between devices with their start and end apart: 15, of which 13 were waited for; matrix products, arithmetic and copies ran while one was open for 7% of the time, Pallas kernels for 0%

commit v1 on v0

v1 whole, which is shorter than its diff:
```python
import jax
import jax.numpy as jnp
from jax import lax
from jax.sharding import PartitionSpec as P

HEADS = 16
HEAD_DIM = 128
eps_norm = 1e-06
rope_base = 500000.0
masked_value = -1e30
bf16 = jnp.bfloat16
f32 = jnp.float32


def dot(a, b):
    return jnp.dot(a, b, preferred_element_type=f32)


def dot_t(a, b):
    return lax.dot_general(a, b, (((1,), (1,)), ((), ())), preferred_element_type=f32)


def t_dot(a, b):
    return lax.dot_general(a, b, (((0,), (0,)), ((), ())), preferred_element_type=f32)


def inverse_rms(values):
    return lax.rsqrt(jnp.mean(values * values, axis=-1, keepdims=True) + eps_norm)


def normalize_back(grad_out, normed, inverse, gain_vec):
    scaled = grad_out * gain_vec
    grad_in = inverse * (scaled - normed * jnp.mean(scaled * normed, axis=-1, keepdims=True))
    return grad_in, jnp.sum(grad_out * normed, axis=0)


def rotation_tables(positions):
    half_dim = HEAD_DIM // 2
    frequency = rope_base ** (-jnp.arange(half_dim, dtype=f32) * 2.0 / HEAD_DIM)
    angles = positions.astype(f32)[:, None] * frequency[None, :]
    return jnp.cos(angles)[:, None, :], jnp.sin(angles)[:, None, :]


def rotate(values, cosine, sine_table):
    half_dim = values.shape[-1] // 2
    first_half = values[..., :half_dim]
    second_half = values[..., half_dim:]
    return jnp.concatenate(
        [
            first_half * cosine - second_half * sine_table,
            second_half * cosine + first_half * sine_table,
        ],
        axis=-1,
    )


def seq_gather(block):
    return lax.all_gather(block, "seq", axis=0, tiled=True)


def seq_scatter(partial):
    return lax.psum_scatter(partial.astype(bf16), "seq", scatter_dimension=0, tiled=True).astype(f32)


def wide_gather(block):
    return lax.all_gather(block, "wide", axis=0, tiled=True)


def wide_scatter(partial):
    return lax.psum_scatter(partial.astype(bf16), "wide", scatter_dimension=0, tiled=True)


def on_device(n_w, n_s, inputs, documents, cotangent, query_weight, key_weight, value_weight, output_weight,
              query_gain, key_gain, attention_gain, gate_weight, up_weight, down_weight, feed_gain):
    micro, _, local_len, width = inputs.shape
    tokens = micro * local_len
    heads = HEADS // n_s
    cols = heads * HEAD_DIM
    row_len = documents.shape[2]
    feed = gate_weight.shape[1]
    feed_block = feed // (n_w * n_s)
    rows = query_weight.shape[0]
    scale = HEAD_DIM ** (-0.5)
    s_index = lax.axis_index("seq")

    qkv = jnp.stack([query_weight, key_weight, value_weight], axis=1).reshape(rows, 3, n_s, cols)
    qkv = jnp.moveaxis(qkv, 2, 0).reshape(n_s * rows, 3 * cols)
    qkv = lax.all_to_all(qkv, "seq", 0, 0, tiled=True)
    qkv_all = wide_gather(qkv)
    gate_up = jnp.stack([gate_weight, up_weight], axis=1).reshape(rows, 2, n_w, n_s, feed_block)
    gate_up = jnp.moveaxis(gate_up, 3, 0).reshape(n_s * rows, 2 * n_w * feed_block)
    gate_up = lax.all_to_all(gate_up, "seq", 0, 0, tiled=True)
    gate_up_all = wide_gather(gate_up)
    down_all = wide_gather(down_weight)
    n_dev = n_w * n_s
    out_perm = [(b, (b % n_w) * n_s + b // n_w) for b in range(n_dev)]
    out_all = wide_gather(lax.ppermute(output_weight, ("wide", "seq"), out_perm))

    gains = lax.all_gather(jnp.stack([query_gain, key_gain, attention_gain, feed_gain]), ("wide", "seq"), axis=1, tiled=True).astype(f32)
    own_gains = lax.dynamic_slice_in_dim(gains, s_index * cols, cols, 1)

    flat = inputs.reshape(tokens, width)
    x_all = seq_gather(flat)
    lin = dot(x_all, qkv_all)
    q_lin, k_lin, v_lin = (lin[:, i * cols:(i + 1) * cols] for i in range(3))
    sums = lax.psum(jnp.stack([jnp.sum(q_lin * q_lin, 1), jnp.sum(k_lin * k_lin, 1)]), "seq")
    inv = lax.rsqrt(sums / width + eps_norm)

    def by_row(v):
        v = v.reshape(n_s, micro, local_len, -1)
        return jnp.swapaxes(v, 0, 1).reshape(micro, row_len, heads, HEAD_DIM)

    def by_token(v):
        v = v.reshape(micro, n_s, local_len, cols)
        return jnp.swapaxes(v, 0, 1).reshape(n_s * tokens, cols)

    cosine, sine = rotation_tables(jnp.arange(row_len, dtype=jnp.int32))
    q_n = q_lin * inv[0][:, None]
    k_n = k_lin * inv[1][:, None]
    queries = rotate(by_row(q_n * own_gains[0]), cosine, sine).astype(bf16)
    keys = rotate(by_row(k_n * own_gains[1]), cosine, sine).astype(bf16)
    values = by_row(v_lin).astype(bf16)
    docs = documents[:, 0, :]
    pos = jnp.arange(row_len)
    allowed = (pos[None, :] <= pos[:, None])[None] & (docs[:, None, :] == docs[:, :, None])
    scores = jnp.einsum("mqhd,mkhd->mhqk", queries, keys, preferred_element_type=f32) * scale
    scores = jnp.where(allowed[:, None], scores, masked_value)
    top = jnp.max(scores, -1, keepdims=True)
    e = jnp.exp(scores - top)
    probs = e / jnp.sum(e, -1, keepdims=True)
    probs_low = probs.astype(bf16)
    attended = by_token(jnp.einsum("mhqk,mkhd->mqhd", probs_low, values, preferred_element_type=f32)).astype(bf16)

    mixed = seq_scatter(dot(attended, out_all))
    mixed_inv = inverse_rms(mixed)
    mixed_n = mixed * mixed_inv
    hidden = flat.astype(f32) + mixed_n * gains[2]
    hidden_all = seq_gather(hidden.astype(bf16))
    gate_up_lin = dot(hidden_all, gate_up_all)
    half = n_w * feed_block
    gate_lin, upward = gate_up_lin[:, :half], gate_up_lin[:, half:]
    sigma = jax.nn.sigmoid(gate_lin)
    silu_gate = gate_lin * sigma
    active = (silu_gate * upward).astype(bf16)
    down = seq_scatter(dot(active, down_all))
    down_inv = inverse_rms(down)
    down_n = down * down_inv
    layer_out = (hidden + down_n * gains[3]).astype(bf16).reshape(inputs.shape)

    grad_out = cotangent.reshape(tokens, width).astype(f32)
    d_down, feed_term = normalize_back(grad_out, down_n, down_inv, gains[3])
    d_down_all = seq_gather(d_down.astype(bf16))
    down_grad = wide_scatter(t_dot(active, d_down_all)).astype(f32)
    d_active = dot_t(d_down_all, down_all)
    d_gate = (d_active * upward * sigma * (1.0 + gate_lin * (1.0 - sigma))).astype(bf16)
    d_up = (d_active * silu_gate).astype(bf16)
    d_gate_up = jnp.concatenate([d_gate, d_up], axis=1)
    mlp_grad = wide_scatter(t_dot(hidden_all, d_gate_up))
    d_hidden = grad_out + seq_scatter(dot_t(d_gate_up, gate_up_all))
    d_mixed, attention_term = normalize_back(d_hidden, mixed_n, mixed_inv, gains[2])
    d_mixed_all = seq_gather(d_mixed.astype(bf16))
    out_grad = wide_scatter(t_dot(attended, d_mixed_all))
    d_attended = by_row(dot_t(d_mixed_all, out_all)).astype(bf16)

    d_probs = jnp.einsum("mqhd,mkhd->mhqk", d_attended, values, preferred_element_type=f32)
    delta = jnp.sum(probs * d_probs, -1, keepdims=True)
    d_scores = (probs * (d_probs - delta)).astype(bf16)
    d_q = jnp.einsum("mhqk,mkhd->mqhd", d_scores, keys, preferred_element_type=f32) * scale
    d_k = jnp.einsum("mhqk,mqhd->mkhd", d_scores, queries, preferred_element_type=f32) * scale
    d_v = jnp.einsum("mhqk,mqhd->mkhd", probs_low, d_attended, preferred_element_type=f32)
    d_q = by_token(rotate(d_q, cosine, -sine))
    d_k = by_token(rotate(d_k, cosine, -sine))
    d_qg = d_q * own_gains[0]
    d_kg = d_k * own_gains[1]
    means = lax.psum(jnp.stack([jnp.sum(d_qg * q_n, 1), jnp.sum(d_kg * k_n, 1)]), "seq") / width
    query_term = jnp.sum(d_q * q_n, 0)
    key_term = jnp.sum(d_k * k_n, 0)
    d_q_lin = (inv[0][:, None] * (d_qg - q_n * means[0][:, None])).astype(bf16)
    d_k_lin = (inv[1][:, None] * (d_kg - k_n * means[1][:, None])).astype(bf16)
    d_lin = jnp.concatenate([d_q_lin, d_k_lin, by_token(d_v).astype(bf16)], axis=1)
    input_back = seq_scatter(dot_t(d_lin, qkv_all))
    input_grad = (d_hidden + input_back).reshape(inputs.shape)
    qkv_grad = wide_scatter(t_dot(x_all, d_lin))

    qkv_grad = lax.all_to_all(qkv_grad, "seq", 0, 0, tiled=True).reshape(n_s, rows, 3, cols)
    qkv_grad = jnp.moveaxis(qkv_grad, 0, 2).reshape(rows, 3, width).astype(f32)
    mlp_grad = lax.all_to_all(mlp_grad, "seq", 0, 0, tiled=True).reshape(n_s, rows, 2, n_w, feed_block)
    mlp_grad = jnp.moveaxis(mlp_grad, 0, 3).reshape(rows, 2, feed).astype(f32)
    out_grad = lax.ppermute(out_grad, ("wide", "seq"), [(b, a) for a, b in out_perm]).astype(f32)

    zero = jnp.zeros((width,), f32)
    terms = jnp.stack([
        lax.dynamic_update_slice_in_dim(zero, query_term, s_index * cols, 0),
        lax.dynamic_update_slice_in_dim(zero, key_term, s_index * cols, 0),
        attention_term,
        feed_term,
    ])
    gain_grads = lax.psum_scatter(terms, ("wide", "seq"), scatter_dimension=1, tiled=True)
    return (layer_out, input_grad, qkv_grad[:, 0], qkv_grad[:, 1], qkv_grad[:, 2], out_grad,
            gain_grads[0], gain_grads[1], gain_grads[2], mlp_grad[:, 0], mlp_grad[:, 1], down_grad, gain_grads[3])


def solution(mesh):
    tok = P(None, "wide", "seq", None)
    docs = P(None, "wide", None)
    mat = P(("wide", "seq"), None)
    vec = P(("wide", "seq"))

    def body(*args):
        return on_device(mesh.shape["wide"], mesh.shape["seq"], *args)

    return jax.shard_map(
        body, mesh=mesh,
        in_specs=(tok, docs, tok, mat, mat, mat, mat, vec, vec, vec, mat, mat, mat, vec),
        out_specs=(tok, tok, mat, mat, mat, mat, vec, vec, vec, mat, mat, mat, vec),
        check_vma=False,
    )
```

time: 4650 us -> 1170 us (0.25)
  waiting for transfers between devices: 4140 us -> 663 us
  matrix products: 268 us -> 122 us
  blocking collectives: 41 us -> 175 us
    unnamed x18, waiting for transfers between devices: 2530 us -> 126 us
    all_gather x9 -> x8, waiting for transfers between devices: 871 us -> 286 us  [the longest x4 165 us: seq_gather(): return lax.all_gather(block, 'seq', axis=0, tiled=True)]
    reduce_scatter x3 -> x8, waiting for transfers between devices: 735 us -> 227 us  [the longest x4 125 us: seq_scatter(): lax.psum_scatter(partial.astype(bf16), 'seq', scatter_dimension=0, tiled=...]
    dot_general x30 -> x17, matrix products: 268 us -> 116 us  [the longest x4 36 us: dot_t(): lax.dot_general(a, b, (((1,), (1,)), ((), ())), preferred_element_type=f32)]
    all_to_all x0 -> x2, blocking collectives: none -> 105 us  [the longest x1 81.1 us: on_device(): gate_up = lax.all_to_all(gate_up, 'seq', 0, 0, tiled=True)]
    unnamed x121 -> x59, local copies, waits for them, and re-layouts: 85.8 us -> 16.3 us
    all_gather x0 -> x1, blocking collectives: none -> 47.4 us  [on_device(): lax.all_gather(jnp.stack([query_gain, key_gain, attention_gain, feed_gain...]
  transfers between devices with their start and end apart: 15 -> 21, of which waited for: 13 -> 15; matrix products, arithmetic and copies ran while one was open for 7% -> 18% of each run, Pallas kernels for 0% -> 0%
where the time goes in v1:
time: 1170 us
  waiting for transfers between devices  663 us (57%)
  blocking collectives  175 us (15%)
  matrix products  122 us (10%)
  local copies, waits for them, and re-layouts  120 us (10%)
  other arithmetic  43.5 us (4%)
  starting transfers between devices  28.4 us (2%)
  between operations  14.8 us (1%)
    all_gather x4, waiting for transfers between devices, seq_gather(): return lax.all_gather(block, 'seq', axis=0, tiled=True)  165 us
    unnamed x18, waiting for transfers between devices  126 us
    reduce_scatter x4, waiting for transfers between devices, seq_scatter(): lax.psum_scatter(partial.astype(bf16), 'seq', scatter_dimension=0, tiled=...  125 us
    all_gather x4, waiting for transfers between devices, wide_gather(): return lax.all_gather(block, 'wide', axis=0, tiled=True)  120 us
    reduce_scatter x4, waiting for transfers between devices, wide_scatter(): lax.psum_scatter(partial.astype(bf16), 'wide', scatter_dimension=0, tiled...  102 us
    all_to_all x1, blocking collectives, on_device(): gate_up = lax.all_to_all(gate_up, 'seq', 0, 0, tiled=True)  81.1 us
    all_gather x1, blocking collectives, on_device(): lax.all_gather(jnp.stack([query_gain, key_gain, attention_gain, feed_gain...  47.4 us
    dot_general x4, matrix products, dot_t(): lax.dot_general(a, b, (((1,), (1,)), ((), ())), preferred_element_type=f32)  36 us
  transfers between devices with their start and end apart: 21, of which 15 were waited for; matrix products, arithmetic and copies ran while one was open for 18% of the time, Pallas kernels for 0%

profile of v1, /device:TPU:9, one launch (start us, length us, event | category | flops | bytes accessed | tf_op | source)
XLA Modules:
  0.0 1166.1 jit_solution(8451970106977896269)
XLA Ops:
  14.3 23.4 %all_to_all.42 = bf16[8,64,768]{2,1,0:T(8,128)(2,1)} all-to-all(bf16[8,64,768]{2,1,0:T(8,128)(2,1)S(1)} %all_to_all.28), channel_id=1, replica_groups=mesh['wide'=4,'seq'=8] {'seq'}, dimensions={0} | all-to-all | bytes 1572864 | tf_op jit(solution)/shard_map/all_to_all | solution.py:88
  38.5 6.9 collective-permute-start
  45.5 47.4 %all-gather = bf16[32,64,4]{1,2,0:T(4,128)(2,1)S(1)} all-gather(bf16[1,64,4]{1,2,0:T(4,128)(2,1)S(1)} %maximum_bitcast_fusion.2), channel_id=1, replica_groups=mesh['wide'=4,'seq'=8] {'wide','seq'}, dimensions={0}, use_global_device_ids=true | all-gather | bytes 16896 | tf_op jit(solution)/shard_map/all_gather | solution.py:99
  97.0 40.1 %all-gather.12.cloned.1.call-done = bf16[1024,2048]{1,0:T(8,128)(2,1)} async-done(((bf16[128,2048]{1,0:T(8,128)(2,1)}), bf16[1024,2048]{1,0:T(8,128)(2,1)}) %all-gather.12.cloned.1.call-update) | async-done | bytes 4194320 | tf_op jit(solution)/shard_map/all_gather | solution.py:58
  137.1 6.2 convolution_bitcast_fusion
  144.5 11.6 psum.14
  178.6 4.5 fusion.50
  184.9 5.7 fusion.57
  190.6 3.7 fusion.17
  200.4 4.6 convolution_convert_fusion.2
  210.7 4.4 all_to_all.31
  215.1 81.1 %all_to_all.43 = bf16[8,64,2048]{2,1,0:T(8,128)(2,1)} all-to-all(bf16[8,64,2048]{2,1,0:T(8,128)(2,1)} %all_to_all.31), channel_id=1, replica_groups=mesh['wide'=4,'seq'=8] {'seq'}, dimensions={0} | all-to-all | bytes 4194304 | tf_op jit(solution)/shard_map/all_to_all | solution.py:92
  296.3 5.3 reduce-scatter.12.cloned.1.call-done
  305.9 84.2 %all-gather.18.cloned.1.call-done = bf16[2048,2048]{1,0:T(8,128)(2,1)} async-done(((bf16[512,2048]{1,0:T(8,128)(2,1)}), bf16[2048,2048]{1,0:T(8,128)(2,1)}) %all-gather.18.cloned.1.call-update) | async-done | bytes 8388624 | tf_op jit(solution)/shard_map/all_gather | solution.py:66
  390.1 48.1 %all-gather.16.cloned.1.call-done = bf16[1024,2048]{1,0:T(8,128)(2,1)} async-done(((bf16[128,2048]{1,0:T(8,128)(2,1)}), bf16[1024,2048]{1,0:T(8,128)(2,1)}) %all-gather.16.cloned.1.call-update) | async-done | bytes 4194320 | tf_op jit(solution)/shard_map/all_gather | solution.py:58
  438.2 12.5 %fusion.58 = f32[1024,2048]{1,0:T(8,128)S(1)} fusion(bf16[1024,2048]{1,0:T(8,128)(2,1)} %all-gather.16.cloned.1.call-done, bf16[2048,2048]{1,0:T(8,128)(2,1)} %all-gather.18.cloned.1.call-done), kind=kOutput, calls=%fused_computation.143 | convolution fusion | flops 8589934592 | bytes 20971520 | tf_op jit(solution)/shard_map/dot_general | solution.py:16
  450.7 3.2 copy-done.1
  456.7 36.0 %all-gather.20.cloned.1.call-done = bf16[1024,2048]{1,0:T(8,128)(2,1)} async-done(((bf16[256,2048]{1,0:T(8,128)(2,1)}), bf16[1024,2048]{1,0:T(8,128)(2,1)}) %all-gather.20.cloned.1.call-update) | async-done | bytes 4194320 | tf_op jit(solution)/shard_map/all_gather | solution.py:66
  492.6 9.3 convolution_convert_fusion.5
  502.4 48.2 %reduce-scatter.14.cloned.1.call-done = bf16[128,2048]{1,0:T(8,128)(2,1)} async-done(((bf16[1024,2048]{1,0:T(8,128)(2,1)}), bf16[128,2048]{1,0:T(8,128)(2,1)}) %reduce-scatter.14.cloned.1.call-update) | async-done | bytes 524304 | tf_op jit(solution)/shard_map/reduce_scatter | solution.py:62
  555.9 45.8 %all-gather.22.cloned.1.call-done = bf16[1024,2048]{1,0:T(8,128)(2,1)} async-done(((bf16[128,2048]{1,0:T(8,128)(2,1)}), bf16[1024,2048]{1,0:T(8,128)(2,1)}) %all-gather.22.cloned.1.call-update) | async-done | bytes 4194320 | tf_op jit(solution)/shard_map/all_gather | solution.py:58
  601.7 11.7 multiply_convert_fusion.2
  615.3 12.6 %convolution_convert_fusion.1 = bf16[1024,2048]{1,0:T(8,128)(2,1)} fusion(bf16[2048,2048]{1,0:T(8,128)(2,1)} %all-gather.18.cloned.1.call-done, bf16[1024,1024]{1,0:T(8,128)(2,1)S(1)} %get-tuple-element.104, bf16[1024,1024]{1,0:T(8,128)(2,1)S(1)} %get-tuple-element.103), kind=kOutput, calls=%fused_computation.13 | convolution fusion | flops 8600420352 | bytes 16777216 | tf_op jit(solution)/shard_map/dot_general | solution.py:20
  628.0 48.4 %reduce-scatter.16.cloned.1.call-done = bf16[128,2048]{1,0:T(8,128)(2,1)} async-done(((bf16[1024,2048]{1,0:T(8,128)(2,1)}), bf16[128,2048]{1,0:T(8,128)(2,1)}) %reduce-scatter.16.cloned.1.call-update) | async-done | bytes 524304 | tf_op jit(solution)/shard_map/reduce_scatter | solution.py:62
  678.3 3.3 fusion.25
  681.8 14.0 %convolution_convert_fusion = bf16[2048,2048]{1,0:T(8,128)(2,1)} fusion(bf16[1024,2048]{1,0:T(8,128)(2,1)} %all-gather.16.cloned.1.call-done, bf16[1024,1024]{1,0:T(8,128)(2,1)} %copy-done.23, bf16[1024,1024]{1,0:T(8,128)(2,1)} %copy-done.22), kind=kOutput, calls=%fused_computation.1 | convolution fusion | flops 8602517504 | bytes 16777216 | tf_op jit(solution)/shard_map/dot_general | solution.py:24
  696.0 31.5 %all-gather.24.cloned.1.call-done = bf16[1024,2048]{1,0:T(8,128)(2,1)} async-done(((bf16[128,2048]{1,0:T(8,128)(2,1)}), bf16[1024,2048]{1,0:T(8,128)(2,1)}) %all-gather.24.cloned.1.call-update) | async-done | bytes 4194320 | tf_op jit(solution)/shard_map/all_gather | solution.py:58
  727.5 4.6 convolution_convert_fusion.7
  732.1 9.3 convolution_convert_fusion.4
  741.6 4.0 convolution_convert_fusion.10
  750.6 3.6 multiply_reduce_fusion
  785.8 4.0 fusion.18
  797.9 11.0 psum.15
  812.4 6.2 fusion.3
  818.7 7.7 convolution_convert_fusion.3
  826.4 9.2 all-to-all-start.3
  835.6 11.9 %reduce-scatter.22.cloned.1.call-done = bf16[64,2048]{1,0:T(8,128)(2,1)} async-done(((bf16[256,2048]{1,0:T(8,128)(2,1)}), bf16[64,2048]{1,0:T(8,128)(2,1)}) %reduce-scatter.22.cloned.1.call-update) | async-done | bytes 262160 | tf_op jit(solution)/shard_map/reduce_scatter | solution.py:70
  847.5 4.6 collective-permute-start.1
  852.1 56.5 %reduce-scatter.26.cloned.1.call-done = bf16[256,2048]{1,0:T(8,128)(2,1)} async-done(((bf16[1024,2048]{1,0:T(8,128)(2,1)}), bf16[256,2048]{1,0:T(8,128)(2,1)}) %reduce-scatter.26.cloned.1.call-update) | async-done | bytes 1048592 | tf_op jit(solution)/shard_map/reduce_scatter | solution.py:70
  911.4 124.2 %reduce-scatter.28.cloned.1.call-done = f32[64,4]{1,0:T(8,128)} async-done(((f32[2048,4]{1,0:T(8,128)}), f32[64,4]{1,0:T(8,128)}) %reduce-scatter.28.cloned.1.call-update) | async-done | bytes 1040
  1039.9 4.5 reshape.272
  1044.3 6.6 copy.333
  1050.9 5.0 reshape.270
  1055.9 33.5 %reduce-scatter.20.cloned.1.call-done = bf16[512,768]{0,1:T(8,128)(2,1)} async-done(((bf16[2048,768]{0,1:T(8,128)(2,1)}), bf16[512,768]{0,1:T(8,128)(2,1)}) %reduce-scatter.20.cloned.1.call-update) | async-done | bytes 786448 | tf_op jit(solution)/shard_map/reduce_scatter | solution.py:70
  1091.7 6.0 all-to-all-start.2
  1097.7 4.8 slice_bitcast_fusion
  1102.5 24.3 %all-to-all-done.2 = bf16[8,64,768]{2,1,0:T(8,128)(2,1)} async-done(((bf16[8,64,768]{2,1,0:T(8,128)(2,1)}), bf16[8,64,768]{2,1,0:T(8,128)(2,1)}, u32[]{:S(2)}, u32[]{:S(2)}) %all-to-all-start.2) | async-done | bytes 786464 | tf_op jit(solution)/shard_map/all_to_all | solution.py:185
  1134.1 23.1 %reduce-scatter.18.cloned.1.call-done = bf16[128,2048]{1,0:T(8,128)(2,1)} async-done(((bf16[1024,2048]{1,0:T(8,128)(2,1)}), bf16[128,2048]{1,0:T(8,128)(2,1)}) %reduce-scatter.18.cloned.1.call-update) | async-done | bytes 524304 | tf_op jit(solution)/shard_map/reduce_scatter | solution.py:62
  (187 shorter events, 132.9 us)
Async XLA Ops:
  7.2 89.9 %all-gather.10.cloned.1.call-start = ((), (), s32[]{:S(2)}) async-start(), calls=%async_computation.13 | async-start | bytes 3932160 | tf_op jit(solution)/shard_map/all_gather | solution.py:66
  11.1 34.4 %copy-start.17 = (bf16[64]{0:T(256)(128)(2,1)S(1)}, bf16[64]{0:T(256)(128)(2,1)}, u32[]{:S(2)}) copy-start(bf16[64]{0:T(256)(128)(2,1)} %param.27) | copy-start | bytes 388
  11.1 34.4 %copy-start.18 = (bf16[64]{0:T(256)(128)(2,1)S(1)}, bf16[64]{0:T(256)(128)(2,1)}, u32[]{:S(2)}) copy-start(bf16[64]{0:T(256)(128)(2,1)} %param.23) | copy-start | bytes 388
  11.1 34.4 %copy-start.19 = (bf16[64]{0:T(256)(128)(2,1)S(1)}, bf16[64]{0:T(256)(128)(2,1)}, u32[]{:S(2)}) copy-start(bf16[64]{0:T(256)(128)(2,1)} %param.22) | copy-start | bytes 388
  11.1 34.3 %copy-start.20 = (bf16[64]{0:T(256)(128)(2,1)S(1)}, bf16[64]{0:T(256)(128)(2,1)}, u32[]{:S(2)}) copy-start(bf16[64]{0:T(256)(128)(2,1)} %param.21) | copy-start | bytes 388
  11.5 83.4 %copy-start.16 = (s32[2,1,512]{2,1,0:T(1,128)S(1)}, s32[2,1,512]{2,1,0:T(1,128)}, u32[]{:S(2)}) copy-start(s32[2,1,512]{2,1,0:T(1,128)} %param.15) | copy-start | bytes 12292
  37.7 99.4 %all-gather.12.cloned.1.call-start = ((), (), s32[]{:S(2)}) async-start(), calls=%async_computation.14 | async-start | bytes 4718592 | tf_op jit(solution)/shard_map/all_gather | solution.py:58
  38.5 161.9 %all-gather.14.cloned.1.call-start = ((), (), s32[]{:S(2)}) async-start(), calls=%async_computation.15 | async-start | bytes 1310720 | tf_op jit(solution)/shard_map/all_gather | solution.py:66
  38.5 57.7 %collective-permute-start = (bf16[64,2048]{1,0:T(8,128)(2,1)}, bf16[64,2048]{1,0:T(8,128)(2,1)S(1)}, u32[]{:S(2)}, u32[]{:S(2)}) collective-permute-start(bf16[64,2048]{1,0:T(8,128)(2,1)} %param.20), channel_id=1, source_target_pairs={{0,0},{1,8},{2,16},{3,24},{4,1},{5,9},{6,17},{7,25},{8,2},{9,10},{... | collective-permute-start | bytes 786440 | tf_op jit(solution)/shard_map/ppermute | solution.py:97
  96.2 0.7 copy-start.15
  97.0 204.6 %reduce-scatter.12.cloned.1.call-start = ((), (), s32[]{:S(2)}) async-start(), calls=%async_computation.16 | async-start | bytes 4718592 | tf_op jit(solution)/shard_map/reduce_scatter | solution.py:62
  178.6 4.5 copy-start.10
  205.0 185.1 %all-gather.18.cloned.1.call-start = ((), (), s32[]{:S(2)}) async-start(), calls=%async_computation.18 | async-start | bytes 10485760 | tf_op jit(solution)/shard_map/all_gather | solution.py:66
  205.3 2.0 copy-start.8
  296.3 142.0 %all-gather.16.cloned.1.call-start = ((), (), s32[]{:S(2)}) async-start(), calls=%async_computation.17 | async-start | bytes 4718592 | tf_op jit(solution)/shard_map/all_gather | solution.py:58
  305.1 187.5 %all-gather.20.cloned.1.call-start = ((), (), s32[]{:S(2)}) async-start(), calls=%async_computation.19 | async-start | bytes 5242880 | tf_op jit(solution)/shard_map/all_gather | solution.py:66
  305.9 244.7 %reduce-scatter.14.cloned.1.call-start = ((), (), s32[]{:S(2)}) async-start(), calls=%async_computation.20 | async-start | bytes 4718592 | tf_op jit(solution)/shard_map/reduce_scatter | solution.py:62
  450.7 3.2 copy-start.1
  501.9 99.7 %all-gather.22.cloned.1.call-start = ((), (), s32[]{:S(2)}) async-start(), calls=%async_computation.21 | async-start | bytes 4718592 | tf_op jit(solution)/shard_map/all_gather | solution.py:58
  555.8 120.7 %reduce-scatter.16.cloned.1.call-start = ((), (), s32[]{:S(2)}) async-start(), calls=%async_computation.22 | async-start | bytes 4718592 | tf_op jit(solution)/shard_map/reduce_scatter | solution.py:62
  613.3 1.3 copy-start.22
  613.3 2.0 copy-start.23
  628.0 99.5 %all-gather.24.cloned.1.call-start = ((), (), s32[]{:S(2)}) async-start(), calls=%async_computation.23 | async-start | bytes 4718592 | tf_op jit(solution)/shard_map/all_gather | solution.py:58
  681.6 144.8 %reduce-scatter.24.cloned.1.call-start = ((), (), s32[]{:S(2)}) async-start(), calls=%async_computation.27 | async-start | bytes 10485760 | tf_op jit(solution)/shard_map/reduce_scatter | solution.py:70
  695.9 151.6 %reduce-scatter.22.cloned.1.call-start = ((), (), s32[]{:S(2)}) async-start(), calls=%async_computation.26 | async-start | bytes 1310720 | tf_op jit(solution)/shard_map/reduce_scatter | solution.py:70
  732.1 176.6 %reduce-scatter.26.cloned.1.call-start = ((), (), s32[]{:S(2)}) async-start(), calls=%async_computation.28 | async-start | bytes 5242880 | tf_op jit(solution)/shard_map/reduce_scatter | solution.py:70
  741.5 294.2 %reduce-scatter.28.cloned.1.call-start = ((), (), s32[]{:S(2)}) async-start(), calls=%async_computation.29 | async-start | bytes 1081344
  750.6 4.1 copy-start.3
  754.7 1.2 copy-start.6
  754.7 1.2 copy-start.7
  755.9 1.0 copy-start.4
  755.9 1.2 copy-start.5
  756.0 2.3 copy-start.9
  809.0 280.4 %reduce-scatter.20.cloned.1.call-start = ((), (), s32[]{:S(2)}) async-start(), calls=%async_computation.25 | async-start | bytes 3932160 | tf_op jit(solution)/shard_map/reduce_scatter | solution.py:70
  809.3 3.1 copy-start.13
  809.3 3.1 copy-start.21
  811.4 0.8 copy-start.11
  811.4 1.0 copy-start.12
  812.4 6.3 copy-start.14
  818.6 338.6 %reduce-scatter.18.cloned.1.call-start = ((), (), s32[]{:S(2)}) async-start(), calls=%async_computation.24 | async-start | bytes 4718592 | tf_op jit(solution)/shard_map/reduce_scatter | solution.py:62
  826.4 213.4 %all-to-all-start.3 = ((bf16[8,64,2048]{2,1,0:T(8,128)(2,1)}), bf16[8,64,2048]{2,1,0:T(8,128)(2,1)S(1)}, u32[]{:S(2)}, u32[]{:S(2)}) async-start(bf16[8,64,2048]{2,1,0:T(8,128)(2,1)} %bitcast.187), calls=%async_computation.10 | async-start | bytes 4194304 | tf_op jit(solution)/shard_map/all_to_all | solution.py:187
  847.5 191.5 %collective-permute-start.1 = (bf16[64,2048]{1,0:T(8,128)(2,1)}, bf16[64,2048]{1,0:T(8,128)(2,1)S(1)}, u32[]{:S(2)}, u32[]{:S(2)}) collective-permute-start(bf16[64,2048]{1,0:T(8,128)(2,1)} %reduce-scatter.22.cloned.1.call-done), channel_id=1, source_target_pairs={{0,0},{8,1},{16,2},{24,3},{1,4},{9,5},{17,6},{25,7},{2,8},{10,9},{... | collective-permute-start | bytes 786440 | tf_op jit(solution)/shard_map/ppermute | solution.py:189
  1091.7 35.1 %all-to-all-start.2 = ((bf16[8,64,768]{2,1,0:T(8,128)(2,1)}), bf16[8,64,768]{2,1,0:T(8,128)(2,1)}, u32[]{:S(2)}, u32[]{:S(2)}) async-start(bf16[8,64,768]{2,1,0:T(8,128)(2,1)} %bitcast.53), calls=%async_computation.7 | async-start | bytes 1572864 | tf_op jit(solution)/shard_map/all_to_all | solution.py:185
  1129.3 27.9 %copy-start = (bf16[2,1,64,2048]{3,2,1,0:T(8,128)(2,1)S(1)}, bf16[2,1,64,2048]{3,2,1,0:T(8,128)(2,1)}, u32[]{:S(2)}) copy-start(bf16[2,1,64,2048]{3,2,1,0:T(8,128)(2,1)} %param.16) | copy-start | bytes 1572868
  1129.3 27.9 %copy-start.2 = (bf16[128,2048]{1,0:T(8,128)(2,1)S(1)}, bf16[128,2048]{1,0:T(8,128)(2,1)}, u32[]{:S(2)}) copy-start(bf16[128,2048]{1,0:T(8,128)(2,1)} %reduce-scatter.16.cloned.1.call-done) | copy-start | bytes 1572868
Sparse Core Ops, SparseCore 0:
  37.8 51.5 all-gather.9
  91.0 46.0 all-gather.11
  139.6 26.4 all-gather.13
  205.2 96.3 reduce-scatter.11
  303.3 86.7 all-gather.17
  392.2 46.0 all-gather.15
  440.1 52.5 all-gather.19
  502.0 48.4 reduce-scatter.13
  556.0 45.6 all-gather.21
  628.1 48.3 reduce-scatter.15
  681.7 45.6 all-gather.23
  730.4 86.2 reduce-scatter.23
  819.8 27.7 reduce-scatter.21
  850.4 58.2 reduce-scatter.25
  911.4 124.2 reduce-scatter.27
  1038.5 50.8 reduce-scatter.19
  1091.5 65.6 reduce-scatter.17

commit v2 on v1

v2 whole, which is shorter than its diff:
```python
import functools

import jax
import jax.numpy as jnp
from jax import lax
from jax.experimental import pallas as pl
from jax.experimental.pallas import tpu as pltpu
from jax.sharding import PartitionSpec as P

HEADS = 16
HEAD_DIM = 128
eps_norm = 1e-06
rope_base = 500000.0
masked_value = -1e30
bf16 = jnp.bfloat16
f32 = jnp.float32
MESH = pl.DeviceIdType.MESH
ANY = pl.BlockSpec(memory_space=pl.ANY)
VM = pl.BlockSpec(memory_space=pltpu.VMEM)


def greet(barrier, targets):
    count = 0
    for cond, dev in targets:
        if cond is None:
            pl.semaphore_signal(barrier, inc=1, device_id=dev, device_id_type=MESH)
            count = count + 1
        else:
            @pl.when(cond)
            def _():
                pl.semaphore_signal(barrier, inc=1, device_id=dev, device_id_type=MESH)
            count = count + cond.astype(jnp.int32)
    pl.semaphore_wait(barrier, count)

def gather_kernel(n_s, chunks, x_ref, o_ref, send, recv, mate_send, mate_recv, local_sem):
    s = lax.axis_index("seq")
    nz = n_s // 2
    z, c = s // 2, s % 2
    mate = {"seq": s + 1 - 2 * c}
    rows = x_ref.shape[0] // chunks
    ups = {1: z < nz - 1, -1: z > 0}
    greet(pltpu.get_barrier_semaphore(), [(ups[1], {"seq": s + 2}), (ups[-1], {"seq": s - 2}), (None, mate)])

    def part(ref, slot, k):
        return ref.at[slot, pl.ds(k * rows, rows)]

    def hop(d, direction, k, slot):
        i = 0 if direction == 1 else 1
        src = x_ref.at[pl.ds(k * rows, rows)] if d == 0 else part(o_ref, slot, k)
        return pltpu.make_async_remote_copy(src, part(o_ref, slot, k), send.at[i, d, k], recv.at[i, d, k],
                                            device_id={"seq": s + 2 * direction}, device_id_type=MESH)

    def share(i, d, k, slot):
        src = x_ref.at[pl.ds(k * rows, rows)] if d == 0 else part(o_ref, slot, k)
        return pltpu.make_async_remote_copy(src, part(o_ref, slot, k), mate_send.at[i, d, k], mate_recv.at[i, d, k],
                                            device_id=mate, device_id_type=MESH)

    own = pltpu.make_async_copy(x_ref, o_ref.at[s], local_sem)
    for k in range(chunks):
        for direction in (1, -1):
            @pl.when(ups[direction])
            def _():
                hop(0, direction, k, s).start()
    for k in range(chunks):
        share(0, 0, k, s).start()
    own.start()
    for d in range(1, nz):
        for k in range(chunks):
            for i, direction in enumerate((1, -1)):
                origin = z - direction * d
                there = (origin >= 0) & (origin < nz)
                slot = 2 * origin + c
                @pl.when(there)
                def _():
                    hop(d - 1, direction, k, slot).wait_recv()
                    share(i, d, k, slot).start()
                    if d < nz - 1:
                        @pl.when(ups[direction])
                        def _():
                            hop(d, direction, k, slot).start()
    for k in range(chunks):
        share(0, 0, k, s + 1 - 2 * c).wait_recv()
    for d in range(1, nz):
        for k in range(chunks):
            for i, direction in enumerate((1, -1)):
                origin = z - direction * d
                there = (origin >= 0) & (origin < nz)
                @pl.when(there)
                def _():
                    share(i, d, k, 2 * origin + 1 - c).wait_recv()
    own.wait()
    for k in range(chunks):
        share(0, 0, k, s).wait_send()
        for direction in (1, -1):
            @pl.when(ups[direction])
            def _():
                hop(0, direction, k, s).wait_send()
    for d in range(1, nz):
        for k in range(chunks):
            for i, direction in enumerate((1, -1)):
                origin = z - direction * d
                there = (origin >= 0) & (origin < nz)
                slot = 2 * origin + c
                @pl.when(there)
                def _():
                    share(i, d, k, slot).wait_send()
                    if d < nz - 1:
                        @pl.when(ups[direction])
                        def _():
                            hop(d, direction, k, slot).wait_send()

def seq_gather(x, n_s, cid, chunks=2):
    rows, width = x.shape
    nz = n_s // 2
    sem = pltpu.SemaphoreType.DMA((2, nz, chunks))
    out = pl.pallas_call(
        functools.partial(gather_kernel, n_s, chunks),
        out_shape=jax.ShapeDtypeStruct((n_s, rows, width), x.dtype),
        in_specs=[pl.BlockSpec(memory_space=pl.ANY)],
        out_specs=pl.BlockSpec(memory_space=pl.ANY),
        scratch_shapes=[sem, sem, sem, sem, pltpu.SemaphoreType.DMA],
        compiler_params=pltpu.CompilerParams(collective_id=cid, has_side_effects=True),
    )(x)
    return out.reshape(n_s * rows, width)

def scatter_kernel(n_s, chunks, p_ref, o_ref, from_mate, run, send, recv, mate_send, mate_recv):
    s = lax.axis_index("seq")
    nz = n_s // 2
    z, c = s // 2, s % 2
    mate = {"seq": s + 1 - 2 * c}
    rows = p_ref.shape[1] // chunks
    ups = {1: z < nz - 1, -1: z > 0}
    greet(pltpu.get_barrier_semaphore(), [(ups[1], {"seq": s + 2}), (ups[-1], {"seq": s - 2}), (None, mate)])

    def give(zd, k):
        rs = pl.ds(k * rows, rows)
        return pltpu.make_async_remote_copy(p_ref.at[2 * zd + 1 - c, rs], from_mate.at[zd, rs], mate_send.at[zd, k], mate_recv.at[zd, k],
                                            device_id=mate, device_id_type=MESH)

    def hop(i, zd, k):
        rs = pl.ds(k * rows, rows)
        return pltpu.make_async_remote_copy(run.at[i, zd, rs], run.at[i, zd, rs], send.at[i, zd, k], recv.at[i, zd, k],
                                            device_id={"seq": s + (2 if i == 0 else -2)}, device_id_type=MESH)

    order = []
    for a in range((nz + 1) // 2):
        order += [nz - 1 - a] if nz - 1 - a == a else [nz - 1 - a, a]
    for zd in order:
        for k in range(chunks):
            give(zd, k).start()

    def pair(zd, k):
        rs = pl.ds(k * rows, rows)
        return p_ref[2 * zd + c, rs].astype(f32) + from_mate[zd, rs].astype(f32)

    for step in range(nz - 1):
        for k in range(chunks):
            rs = pl.ds(k * rows, rows)
            for i, zd in ((0, nz - 1 - step), (1, step)):
                going = z < zd if i == 0 else z > zd
                behind = z > 0 if i == 0 else z < nz - 1
                @pl.when(going)
                def _():
                    give(zd, k).wait_recv()
                    @pl.when(behind)
                    def _():
                        hop(i, zd, k).wait_recv()
                        run[i, zd, rs] = (pair(zd, k) + run[i, zd, rs].astype(f32)).astype(bf16)
                    @pl.when(jnp.logical_not(behind))
                    def _():
                        run[i, zd, rs] = pair(zd, k).astype(bf16)
                    hop(i, zd, k).start()
    for zd in range(nz):
        @pl.when(z == zd)
        def _():
            for k in range(chunks):
                rs = pl.ds(k * rows, rows)
                give(zd, k).wait_recv()
                total = pair(zd, k)
                if zd > 0:
                    hop(0, zd, k).wait_recv()
                    total = total + run[0, zd, rs].astype(f32)
                if zd < nz - 1:
                    hop(1, zd, k).wait_recv()
                    total = total + run[1, zd, rs].astype(f32)
                o_ref[rs] = total
    for zd in range(nz):
        for k in range(chunks):
            give(zd, k).wait_send()
    for step in range(nz - 1):
        for k in range(chunks):
            for i, zd in ((0, nz - 1 - step), (1, step)):
                going = z < zd if i == 0 else z > zd
                @pl.when(going)
                def _():
                    hop(i, zd, k).wait_send()

def seq_scatter(p, n_s, cid, chunks=2):
    rows, width = p.shape[0] // n_s, p.shape[1]
    nz = n_s // 2
    sem = pltpu.SemaphoreType.DMA((2, nz, chunks))
    msem = pltpu.SemaphoreType.DMA((nz, chunks))
    vm = pl.BlockSpec(memory_space=pltpu.VMEM)
    return pl.pallas_call(
        functools.partial(scatter_kernel, n_s, chunks),
        out_shape=jax.ShapeDtypeStruct((rows, width), f32),
        in_specs=[vm], out_specs=vm,
        scratch_shapes=[pltpu.VMEM((nz, rows, width), bf16), pltpu.VMEM((2, nz, rows, width), bf16), sem, sem, msem, msem],
        compiler_params=pltpu.CompilerParams(collective_id=cid, has_side_effects=True, vmem_limit_bytes=40 * 2**20),
    )(p.astype(bf16).reshape(n_s, rows, width))

def swap_kernel(n_s, x_ref, o_ref, send, recv, local_sem):
    s = lax.axis_index("seq")
    others = [lax.rem(s + k, n_s) for k in range(1, n_s)]
    greet(pltpu.get_barrier_semaphore(), [(None, {"seq": o}) for o in others])
    own = pltpu.make_async_copy(x_ref.at[s], o_ref.at[s], local_sem)
    def copy(k):
        to = lax.rem(s + k, n_s)
        return pltpu.make_async_remote_copy(x_ref.at[to], o_ref.at[s], send.at[k], recv.at[k], device_id={"seq": to}, device_id_type=MESH)
    for k in range(1, n_s):
        copy(k).start()
    own.start()
    for k in range(1, n_s):
        copy(k).wait()
    own.wait()

def seq_swap(x, n_s, cid):
    sem = pltpu.SemaphoreType.DMA((n_s,))
    anys = pl.BlockSpec(memory_space=pl.ANY)
    return pl.pallas_call(
        functools.partial(swap_kernel, n_s),
        out_shape=jax.ShapeDtypeStruct(x.shape, x.dtype),
        in_specs=[anys], out_specs=anys,
        scratch_shapes=[sem, sem, pltpu.SemaphoreType.DMA],
        compiler_params=pltpu.CompilerParams(collective_id=cid, has_side_effects=True),
    )(x)

def share_kernel(n_w, n_s, whole, x_ref, o_ref, send, recv, local_sem):
    w, s = lax.axis_index("wide"), lax.axis_index("seq")
    wides = range(n_w) if whole else (0,)
    steps = [(a, b) for a in wides for b in range(n_s) if a or b]

    def at(a, b):
        return (lax.rem(w + a, n_w), lax.rem(s + b, n_s))

    def name(place):
        return {"wide": place[0], "seq": place[1]}

    greet(pltpu.get_barrier_semaphore(), [(None, name(at(a, b))) for a, b in steps])
    me = w * n_s + s if whole else s
    swap = len(x_ref.shape) == 3

    def block(place):
        return x_ref.at[place[0] * n_s + place[1] if whole else place[1]] if swap else x_ref

    own = pltpu.make_async_copy(block((w, s)), o_ref.at[me], local_sem)

    def copy(a, b):
        to = at(a, b)
        i = a * n_s + b
        return pltpu.make_async_remote_copy(
            block(to), o_ref.at[me], send.at[i], recv.at[i], device_id=name(to), device_id_type=MESH
        )

    for a, b in steps:
        copy(a, b).start()
    own.start()
    for a, b in steps:
        copy(a, b).wait()
    own.wait()


def exchange(x, n_w, n_s, whole, cid):
    count = n_w * n_s if whole else n_s
    sem = pltpu.SemaphoreType.DMA((count,))
    return pl.pallas_call(
        functools.partial(share_kernel, n_w, n_s, whole),
        out_shape=jax.ShapeDtypeStruct((count, *x.shape[-2:]), x.dtype),
        in_specs=[VM],
        out_specs=VM,
        scratch_shapes=[sem, sem, pltpu.SemaphoreType.DMA],
        compiler_params=pltpu.CompilerParams(collective_id=cid, has_side_effects=True),
    )(x)


def columns_kernel(n_s, plan, to_rows, *refs):
    n = len(plan)
    *arrays, send, recv, local_sem = refs
    split, joined = (arrays[:n], arrays[n]) if not to_rows else (arrays[1:], arrays[0])
    s = lax.axis_index("seq")
    greet(pltpu.get_barrier_semaphore(), [(None, {"seq": lax.rem(s + k, n_s)}) for k in range(1, n_s)])

    def pieces(k):
        there = lax.rem(s + k, n_s)
        for array, parts in zip(split, plan):
            for step, offset, width, column in parts:
                if to_rows:
                    src = joined.at[there, :, pl.ds(column, width)]
                    dst = array.at[:, pl.ds(pl.multiple_of(s * step + offset, 128), width)]
                else:
                    src = array.at[:, pl.ds(pl.multiple_of(there * step + offset, 128), width)]
                    dst = joined.at[s, :, pl.ds(column, width)]
                yield src, dst, {"seq": there}

    for k in range(1, n_s):
        for src, dst, dev in pieces(k):
            pltpu.make_async_remote_copy(src, dst, send.at[k], recv.at[k], device_id=dev, device_id_type=MESH).start()
    for src, dst, dev in pieces(0):
        pltpu.make_async_copy(src, dst, local_sem).start()
    slot = joined.at[0]
    for k in range(1, n_s):
        done = pltpu.make_async_remote_copy(slot, slot, send.at[k], recv.at[k], device_id={"seq": lax.rem(s + k, n_s)}, device_id_type=MESH)
        done.wait_recv()
        done.wait_send()
    pltpu.make_async_copy(slot, slot, local_sem).wait()


def columns_call(arrays, shapes, n_s, plan, to_rows, cid):
    sem = pltpu.SemaphoreType.DMA((n_s,))
    return pl.pallas_call(
        functools.partial(columns_kernel, n_s, plan, to_rows),
        out_shape=shapes,
        in_specs=[ANY] * len(arrays),
        out_specs=[ANY] * len(shapes) if to_rows else ANY,
        scratch_shapes=[sem, sem, pltpu.SemaphoreType.DMA],
        compiler_params=pltpu.CompilerParams(collective_id=cid, has_side_effects=True),
    )(*arrays)


def dot(a, b):
    return jnp.dot(a, b, preferred_element_type=f32)


def dot_t(a, b):
    return lax.dot_general(a, b, (((1,), (1,)), ((), ())), preferred_element_type=f32)


def t_dot(a, b):
    return lax.dot_general(a, b, (((0,), (0,)), ((), ())), preferred_element_type=f32)


def turn(v, cosine, sine):
    return v * cosine + pltpu.roll(v, HEAD_DIM // 2, 1) * sine


def allowed_pairs(doc_q, doc_k, length):
    rows = lax.broadcasted_iota(jnp.int32, (length, length), 0)
    cols = lax.broadcasted_iota(jnp.int32, (length, length), 1)
    return (cols <= rows) & (doc_q == doc_k)


def attend_kernel(scale, ql, kl, vl, inv, gq, gk, cos, sin, doc_q, doc_k, att, q_out, k_out, v_out, lse):
    length = cos.shape[0]

    def flat(ref):
        return ref[...].reshape(length, -1)

    scales = flat(inv)
    q = turn(flat(ql) * scales[:, 0:1] * gq[...], cos[...], sin[...]).astype(bf16)
    k = turn(flat(kl) * scales[:, 1:2] * gk[...], cos[...], sin[...]).astype(bf16)
    v = flat(vl).astype(bf16)
    q_out[...] = q.reshape(q_out.shape)
    k_out[...] = k.reshape(k_out.shape)
    v_out[...] = v.reshape(v_out.shape)
    allowed = allowed_pairs(doc_q[0], doc_k[0], length)
    scores = jnp.where(allowed, dot_t(q, k) * scale, masked_value)
    top = jnp.max(scores, 1, keepdims=True)
    e = jnp.exp(scores - top)
    total = jnp.sum(e, 1, keepdims=True)
    probs = (e * (1.0 / total)).astype(bf16)
    att[...] = dot(probs, v).astype(bf16).reshape(att.shape)
    lse[...] = (top + jnp.log(total)).reshape(lse.shape)


def attend_back_kernel(scale, q, k, v, lse, da, cos, sin, doc_q, doc_k, dq_out, dk_out, dv_out):
    length = cos.shape[0]

    def flat(ref):
        return ref[...].reshape(length, -1)

    queries, keys, values, d_att = flat(q), flat(k), flat(v), flat(da)
    allowed = allowed_pairs(doc_q[0], doc_k[0], length)
    scores = jnp.where(allowed, dot_t(queries, keys) * scale, masked_value)
    probs = jnp.exp(scores - flat(lse))
    d_probs = dot_t(d_att, values)
    delta = jnp.sum(probs * d_probs, 1, keepdims=True)
    d_scores = (probs * (d_probs - delta)).astype(bf16)
    d_q = dot(d_scores, keys) * scale
    d_k = t_dot(d_scores, queries) * scale
    dv_out[...] = t_dot(probs.astype(bf16), d_att).astype(bf16).reshape(dv_out.shape)
    dq_out[...] = turn(d_q, cos[...], -sin[...]).reshape(dq_out.shape)
    dk_out[...] = turn(d_k, cos[...], -sin[...]).reshape(dk_out.shape)


def attention_specs(n_s, local, length):
    def tok(first):
        return pl.BlockSpec((n_s, 1, local, HEAD_DIM), lambda m, h: (0, m, 0, first + h))

    gain = pl.BlockSpec((1, HEAD_DIM), lambda m, h: (0, h))
    table = pl.BlockSpec((length, HEAD_DIM), lambda m, h: (0, 0))
    doc_q = pl.BlockSpec((1, length, 1), lambda m, h: (m, 0, 0))
    doc_k = pl.BlockSpec((1, 1, length), lambda m, h: (m, 0, 0))
    col = pl.BlockSpec((1, n_s, 1, local, 1), lambda m, h: (h, 0, m, 0, 0))
    return tok, gain, table, doc_q, doc_k, col


def attend(lin, inv, gains, tables, docs, heads, scale):
    n_s, micro, local, _ = lin.shape
    length = n_s * local
    tok, gain, table, doc_q, doc_k, col = attention_specs(n_s, local, length)
    inv_spec = pl.BlockSpec((n_s, 1, local, 2), lambda m, h: (0, m, 0, 0))
    out = jax.ShapeDtypeStruct((n_s, micro, local, heads * HEAD_DIM), bf16)
    return pl.pallas_call(
        functools.partial(attend_kernel, scale),
        grid=(micro, heads),
        out_shape=[out, out, out, out, jax.ShapeDtypeStruct((heads, n_s, micro, local, 1), f32)],
        in_specs=[tok(0), tok(heads), tok(2 * heads), inv_spec, gain, gain, table, table, doc_q, doc_k],
        out_specs=[tok(0)] * 4 + [col],
        compiler_params=pltpu.CompilerParams(vmem_limit_bytes=48 * 2**20),
    )(lin, lin, lin, inv, gains[0:1], gains[1:2], *tables, docs[:, :, None], docs[:, None, :])


def attend_back(q, k, v, lse, d_att, tables, docs, heads, scale):
    n_s, micro, local, width = q.shape
    length = n_s * local
    tok, gain, table, doc_q, doc_k, col = attention_specs(n_s, local, length)
    return pl.pallas_call(
        functools.partial(attend_back_kernel, scale),
        grid=(micro, heads),
        out_shape=[jax.ShapeDtypeStruct(q.shape, f32)] * 2 + [jax.ShapeDtypeStruct(q.shape, bf16)],
        in_specs=[tok(0)] * 3 + [col, tok(0), table, table, doc_q, doc_k],
        out_specs=[tok(0)] * 3,
        compiler_params=pltpu.CompilerParams(vmem_limit_bytes=48 * 2**20),
    )(q, k, v, lse, d_att, *tables, docs[:, :, None], docs[:, None, :])


def inverse_rms(values):
    return lax.rsqrt(jnp.mean(values * values, axis=-1, keepdims=True) + eps_norm)


def normalize_back(grad_out, normed, inverse, gain_vec):
    scaled = grad_out * gain_vec
    grad_in = inverse * (scaled - normed * jnp.mean(scaled * normed, axis=-1, keepdims=True))
    return grad_in, jnp.sum(grad_out * normed, axis=0)


def rotation_tables(positions):
    half_dim = HEAD_DIM // 2
    frequency = rope_base ** (-jnp.arange(half_dim, dtype=f32) * 2.0 / HEAD_DIM)
    angles = positions.astype(f32)[:, None] * frequency[None, :]
    cosine, sine = jnp.cos(angles), jnp.sin(angles)
    return jnp.concatenate([cosine, cosine], 1), jnp.concatenate([-sine, sine], 1)


def wide_gather(block):
    return lax.all_gather(block, "wide", axis=0, tiled=True)


def wide_scatter(partial):
    return lax.psum_scatter(partial.astype(bf16), "wide", scatter_dimension=0, tiled=True)


def on_device(n_w, n_s, inputs, documents, cotangent, query_weight, key_weight, value_weight, output_weight,
              query_gain, key_gain, attention_gain, gate_weight, up_weight, down_weight, feed_gain):
    micro, _, local, width = inputs.shape
    tokens = micro * local
    n_dev = n_w * n_s
    heads = HEADS // n_s
    cols = heads * HEAD_DIM
    row_len = documents.shape[2]
    feed = gate_weight.shape[1]
    feed_block = feed // n_dev
    half = n_w * feed_block
    rows = query_weight.shape[0]
    scale = HEAD_DIM ** (-0.5)
    s_index = lax.axis_index("seq")

    flat = inputs.reshape(tokens, width)
    qkv_plan = [[(cols, 0, cols, i * cols)] for i in range(3)]
    own_blocks = feed_block % 128 == 0
    moves = [(b, (b % n_w) * n_s + b // n_w) for b in range(n_dev)]
    back_moves = [(b, a) for a, b in moves]
    if own_blocks:
        feed_plan = [[(feed_block, a * n_s * feed_block, feed_block, i * half + a * feed_block) for a in range(n_w)] for i in range(2)]
    else:
        feed_plan = [[(half, 0, half, i * half)] for i in range(2)]
    qkv = columns_call((query_weight, key_weight, value_weight), jax.ShapeDtypeStruct((n_s, rows, 3 * cols), bf16), n_s, qkv_plan, False, 0)
    qkv_all = wide_gather(qkv.reshape(n_s * rows, 3 * cols))
    x_all = seq_gather(flat, n_s, 1)
    gate_up = columns_call((gate_weight, up_weight), jax.ShapeDtypeStruct((n_s, rows, 2 * half), bf16), n_s, feed_plan, False, 2)
    gate_up_all = wide_gather(gate_up.reshape(n_s * rows, 2 * half))
    down_all = wide_gather(down_weight if own_blocks else lax.ppermute(down_weight, ("wide", "seq"), moves))
    out_all = wide_gather(lax.ppermute(output_weight, ("wide", "seq"), moves))

    own_gain = jnp.stack([query_gain, key_gain, attention_gain, feed_gain]).astype(f32)
    own_gain = jnp.pad(own_gain, ((0, 4), (0, 128 - rows)))
    gains = exchange(own_gain, n_w, n_s, True, 3)[:, :4, :rows]
    gains = jnp.swapaxes(gains, 0, 1).reshape(4, width)
    own_gains = lax.dynamic_slice_in_dim(gains, s_index * cols, cols, 1)

    lin = dot(x_all, qkv_all)
    q_lin, k_lin = lin[:, :cols], lin[:, cols:2 * cols]

    def seq_sums(a, b, cid):
        return jnp.sum(exchange(jnp.stack([a, b] + [jnp.zeros_like(a)] * 6), n_w, n_s, False, cid), 0)[:2]

    inv = lax.rsqrt(seq_sums(jnp.sum(q_lin * q_lin, 1), jnp.sum(k_lin * k_lin, 1), 4) / width + eps_norm).T
    tables = rotation_tables(jnp.arange(row_len, dtype=jnp.int32))
    docs = documents[:, 0, :]
    shape4 = (n_s, micro, local, -1)
    attended, q, k, v, lse = attend(lin.reshape(shape4), inv.reshape(shape4), own_gains, tables, docs, heads, scale)
    attended = attended.reshape(n_s * tokens, cols)

    mixed = seq_scatter(dot(attended, out_all), n_s, 5)
    mixed_inv = inverse_rms(mixed)
    mixed_n = mixed * mixed_inv
    hidden = flat.astype(f32) + mixed_n * gains[2]
    hidden_all = seq_gather(hidden.astype(bf16), n_s, 6)
    gate_up_lin = dot(hidden_all, gate_up_all)
    gate_lin, upward = gate_up_lin[:, :half], gate_up_lin[:, half:]
    sigma = jax.nn.sigmoid(gate_lin)
    silu_gate = gate_lin * sigma
    active = (silu_gate * upward).astype(bf16)
    down = seq_scatter(dot(active, down_all), n_s, 7)
    down_inv = inverse_rms(down)
    down_n = down * down_inv
    layer_out = (hidden + down_n * gains[3]).astype(bf16).reshape(inputs.shape)

    grad_out = cotangent.reshape(tokens, width).astype(f32)
    d_down, feed_term = normalize_back(grad_out, down_n, down_inv, gains[3])
    d_down_all = seq_gather(d_down.astype(bf16), n_s, 8)
    down_grad = wide_scatter(t_dot(active, d_down_all))
    if not own_blocks:
        down_grad = lax.ppermute(down_grad, ("wide", "seq"), back_moves)
    down_grad = down_grad.astype(f32)
    d_active = dot_t(d_down_all, down_all)
    d_gate = (d_active * upward * sigma * (1.0 + gate_lin * (1.0 - sigma))).astype(bf16)
    d_up = (d_active * silu_gate).astype(bf16)
    d_gate_up = jnp.concatenate([d_gate, d_up], axis=1)
    mlp_grad = wide_scatter(t_dot(hidden_all, d_gate_up))
    d_hidden = grad_out + seq_scatter(dot_t(d_gate_up, gate_up_all), n_s, 9)
    d_mixed, attention_term = normalize_back(d_hidden, mixed_n, mixed_inv, gains[2])
    d_mixed_all = seq_gather(d_mixed.astype(bf16), n_s, 10)
    out_grad = wide_scatter(t_dot(attended, d_mixed_all))
    d_attended = dot_t(d_mixed_all, out_all).astype(bf16).reshape(shape4)

    d_q, d_k, d_v = attend_back(q, k, v, lse, d_attended, tables, docs, heads, scale)
    d_q, d_k, d_v = (t.reshape(n_s * tokens, cols) for t in (d_q, d_k, d_v))
    q_n, k_n = q_lin * inv[:, 0:1], k_lin * inv[:, 1:2]
    d_qg, d_kg = d_q * own_gains[0], d_k * own_gains[1]
    means = seq_sums(jnp.sum(d_qg * q_n, 1), jnp.sum(d_kg * k_n, 1), 11).T / width
    query_term = jnp.sum(d_q * q_n, 0)
    key_term = jnp.sum(d_k * k_n, 0)
    d_q_lin = (inv[:, 0:1] * (d_qg - q_n * means[:, 0:1])).astype(bf16)
    d_k_lin = (inv[:, 1:2] * (d_kg - k_n * means[:, 1:2])).astype(bf16)
    d_lin = jnp.concatenate([d_q_lin, d_k_lin, d_v], axis=1)
    input_back = seq_scatter(dot_t(d_lin, qkv_all), n_s, 12)
    input_grad = (d_hidden + input_back).reshape(inputs.shape)
    qkv_grad = wide_scatter(t_dot(x_all, d_lin))

    mat = jax.ShapeDtypeStruct((rows, width), bf16)
    wide_mat = jax.ShapeDtypeStruct((rows, feed), bf16)
    gate_grad, up_grad = columns_call((mlp_grad.reshape(n_s, rows, 2 * half),), [wide_mat] * 2, n_s, feed_plan, True, 13)
    query_grad, key_grad, value_grad = columns_call((qkv_grad.reshape(n_s, rows, 3 * cols),), [mat] * 3, n_s, qkv_plan, True, 14)
    out_grad = lax.ppermute(out_grad, ("wide", "seq"), back_moves)

    zero = jnp.zeros((width,), f32)
    terms = jnp.stack([
        lax.dynamic_update_slice_in_dim(zero, query_term, s_index * cols, 0),
        lax.dynamic_update_slice_in_dim(zero, key_term, s_index * cols, 0),
        attention_term,
        feed_term,
    ])
    terms = jnp.swapaxes(terms.reshape(4, n_dev, rows), 0, 1)
    terms = jnp.pad(terms, ((0, 0), (0, 4), (0, 128 - rows)))
    gain_grads = jnp.sum(exchange(terms, n_w, n_s, True, 15), 0)[:4, :rows]
    return (layer_out, input_grad, *(g.astype(f32) for g in (query_grad, key_grad, value_grad, out_grad)),
            gain_grads[0], gain_grads[1], gain_grads[2], gate_grad.astype(f32), up_grad.astype(f32), down_grad, gain_grads[3])


def solution(mesh):
    tok = P(None, "wide", "seq", None)
    docs = P(None, "wide", None)
    mat = P(("wide", "seq"), None)
    vec = P(("wide", "seq"))

    def body(*args):
        return on_device(mesh.shape["wide"], mesh.shape["seq"], *args)

    return jax.shard_map(
        body,
        mesh=mesh,
        in_specs=(tok, docs, tok, mat, mat, mat, mat, vec, vec, vec, mat, mat, mat, vec),
        out_specs=(tok, tok, mat, mat, mat, mat, vec, vec, vec, mat, mat, mat, vec),
        check_vma=False,
    )
```

time: 1170 us -> 820 us (0.70)
  waiting for transfers between devices: 663 us -> 81.7 us
  Pallas kernels: 0 us -> 541 us
  blocking collectives: 175 us -> 0 us
  local copies, waits for them, and re-layouts: 120 us -> 26.6 us
  matrix products: 122 us -> 97.7 us
  starting transfers between devices: 28.4 us -> 10.8 us
    pallas_call x0 -> x18, Pallas kernels: none -> 541 us  [the longest x4 186 us: seq_scatter(): pl.pallas_call(functools.partial(scatter_kernel, n_s, chunks), out_shape=...]
    all_gather x4 -> x0, waiting for transfers between devices: 165 us -> none  [seq_gather(): return lax.all_gather(block, 'seq', axis=0, tiled=True)]
    unnamed x18 -> x8, waiting for transfers between devices: 126 us -> 0.64 us
    reduce_scatter x4 -> x0, waiting for transfers between devices: 125 us -> none  [seq_scatter(): lax.psum_scatter(partial.astype(bf16), 'seq', scatter_dimension=0, tiled=...]
    all_gather x4, waiting for transfers between devices: 120 us -> 0.05 us  [wide_gather(): return lax.all_gather(block, 'wide', axis=0, tiled=True)]
    all_to_all x2 -> x0, blocking collectives: 105 us -> none  [the longest x1 81.1 us: on_device(): gate_up = lax.all_to_all(gate_up, 'seq', 0, 0, tiled=True)]
    all_gather x1 -> x0, blocking collectives: 47.4 us -> none  [on_device(): lax.all_gather(jnp.stack([query_gain, key_gain, attention_gain, feed_gain...]
    convert_element_type x19 -> x0, local copies, waits for them, and re-layouts: 45.3 us -> none  [the longest x3 16 us: on_device(): mlp_grad = jnp.moveaxis(mlp_grad, 0, 3).reshape(rows, 2, feed).astype(f32)]
  transfers between devices with their start and end apart: 21 -> 10, of which waited for: 15 -> 2; matrix products, arithmetic and copies ran while one was open for 18% -> 13% of each run, Pallas kernels for 0% -> 37%
where the time goes in v2:
time: 820 us; the launch traced here: 811 us
  Pallas kernels  541 us (66%)
  matrix products  97.7 us (12%)
  waiting for transfers between devices  81.7 us (10%)
  other arithmetic  37.8 us (5%)
  local copies, waits for them, and re-layouts  26.6 us (3%)
  between operations  15.2 us (2%)
  starting transfers between devices  10.8 us (1%)
    pallas_call x4, Pallas kernels, seq_scatter(): pl.pallas_call(functools.partial(scatter_kernel, n_s, chunks), out_shape=...  186 us
    pallas_call x4, Pallas kernels, seq_gather(): pl.pallas_call(functools.partial(gather_kernel, n_s, chunks), out_shape=j...  147 us
    pallas_call x4, Pallas kernels, columns_call(): pl.pallas_call(functools.partial(columns_kernel, n_s, plan, to_rows), out...  145 us
    reduce_scatter x4, waiting for transfers between devices, wide_scatter(): lax.psum_scatter(partial.astype(bf16), 'wide', scatter_dimension=0, tiled...  64.1 us
    pallas_call x4, Pallas kernels, exchange(): pl.pallas_call(functools.partial(share_kernel, n_w, n_s, whole), out_shap...  49.6 us
    dot_general x4, matrix products, t_dot(): lax.dot_general(a, b, (((0,), (0,)), ((), ())), preferred_element_type=f32)  33 us
    dot_general x4, matrix products, dot(): return jnp.dot(a, b, preferred_element_type=f32)  32.4 us
    dot_general x4, matrix products, dot_t(): lax.dot_general(a, b, (((1,), (1,)), ((), ())), preferred_element_type=f32)  32.4 us
  transfers between devices with their start and end apart: 10, of which 2 were waited for; matrix products, arithmetic and copies ran while one was open for 13% of the time, Pallas kernels for 37%

profile of v2, /device:TPU:9, one launch (start us, length us, event | category | flops | bytes accessed | tf_op | source)
XLA Modules:
  0.0 811.0 jit_solution(5849039829993340005)
XLA Ops:
  7.2 21.4 %shard_map.237 = bf16[8,64,768]{2,1,0:T(8,128)(2,1)} custom-call(bf16[64,2048]{1,0:T(8,128)(2,1)} %refs_0_.2, bf16[64,2048]{1,0:T(8,128)(2,1)} %refs_1_.2, bf16[64,2048]{1,0:T(8,128)(2,1)} %refs_2_.1), custom_call_target="tpu_custom_call" | custom-call | tf_op jit(solution)/shard_map/pallas_call | solution.py:320
  28.8 1.9 collective-permute-start
  30.7 16.9 %collective-permute-done = bf16[64,2048]{1,0:T(8,128)(2,1)S(1)} collective-permute-done((bf16[64,2048]{1,0:T(8,128)(2,1)}, bf16[64,2048]{1,0:T(8,128)(2,1)S(1)}, u32[]{:S(2)}, u32[]{:S(2)}) %collective-permute-start) | collective-permute-done | bytes 262176 | tf_op jit(solution)/shard_map/ppermute | solution.py:493
  48.4 53.0 %shard_map.244 = bf16[8,64,2048]{2,1,0:T(8,128)(2,1)} custom-call(bf16[64,8192]{1,0:T(8,128)(2,1)} %refs_0_.3, bf16[64,8192]{1,0:T(8,128)(2,1)} %refs_1_.3), custom_call_target="tpu_custom_call" | custom-call | tf_op jit(solution)/shard_map/pallas_call | solution.py:320
  102.7 9.8 %shard_map.240 = f32[32,8,128]{2,1,0:T(8,128)} custom-call(f32[8,128]{1,0:T(8,128)} %fusion.24.x_ref), custom_call_target="tpu_custom_call" | custom-call | tf_op jit(solution)/shard_map/pallas_call | solution.py:276
  113.6 35.6 %shard_map.238 = bf16[8,128,2048]{2,1,0:T(8,128)(2,1)} custom-call(bf16[128,2048]{1,0:T(8,128)(2,1)} %bitcast.117), custom_call_target="tpu_custom_call" | custom-call | tf_op jit(solution)/shard_map/pallas_call | solution.py:116
  151.1 9.7 %convolution_bitcast_fusion = f32[1024,768]{0,1:T(8,128)} fusion(bf16[2048,768]{1,0:T(8,128)(2,1)} %all-gather.5.cloned.1.call-done, bf16[1024,2048]{1,0:T(8,128)(2,1)} %bitcast.118), kind=kOutput, calls=%fused_computation.15 | convolution fusion | flops 3221225472 | bytes 10485760 | tf_op jit(solution)/shard_map/dot_general | solution.py:331
  160.8 3.6 copy.39
  164.4 1.8 multiply_reduce_fusion.9
  166.9 13.4 %shard_map.239 = f32[8,8,1024]{2,1,0:T(8,128)} custom-call(f32[8,1024]{1,0:T(8,128)} %maximum_maximum_fusion.x_ref), custom_call_target="tpu_custom_call" | custom-call | tf_op jit(solution)/shard_map/pallas_call | solution.py:276
  181.5 7.3 shard_map.241
  191.4 2.9 convolution_convert_fusion.2
  194.3 43.3 %shard_map.242 = f32[128,2048]{1,0:T(8,128)S(1)} custom-call(bf16[8,128,2048]{2,1,0:T(8,128)(2,1)S(1)} %bitcast.98), custom_call_target="tpu_custom_call" | custom-call | tf_op jit(solution)/shard_map/pallas_call | solution.py:204
  238.8 36.5 %shard_map.243 = bf16[8,128,2048]{2,1,0:T(8,128)(2,1)} custom-call(bf16[128,2048]{1,0:T(8,128)(2,1)} %fusion.8.x_ref), custom_call_target="tpu_custom_call" | custom-call | tf_op jit(solution)/shard_map/pallas_call | solution.py:116
  275.3 12.5 %fusion.35 = f32[1024,2048]{1,0:T(8,128)S(1)} fusion(bf16[1024,2048]{1,0:T(8,128)(2,1)} %bitcast.120, bf16[2048,2048]{1,0:T(8,128)(2,1)} %all-gather.9.cloned.1.call-done), kind=kOutput, calls=%fused_computation.98 | convolution fusion | flops 8589934592 | bytes 20971520 | tf_op jit(solution)/shard_map/dot_general | solution.py:331
  287.8 3.2 copy-done.21
  291.1 2.7 multiply_convert_fusion.2
  293.8 7.3 convolution_convert_fusion.5
  301.1 48.5 %shard_map.245 = f32[128,2048]{1,0:T(8,128)S(1)} custom-call(bf16[8,128,2048]{2,1,0:T(8,128)(2,1)S(1)} %bitcast.101), custom_call_target="tpu_custom_call" | custom-call | tf_op jit(solution)/shard_map/pallas_call | solution.py:204
  351.3 37.4 %shard_map.246 = bf16[8,128,2048]{2,1,0:T(8,128)(2,1)} custom-call(bf16[128,2048]{1,0:T(8,128)(2,1)} %fusion.6.x_ref), custom_call_target="tpu_custom_call" | custom-call | tf_op jit(solution)/shard_map/pallas_call | solution.py:116
  388.7 11.7 %multiply_convert_fusion.1 = (bf16[1024,1024]{1,0:T(8,128)(2,1)S(1)}, bf16[1024,1024]{1,0:T(8,128)(2,1)S(1)}) fusion(f32[1024,2048]{1,0:T(8,128)} %copy-done.21, bf16[1024,2048]{1,0:T(8,128)(2,1)} %bitcast.122, bf16[1024,2048]{1,0:T(8,128)(2,1)} %all-gather.11.cloned.1.call-done), kind=kOutput, calls=%fused_computation.3 | convolution fusion | flops 4308598784 | bytes 20971520 | tf_op jit(solution)/shard_map/dot_general | solution.py:335
  401.7 11.4 %convolution_convert_fusion.1 = bf16[1024,2048]{1,0:T(8,128)(2,1)S(1)} fusion(bf16[2048,2048]{1,0:T(8,128)(2,1)} %all-gather.9.cloned.1.call-done, bf16[1024,1024]{1,0:T(8,128)(2,1)S(1)} %get-tuple-element.80, bf16[1024,1024]{1,0:T(8,128)(2,1)S(1)} %get-tuple-element.79), kind=kOutput, calls=%fused_computation.7 | convolution fusion | flops 8600420352 | bytes 16777216 | tf_op jit(solution)/shard_map/dot_general | solution.py:335
  413.1 48.2 %shard_map.247 = f32[128,2048]{1,0:T(8,128)S(1)} custom-call(bf16[8,128,2048]{2,1,0:T(8,128)(2,1)S(1)} %bitcast.100), custom_call_target="tpu_custom_call" | custom-call | tf_op jit(solution)/shard_map/pallas_call | solution.py:204
  463.3 37.1 %shard_map.248 = bf16[8,128,2048]{2,1,0:T(8,128)(2,1)} custom-call(bf16[128,2048]{1,0:T(8,128)(2,1)} %get-tuple-element.83.x_ref), custom_call_target="tpu_custom_call" | custom-call | tf_op jit(solution)/shard_map/pallas_call | solution.py:116
  500.4 4.5 convolution_convert_fusion.7
  505.1 3.7 convolution_convert_fusion.8
  508.8 7.0 shard_map.249
  517.5 2.7 copy.46
  521.5 2.9 multiply_reduce_fusion.2
  525.1 14.9 %shard_map.250 = f32[8,8,1024]{2,1,0:T(8,128)} custom-call(f32[8,1024]{1,0:T(8,128)} %maximum_maximum_fusion.1.x_ref), custom_call_target="tpu_custom_call" | custom-call | tf_op jit(solution)/shard_map/pallas_call | solution.py:276
  542.1 2.4 multiply_convert_fusion.4
  545.5 6.2 fusion.1
  551.8 8.4 %convolution_convert_fusion.4 = bf16[1024,2048]{1,0:T(8,128)(2,1)} fusion(bf16[1024,1024]{1,0:T(8,128)(2,1)S(1)} %copy-done.25, bf16[1024,2048]{1,0:T(8,128)(2,1)} %bitcast.123), kind=kOutput, calls=%fused_computation.10 | convolution fusion | flops 4297064448 | bytes 10485760 | tf_op jit(solution)/shard_map/dot_general | solution.py:339
  561.8 13.8 %convolution_convert_fusion = bf16[2048,2048]{1,0:T(8,128)(2,1)} fusion(bf16[1024,2048]{1,0:T(8,128)(2,1)} %bitcast.121, bf16[1024,1024]{1,0:T(8,128)(2,1)} %copy-done.40, bf16[1024,1024]{1,0:T(8,128)(2,1)S(1)} %copy-done.39), kind=kOutput, calls=%fused_computation | convolution fusion | flops 8602517504 | bytes 16777216 | tf_op jit(solution)/shard_map/dot_general | solution.py:339
  577.9 5.7 convolution_convert_fusion.3
  583.6 45.8 %shard_map.251 = f32[128,2048]{1,0:T(8,128)S(1)} custom-call(bf16[8,128,2048]{2,1,0:T(8,128)(2,1)S(1)} %bitcast.99), custom_call_target="tpu_custom_call" | custom-call | tf_op jit(solution)/shard_map/pallas_call | solution.py:204
  630.7 8.1 collective-permute-start.1
  639.5 11.4 %shard_map.253 = f32[32,8,128]{2,1,0:T(8,128)} custom-call(f32[32,8,128]{2,1,0:T(8,128)} %pad.12.x_ref), custom_call_target="tpu_custom_call" | custom-call | tf_op jit(solution)/shard_map/pallas_call | solution.py:276
  653.2 2.3 copy.49
  655.5 21.3 %shard_map.252 = (bf16[64,2048]{1,0:T(8,128)(2,1)}, bf16[64,2048]{1,0:T(8,128)(2,1)}, bf16[64,2048]{1,0:T(8,128)(2,1)}) custom-call(bf16[8,64,768]{2,1,0:T(8,128)(2,1)} %bitcast.127), custom_call_target="tpu_custom_call" | custom-call | tf_op jit(solution)/shard_map/pallas_call | solution.py:320
  676.8 1.8 convert_element_type.125
  678.6 1.8 convert_element_type.126
  680.4 1.8 convert_element_type.127
  682.2 2.8 convert_element_type.134
  685.0 64.1 %reduce-scatter.9.cloned.1.call-done = bf16[512,2048]{1,0:T(8,128)(2,1)} async-done(((bf16[2048,2048]{1,0:T(8,128)(2,1)}), bf16[512,2048]{1,0:T(8,128)(2,1)}) %reduce-scatter.9.cloned.1.call-update) | async-done | bytes 2097168 | tf_op jit(solution)/shard_map/reduce_scatter | solution.py:460
  749.1 49.4 %shard_map.254 = (bf16[64,8192]{1,0:T(8,128)(2,1)}, bf16[64,8192]{1,0:T(8,128)(2,1)}) custom-call(bf16[8,64,2048]{2,1,0:T(8,128)(2,1)} %bitcast.128), custom_call_target="tpu_custom_call" | custom-call | tf_op jit(solution)/shard_map/pallas_call | solution.py:320
  798.6 2.7 convert_element_type.131
  801.2 2.7 convert_element_type.132
  (162 shorter events, 30.7 us)
Async XLA Ops:
  7.2 143.9 %all-gather.5.cloned.1.call-start = ((), (), s32[]{:S(2)}) async-start(), calls=%async_computation.4 | async-start | bytes 3932160 | tf_op jit(solution)/shard_map/all_gather | solution.py:456
  28.7 73.4 %copy-start.34 = (bf16[64]{0:T(256)(128)(2,1)S(1)}, bf16[64]{0:T(256)(128)(2,1)}, u32[]{:S(2)}) copy-start(bf16[64]{0:T(256)(128)(2,1)} %param.27) | copy-start | bytes 388
  28.7 73.4 %copy-start.35 = (bf16[64]{0:T(256)(128)(2,1)S(1)}, bf16[64]{0:T(256)(128)(2,1)}, u32[]{:S(2)}) copy-start(bf16[64]{0:T(256)(128)(2,1)} %param.23) | copy-start | bytes 388
  28.7 73.4 %copy-start.36 = (bf16[64]{0:T(256)(128)(2,1)S(1)}, bf16[64]{0:T(256)(128)(2,1)}, u32[]{:S(2)}) copy-start(bf16[64]{0:T(256)(128)(2,1)} %param.22) | copy-start | bytes 388
  28.7 73.4 %copy-start.37 = (bf16[64]{0:T(256)(128)(2,1)S(1)}, bf16[64]{0:T(256)(128)(2,1)}, u32[]{:S(2)}) copy-start(bf16[64]{0:T(256)(128)(2,1)} %param.21) | copy-start | bytes 388
  28.7 162.6 %all-gather.7.cloned.1.call-start = ((), (), s32[]{:S(2)}) async-start(), calls=%async_computation.5 | async-start | bytes 1310720 | tf_op jit(solution)/shard_map/all_gather | solution.py:456
  28.8 18.8 %collective-permute-start = (bf16[64,2048]{1,0:T(8,128)(2,1)}, bf16[64,2048]{1,0:T(8,128)(2,1)S(1)}, u32[]{:S(2)}, u32[]{:S(2)}) collective-permute-start(bf16[64,2048]{1,0:T(8,128)(2,1)} %param.20), channel_id=1, source_target_pairs={{0,0},{1,8},{2,16},{3,24},{4,1},{5,9},{6,17},{7,25},{8,2},{9,10},{... | collective-permute-start | bytes 786440 | tf_op jit(solution)/shard_map/ppermute | solution.py:493
  48.3 227.0 %all-gather.9.cloned.1.call-start = ((), (), s32[]{:S(2)}) async-start(), calls=%async_computation.6 | async-start | bytes 10485760 | tf_op jit(solution)/shard_map/all_gather | solution.py:456
  101.4 48.0 %copy-start.16 = (s32[2,1,512]{2,1,0:T(1,128)S(1)}, s32[2,1,512]{2,1,0:T(1,128)}, u32[]{:S(2)}) copy-start(s32[2,1,512]{2,1,0:T(1,128)} %doc_k.3) | copy-start | bytes 12292
  101.4 192.4 %all-gather.11.cloned.1.call-start = ((), (), s32[]{:S(2)}) async-start(), calls=%async_computation.7 | async-start | bytes 5242880 | tf_op jit(solution)/shard_map/all_gather | solution.py:456
  102.0 528.7 %reduce-scatter.7.cloned.1.call-start = ((), (), s32[]{:S(2)}) async-start(), calls=%async_computation.9 | async-start | bytes 1310720 | tf_op jit(solution)/shard_map/reduce_scatter | solution.py:460
  149.6 31.9 %copy-start = (s32[2,512,1]{2,1,0:T(8,128)}, s32[2,512,1]{2,1,0:T(8,128)S(1)}, u32[]{:S(2)}) copy-start(s32[2,512,1]{2,1,0:T(8,128)S(1)} %broadcast_in_dim_squeeze.5.doc_q) | copy-start | bytes 12292
  151.1 30.4 %copy-start.2 = (f32[512,128]{1,0:T(8,128)}, f32[512,128]{1,0:T(8,128)S(1)}, u32[]{:S(2)}) copy-start(f32[512,128]{1,0:T(8,128)S(1)} %get-tuple-element.99.sin) | copy-start | bytes 786436
  188.8 1.0 copy-start.6
  189.8 0.8 copy-start.10
  191.4 2.9 copy-start.8
  191.4 46.2 %copy-start.4 = (bf16[8,2,64,256]{3,2,1,0:T(8,128)(2,1)}, bf16[8,2,64,256]{3,2,1,0:T(8,128)(2,1)S(1)}, u32[]{:S(2)}) copy-start(bf16[8,2,64,256]{3,2,1,0:T(8,128)(2,1)S(1)} %get-tuple-element.26) | copy-start | bytes 1572868
  194.3 43.5 %copy-start.22 = (bf16[2,1,64,2048]{3,2,1,0:T(8,128)(2,1)S(1)}, bf16[2,1,64,2048]{3,2,1,0:T(8,128)(2,1)}, u32[]{:S(2)}) copy-start(bf16[2,1,64,2048]{3,2,1,0:T(8,128)(2,1)} %param.14) | copy-start | bytes 1572868
  287.8 3.2 copy-start.21
  301.1 48.6 %copy-start.17 = (bf16[2,1,64,2048]{3,2,1,0:T(8,128)(2,1)S(1)}, bf16[2,1,64,2048]{3,2,1,0:T(8,128)(2,1)}, u32[]{:S(2)}) copy-start(bf16[2,1,64,2048]{3,2,1,0:T(8,128)(2,1)} %param.16) | copy-start | bytes 1572868
  400.4 1.3 copy-start.38
  400.4 12.7 %copy-start.40 = (bf16[1024,1024]{1,0:T(8,128)(2,1)}, bf16[1024,1024]{1,0:T(8,128)(2,1)S(1)}, u32[]{:S(2)}) copy-start(bf16[1024,1024]{1,0:T(8,128)(2,1)S(1)} %get-tuple-element.80) | copy-start | bytes 6291460
  413.1 48.2 %copy-start.18 = (bf16[2,1,64,2048]{3,2,1,0:T(8,128)(2,1)S(1)}, bf16[2,1,64,2048]{3,2,1,0:T(8,128)(2,1)}, u32[]{:S(2)}) copy-start(bf16[2,1,64,2048]{3,2,1,0:T(8,128)(2,1)} %param.16) | copy-start | bytes 1572868
  413.1 48.6 %copy-start.23 = (bf16[2,1,64,2048]{3,2,1,0:T(8,128)(2,1)S(1)}, bf16[2,1,64,2048]{3,2,1,0:T(8,128)(2,1)}, u32[]{:S(2)}) copy-start(bf16[2,1,64,2048]{3,2,1,0:T(8,128)(2,1)} %param.14) | copy-start | bytes 1572868
  463.3 37.1 %copy-start.5 = (bf16[8,2,64,256]{3,2,1,0:T(8,128)(2,1)S(1)}, bf16[8,2,64,256]{3,2,1,0:T(8,128)(2,1)}, u32[]{:S(2)}) copy-start(bf16[8,2,64,256]{3,2,1,0:T(8,128)(2,1)} %copy-done.4) | copy-start | bytes 1572868
  500.4 4.6 copy-start.26
  504.9 3.8 copy-start.1
  504.9 3.8 copy-start.3
  505.0 148.3 %reduce-scatter.5.cloned.1.call-start = ((), (), s32[]{:S(2)}) async-start(), calls=%async_computation.8 | async-start | bytes 3932160 | tf_op jit(solution)/shard_map/reduce_scatter | solution.py:460
  505.0 3.7 copy-start.9
  505.0 3.7 copy-start.11
  505.0 3.7 copy-start.13
  515.8 1.0 copy-start.7
  517.5 22.5 %copy-start.15 = (bf16[8,2,64,256]{3,2,1,0:T(8,128)(2,1)S(1)}, bf16[8,2,64,256]{3,2,1,0:T(8,128)(2,1)}, u32[]{:S(2)}) copy-start(bf16[8,2,64,256]{3,2,1,0:T(8,128)(2,1)} %copy-done.14) | copy-start | bytes 1572868
  521.5 20.5 %copy-start.20 = (f32[1024,256]{0,1:T(8,128)S(1)}, f32[1024,256]{0,1:T(8,128)}, u32[]{:S(2)}) copy-start(f32[1024,256]{0,1:T(8,128)} %copy.46) | copy-start | bytes 3145732
  542.0 3.5 copy-start.24
  542.0 3.5 copy-start.31
  544.5 0.8 copy-start.27
  544.6 1.0 copy-start.29
  545.5 6.3 copy-start.25
  551.8 130.4 %reduce-scatter.11.cloned.1.call-start = ((), (), s32[]{:S(2)}) async-start(), calls=%async_computation.11 | async-start | bytes 5242880 | tf_op jit(solution)/shard_map/reduce_scatter | solution.py:460
  560.2 1.6 copy-start.39
  560.2 188.9 %reduce-scatter.9.cloned.1.call-start = ((), (), s32[]{:S(2)}) async-start(), calls=%async_computation.10 | async-start | bytes 10485760 | tf_op jit(solution)/shard_map/reduce_scatter | solution.py:460
  575.6 2.3 copy-start.28
  575.6 2.3 copy-start.30
  575.6 2.3 copy-start.32
  583.6 45.8 %copy-start.19 = (bf16[2,1,64,2048]{3,2,1,0:T(8,128)(2,1)S(1)}, bf16[2,1,64,2048]{3,2,1,0:T(8,128)(2,1)}, u32[]{:S(2)}) copy-start(bf16[2,1,64,2048]{3,2,1,0:T(8,128)(2,1)} %param.16) | copy-start | bytes 1572868
  630.7 21.7 %collective-permute-start.1 = (bf16[64,2048]{1,0:T(8,128)(2,1)}, bf16[64,2048]{1,0:T(8,128)(2,1)S(1)}, u32[]{:S(2)}, u32[]{:S(2)}) collective-permute-start(bf16[64,2048]{1,0:T(8,128)(2,1)} %reduce-scatter.7.cloned.1.call-done), channel_id=1, source_target_pairs={{0,0},{8,1},{16,2},{24,3},{1,4},{9,5},{17,6},{25,7},{2,8},{10,9},{... | collective-permute-start | bytes 786440 | tf_op jit(solution)/shard_map/ppermute | solution.py:565
  (3 other events, 2.3 us)
Sparse Core Ops, SparseCore 0:
  28.9 50.2 all-gather.4
  81.6 26.6 all-gather.6
  110.1 88.4 all-gather.8
  200.3 52.6 all-gather.10
  505.1 31.2 reduce-scatter.6
  551.9 43.2 reduce-scatter.4
  598.4 58.9 reduce-scatter.10
  660.5 88.5 reduce-scatter.8

commit v3 on v1

v3 whole, which is shorter than its diff:
```python
import functools

import jax
import jax.numpy as jnp
from jax import lax
from jax.experimental import pallas as pl
from jax.experimental.pallas import tpu as pltpu
from jax.sharding import PartitionSpec as P

HEADS = 16
HEAD_DIM = 128
eps_norm = 1e-06
rope_base = 500000.0
masked_value = -1e30
bf16 = jnp.bfloat16
f32 = jnp.float32
MESH = pl.DeviceIdType.MESH
ANY = pl.BlockSpec(memory_space=pl.ANY)
VM = pl.BlockSpec(memory_space=pltpu.VMEM)
DMA = pltpu.SemaphoreType.DMA
PACE = 1
CHUNKS = 4
SUB = 4


def params(cid, megabytes=None):
    limit = {} if megabytes is None else {"vmem_limit_bytes": megabytes * 2**20}
    return pltpu.CompilerParams(collective_id=cid, has_side_effects=True, **limit)


def cost(microseconds):
    return pl.CostEstimate(flops=0, transcendentals=0, bytes_accessed=int(microseconds * 3e6))


def remote(src, dst, send, recv, device):
    return pltpu.make_async_remote_copy(src, dst, send, recv, device_id=device, device_id_type=MESH)


def greet(targets):
    barrier = pltpu.get_barrier_semaphore()
    count = 0
    for cond, dev in targets:
        if cond is None:
            pl.semaphore_signal(barrier, inc=1, device_id=dev, device_id_type=MESH)
            count = count + 1
        else:

            @pl.when(cond)
            def _():
                pl.semaphore_signal(barrier, inc=1, device_id=dev, device_id_type=MESH)

            count = count + cond.astype(jnp.int32)
    pl.semaphore_wait(barrier, count)


class Line:
    def __init__(self, n_s):
        self.s = lax.axis_index("seq")
        self.nz = n_s // 2
        self.z, self.c = self.s // 2, self.s % 2
        self.mate_slot = self.s + 1 - 2 * self.c
        self.mate = {"seq": self.mate_slot}
        self.steps = (1, -1)
        self.more = (self.z < self.nz - 1, self.z > 0)
        self.next = ({"seq": self.s + 2}, {"seq": self.s - 2})

    def neighbours(self):
        return [(self.more[0], self.next[0]), (self.more[1], self.next[1]), (None, self.mate)]


class Gather:
    def __init__(self, line, own, out, chunks, send, recv, mate_send, mate_recv):
        self.line, self.own, self.out = line, own, out
        self.chunks, self.rows = chunks, own.shape[0] // chunks
        self.send, self.recv, self.mate_send, self.mate_recv = send, recv, mate_send, mate_recv

    def part(self, slot, k):
        return self.out.at[slot, pl.ds(k * self.rows, self.rows)]

    def source(self, d, k, slot):
        return self.own.at[pl.ds(k * self.rows, self.rows)] if d == 0 else self.part(slot, k)

    def hop(self, i, d, k, slot):
        return remote(self.source(d, k, slot), self.part(slot, k), self.send.at[i, d, k], self.recv.at[i, d, k], self.line.next[i])

    def share(self, i, d, k, slot):
        return remote(self.source(d, k, slot), self.part(slot, k), self.mate_send.at[i, d, k], self.mate_recv.at[i, d, k], self.line.mate)

    def start(self, k):
        line = self.line
        for i in range(2):

            @pl.when(line.more[i])
            def _():
                self.hop(i, 0, k, line.s).start()

        self.share(0, 0, k, line.s).start()

    def each(self, d, mine=True):
        line = self.line
        for i in range(2):
            origin = line.z - line.steps[i] * d
            yield i, (origin >= 0) & (origin < line.nz), 2 * origin + (line.c if mine else 1 - line.c)

    def pass_on(self, d, k):
        for i, there, slot in self.each(d):

            @pl.when(there)
            def _():
                self.hop(i, d - 1, k, slot).wait_recv()
                if d < self.line.nz - 1:

                    @pl.when(self.line.more[i])
                    def _():
                        self.hop(i, d, k, slot).start()

                self.share(i, d, k, slot).start()

    def finish(self):
        line = self.line
        for k in range(self.chunks):
            self.share(0, 0, k, line.mate_slot).wait_recv()
            for d in range(1, line.nz):
                for i, there, slot in self.each(d, False):

                    @pl.when(there)
                    def _():
                        self.share(i, d, k, slot).wait_recv()

        for k in range(self.chunks):
            self.share(0, 0, k, line.s).wait_send()
            for i in range(2):

                @pl.when(line.more[i])
                def _():
                    self.hop(i, 0, k, line.s).wait_send()

            for d in range(1, line.nz):
                for i, there, slot in self.each(d):

                    @pl.when(there)
                    def _():
                        self.share(i, d, k, slot).wait_send()
                        if d < line.nz - 1:

                            @pl.when(line.more[i])
                            def _():
                                self.hop(i, d, k, slot).wait_send()


class Scatter:
    def __init__(self, line, part, from_mate, run, chunks, send, recv, mate_send, mate_recv):
        self.line, self.part, self.from_mate, self.run = line, part, from_mate, run
        self.chunks, self.rows = chunks, part.shape[1] // chunks
        self.send, self.recv, self.mate_send, self.mate_recv = send, recv, mate_send, mate_recv
        self.steps = line.nz - 1
        self.groups = chunks // SUB
        self.count = self.steps * self.groups

    def span(self, k):
        return pl.ds(pl.multiple_of(k * self.rows, self.rows), self.rows)

    def give(self, zd, k):
        line, rs = self.line, self.span(k)
        return remote(self.part.at[2 * zd + 1 - line.c, rs], self.from_mate.at[zd, rs], self.mate_send.at[zd, k], self.mate_recv.at[zd, k], line.mate)

    def hop(self, i, zd, k):
        ref = self.run.at[i, zd, self.span(k)]
        return remote(ref, ref, self.send.at[i, zd, k], self.recv.at[i, zd, k], self.line.next[i])

    def pair(self, zd, k):
        rs = self.span(k)
        return self.part[2 * zd + self.line.c, rs].astype(f32) + self.from_mate[zd, rs].astype(f32)

    def start(self, k):
        nz = self.line.nz
        for zd in sorted(range(nz), key=lambda zd: (min(zd, nz - 1 - zd), -zd)):
            self.give(zd, k).start()

    def item(self, i, q, j):
        group, step = q // self.steps, lax.rem(q, self.steps)
        return (self.line.nz - 1 - step if i == 0 else step), group * SUB + j

    def slot(self, t):
        line = self.line
        for j, i in ((j, i) for j in range(SUB) for i in range(2)):
            q = t - (line.z if i == 0 else line.nz - 1 - line.z)
            behind = line.z > 0 if i == 0 else line.z < line.nz - 1
            zd, k = self.item(i, jnp.clip(q, 0, self.count - 1), j)
            going = (q >= 0) & (q < self.count) & (line.z < zd if i == 0 else line.z > zd)

            @pl.when(going)
            def _():
                rs = self.span(k)
                self.give(zd, k).wait_recv()

                @pl.when(behind)
                def _():
                    self.hop(i, zd, k).wait_recv()
                    self.run[i, zd, rs] = (self.pair(zd, k) + self.run[i, zd, rs].astype(f32)).astype(bf16)

                @pl.when(jnp.logical_not(behind))
                def _():
                    self.run[i, zd, rs] = self.pair(zd, k).astype(bf16)
                    if t >= PACE:
                        self.hop(i, *self.item(i, jnp.int32(t - PACE), j)).wait_send()

                self.hop(i, zd, k).start()

    def total(self, k, use):
        line, rs = self.line, self.span(k)
        for zd in range(line.nz):

            @pl.when(line.z == zd)
            def _():
                self.give(zd, k).wait_recv()
                total = self.pair(zd, k)
                if zd > 0:
                    self.hop(0, zd, k).wait_recv()
                    total = total + self.run[0, zd, rs].astype(f32)
                if zd < line.nz - 1:
                    self.hop(1, zd, k).wait_recv()
                    total = total + self.run[1, zd, rs].astype(f32)
                use(total)

    def finish(self):
        line = self.line
        for k in range(self.chunks):
            for zd in range(line.nz):
                self.give(zd, k).wait_send()
        for q in range(self.count):
            step = q % self.steps
            for i, zd in ((0, line.nz - 1 - step), (1, step)):
                going = line.z < zd if i == 0 else line.z > zd
                behind = line.z > 0 if i == 0 else line.z < line.nz - 1

                @pl.when(going & behind if q < self.count - PACE else going)
                def _():
                    for j in range(SUB):
                        self.hop(i, zd, q // self.steps * SUB + j).wait_send()


def line_sems(nz, chunks):
    return [DMA((2, nz, chunks))] * 4


def scatter_scratch(n_s, rows, width, chunks):
    nz = n_s // 2
    sums = [pltpu.VMEM((nz, rows, width), bf16), pltpu.VMEM((2, nz, rows, width), bf16)]
    return sums + [DMA((2, nz, chunks))] * 2 + [DMA((nz, chunks))] * 2


def mixed_rows(rs, total, x, gain, hidden, normed, inverse, low):
    inv = inverse_rms(total)
    n = total * inv
    out = x[rs].astype(f32) + n * gain[...]
    hidden[rs] = out
    normed[rs] = n
    inverse[rs] = inv
    low[rs] = out.astype(bf16)


def down_rows(rs, total, hidden, cotangent, gain, out, term, low):
    inv = inverse_rms(total)
    n = total * inv
    g = gain[...]
    out[rs] = (hidden[rs] + n * g).astype(bf16)
    grad = cotangent[rs].astype(f32)
    low[rs], more = back_rows(grad, n, inv, g)
    term[...] += more


def hidden_rows(rs, total, cotangent, normed, inverse, gain, d_hidden, term, low):
    grad = cotangent[rs].astype(f32) + total
    d_hidden[rs] = grad
    low[rs], more = back_rows(grad, normed[rs], inverse[rs], gain[...])
    term[...] += more


def back_rows(grad, n, inv, gain):
    scaled = grad * gain
    d = inv * (scaled - n * jnp.mean(scaled * n, axis=-1, keepdims=True))
    return d.astype(bf16), jnp.sum(grad * n, axis=0, keepdims=True)


def run_slots(scatter, use, gather=None):
    steps, groups = scatter.steps, scatter.groups
    for t in range(steps * (groups + (1 if gather else 0)) + 1):
        if t < steps * (groups + 1):
            scatter.slot(t)
        if gather:
            for group in range(groups):
                if 1 <= t - steps * (group + 1) <= steps:
                    for j in range(SUB):
                        gather.pass_on(t - steps * (group + 1), group * SUB + j)
        if t and t % steps == 0 and t // steps <= groups:
            for k in range((t // steps - 1) * SUB, t // steps * SUB):
                scatter.total(k, lambda total: use(k, total))
                if gather:
                    gather.start(k)


def around_kernel(n_s, chunks, rows_fn, n_in, n_out, adds, *refs):
    part, extra = refs[0], refs[1 : 1 + n_in]
    gathered, outs = refs[1 + n_in], refs[2 + n_in : 2 + n_in + n_out]
    low, local, from_mate, run, *sems = refs[2 + n_in + n_out :]
    line = Line(n_s)
    scatter = Scatter(line, part, from_mate, run, chunks, *sems[:4])
    gather = Gather(line, low, gathered, chunks, *sems[4:])
    greet(line.neighbours())
    for k in range(chunks):
        scatter.start(k)
    if adds:
        outs[-1][...] = jnp.zeros_like(outs[-1])
    run_slots(scatter, lambda k, total: rows_fn(scatter.span(k), total, *extra, *outs, low), gather)
    own = pltpu.make_async_copy(low, gathered.at[line.s], local)
    own.start()
    gather.finish()
    scatter.finish()
    own.wait()


def around(terms, extra, rows_fn, outs, n_s, cid, adds, chunks=CHUNKS):
    rows, width = terms.shape[0] // n_s, terms.shape[1]
    return pl.pallas_call(
        functools.partial(around_kernel, n_s, chunks, rows_fn, len(extra), len(outs), adds),
        out_shape=[jax.ShapeDtypeStruct((n_s, rows, width), bf16)] + [jax.ShapeDtypeStruct(*o) for o in outs],
        in_specs=[VM] * (1 + len(extra)),
        out_specs=[ANY] + [VM] * len(outs),
        scratch_shapes=[pltpu.VMEM((rows, width), bf16), DMA] + scatter_scratch(n_s, rows, width, chunks) + line_sems(n_s // 2, chunks),
        compiler_params=params(cid, 48),
        cost_estimate=cost(70),
    )(terms.reshape(n_s, rows, width), *extra)


def last_kernel(n_s, chunks, part, d_hidden, out, from_mate, run, *sems):
    line = Line(n_s)
    scatter = Scatter(line, part, from_mate, run, chunks, *sems)
    greet(line.neighbours())
    for k in range(chunks):
        scatter.start(k)

    def use(k, total):
        out[scatter.span(k)] = d_hidden[scatter.span(k)] + total

    run_slots(scatter, use)
    scatter.finish()


def last_sum(terms, d_hidden, n_s, cid, chunks=CHUNKS):
    rows, width = terms.shape[0] // n_s, terms.shape[1]
    return pl.pallas_call(
        functools.partial(last_kernel, n_s, chunks),
        out_shape=jax.ShapeDtypeStruct((rows, width), f32),
        in_specs=[VM, VM],
        out_specs=VM,
        scratch_shapes=scatter_scratch(n_s, rows, width, chunks),
        compiler_params=params(cid, 48),
        cost_estimate=cost(40),
    )(terms.reshape(n_s, rows, width), d_hidden)


class Columns:
    def __init__(self, n_s, plan, arrays, slots, back, send, recv, local):
        self.n_s, self.plan, self.arrays, self.slots, self.back = n_s, plan, arrays, slots, back
        self.send, self.recv, self.local = send, recv, local
        self.s = lax.axis_index("seq")

    def place(self, k):
        return lax.rem(self.s + k, self.n_s)

    def pieces(self, k):
        there = self.place(k)
        for array, parts in zip(self.arrays, self.plan):
            for first, width, column in parts:
                at = pl.ds(column, width)
                if self.back:
                    yield self.slots.at[there, :, at], array.at[:, pl.ds(pl.multiple_of(first(self.s), 128), width)]
                else:
                    yield array.at[:, pl.ds(pl.multiple_of(first(there), 128), width)], self.slots.at[self.s, :, at]

    def start(self):
        for k in range(1, self.n_s):
            for src, dst in self.pieces(k):
                remote(src, dst, self.send.at[k], self.recv.at[k], {"seq": self.place(k)}).start()
        for src, dst in self.pieces(0):
            pltpu.make_async_copy(src, dst, self.local).start()

    def finish(self):
        slot = self.slots.at[0]
        for k in range(1, self.n_s):
            done = remote(slot, slot, self.send.at[k], self.recv.at[k], {"seq": self.place(k)})
            done.wait_recv()
            done.wait_send()
        pltpu.make_async_copy(slot, slot, self.local).wait()


def columns_sems(n_s):
    return [DMA((n_s,)), DMA((n_s,)), DMA]


def seq_others(n_s):
    s = lax.axis_index("seq")
    return [(None, {"seq": lax.rem(s + k, n_s)}) for k in range(1, n_s)]


class Share:
    def __init__(self, n_w, n_s, whole, x, out, send, recv, local):
        self.n_w, self.n_s, self.whole = n_w, n_s, whole
        self.x, self.out, self.send, self.recv, self.local = x, out, send, recv, local
        self.w, self.s = lax.axis_index("wide"), lax.axis_index("seq")
        self.steps = [(a, b) for a in (range(n_w) if whole else (0,)) for b in range(n_s) if a or b]

    def at(self, a, b):
        return lax.rem(self.w + a, self.n_w), lax.rem(self.s + b, self.n_s)

    def number(self, a, b):
        w, s = self.at(a, b)
        return w * self.n_s + s if self.whole else s

    def name(self, a, b):
        w, s = self.at(a, b)
        return {"wide": w, "seq": s}

    def others(self):
        return [(None, self.name(a, b)) for a, b in self.steps]

    def block(self, a, b):
        return self.x.at[self.number(a, b)] if len(self.x.shape) == 3 else self.x

    def copy(self, a, b):
        i = a * self.n_s + b
        return remote(self.block(a, b), self.out.at[self.number(0, 0)], self.send.at[i], self.recv.at[i], self.name(a, b))

    def own(self):
        return pltpu.make_async_copy(self.block(0, 0), self.out.at[self.number(0, 0)], self.local)

    def start(self):
        for a, b in self.steps:
            self.copy(a, b).start()
        self.own().start()

    def finish(self):
        for a, b in self.steps:
            self.copy(a, b).wait()
        self.own().wait()


def share_kernel(n_w, n_s, whole, x_ref, o_ref, send, recv, local_sem):
    share = Share(n_w, n_s, whole, x_ref, o_ref, send, recv, local_sem)
    greet(share.others())
    share.start()
    share.finish()


def exchange(x, n_w, n_s, whole, cid):
    count = n_w * n_s if whole else n_s
    return pl.pallas_call(
        functools.partial(share_kernel, n_w, n_s, whole),
        out_shape=jax.ShapeDtypeStruct((count, *x.shape[-2:]), x.dtype),
        in_specs=[VM],
        out_specs=VM,
        scratch_shapes=[DMA((count,)), DMA((count,)), DMA],
        compiler_params=params(cid),
        cost_estimate=cost(10),
    )(x)


class Halves:
    def __init__(self, n_w, natural, heads, back, send, recv, local):
        s = lax.axis_index("seq")
        c = lax.rem(s, 2)
        self.back, self.count = back, n_w // 2
        self.send, self.recv, self.local = send, recv, local
        mate = {"seq": s + 1 - 2 * c}
        self.away, self.stay = [], []
        for i in range(self.count):
            mine, his = c * self.count + i, (1 - c) * self.count + i
            if back:
                pair = heads.at[i, 1 - c], natural.at[mine]
                own = heads.at[i, c], natural.at[mine]
            else:
                pair = natural.at[his], heads.at[i, c]
                own = natural.at[mine], heads.at[i, c]
            self.away.append(remote(*pair, send.at[i], recv.at[i], mate))
            self.stay.append(pltpu.make_async_copy(*own, local.at[i]))

    def start(self):
        for copy in self.away + self.stay:
            copy.start()

    def finish(self):
        for copy in self.away + self.stay:
            copy.wait()


def halves_sems(n_w):
    return [DMA((n_w // 2,))] * 3


def first_kernel(n_s, plan, qw, kw, vw, qkv, *sems):
    columns = Columns(n_s, plan, (qw, kw, vw), qkv, False, *sems)
    greet(seq_others(n_s))
    columns.start()
    columns.finish()


def first_exchange(weights, plan, cols, n_s, cid):
    return pl.pallas_call(
        functools.partial(first_kernel, n_s, plan),
        out_shape=jax.ShapeDtypeStruct((n_s, weights[0].shape[0], cols), bf16),
        in_specs=[ANY] * 3,
        out_specs=ANY,
        scratch_shapes=columns_sems(n_s),
        compiler_params=params(cid),
        cost_estimate=cost(20),
    )(*weights)


def second_kernel(n_w, n_s, chunks, plan, x, gw, uw, gain, x_all, slots, gains, own_sem, *sems):
    line = Line(n_s)
    gather = Gather(line, x, x_all, chunks, *sems[:4])
    columns = Columns(n_s, plan, (gw, uw), slots, False, *sems[4:7])
    share = Share(n_w, n_s, True, gain, gains, *sems[7:])
    greet(share.others())
    own = pltpu.make_async_copy(x, x_all.at[line.s], own_sem)
    for k in range(chunks):
        gather.start(k)
    own.start()
    share.start()
    columns.start()
    for d in range(1, line.nz):
        for k in range(chunks):
            gather.pass_on(d, k)
    gather.finish()
    own.wait()
    share.finish()
    columns.finish()


def second_exchange(x, weights, gain, plan, cols, n_w, n_s, cid, chunks=2):
    rows, width = x.shape
    count = n_w * n_s
    return pl.pallas_call(
        functools.partial(second_kernel, n_w, n_s, chunks, plan),
        out_shape=[
            jax.ShapeDtypeStruct((n_s, rows, width), bf16),
            jax.ShapeDtypeStruct((n_s, weights[0].shape[0], cols), bf16),
            jax.ShapeDtypeStruct((count, *gain.shape), gain.dtype),
        ],
        in_specs=[ANY] * 3 + [VM],
        out_specs=[ANY, ANY, VM],
        scratch_shapes=[DMA] + line_sems(n_s // 2, chunks) + columns_sems(n_s) + [DMA((count,)), DMA((count,)), DMA],
        compiler_params=params(cid),
        cost_estimate=cost(80),
    )(x, *weights, gain)


def back_kernel(n_s, plan, *refs):
    slots, arrays, sems = refs[0], refs[1 : 1 + len(plan)], refs[1 + len(plan) :]
    columns = Columns(n_s, plan, arrays, slots, True, *sems)
    greet(seq_others(n_s))
    columns.start()
    columns.finish()


def columns_back(slots, shapes, plan, n_s, cid):
    return pl.pallas_call(
        functools.partial(back_kernel, n_s, plan),
        out_shape=[jax.ShapeDtypeStruct(s, bf16) for s in shapes],
        in_specs=[ANY],
        out_specs=[ANY] * len(shapes),
        scratch_shapes=columns_sems(n_s),
        compiler_params=params(cid),
        cost_estimate=cost(40),
    )(slots)


def sums_kernel(n_w, n_s, back, x, given, all_x, made, *sems):
    share = Share(n_w, n_s, False, x, all_x, *sems[:3])
    halves = Halves(n_w, *((made, given) if back else (given, made)), back, *sems[3:])
    greet(share.others())
    share.start()
    halves.start()
    share.finish()
    halves.finish()


def sums_exchange(x, given, back, n_w, n_s, cid):
    rows, width = given.shape[-2:]
    made = (n_w, rows, width) if back else (n_w // 2, 2, rows, width)
    return pl.pallas_call(
        functools.partial(sums_kernel, n_w, n_s, back),
        out_shape=[jax.ShapeDtypeStruct((n_s, *x.shape), x.dtype), jax.ShapeDtypeStruct(made, bf16)],
        in_specs=[VM, VM],
        out_specs=[VM, VM],
        scratch_shapes=[DMA((n_s,)), DMA((n_s,)), DMA] + halves_sems(n_w),
        compiler_params=params(cid),
        cost_estimate=cost(10),
    )(x, given)


def final_kernel(n_w, n_s, plan, slots, terms, q, k, v, all_terms, *sems):
    columns = Columns(n_s, plan, (q, k, v), slots, True, *sems[:3])
    share = Share(n_w, n_s, True, terms, all_terms, *sems[3:])
    greet(share.others())
    share.start()
    columns.start()
    share.finish()
    columns.finish()


def final_exchange(slots, terms, width, plan, n_w, n_s, cid):
    mat = jax.ShapeDtypeStruct((slots.shape[1], width), bf16)
    return pl.pallas_call(
        functools.partial(final_kernel, n_w, n_s, plan),
        out_shape=[mat, mat, mat, jax.ShapeDtypeStruct(terms.shape, terms.dtype)],
        in_specs=[ANY, VM],
        out_specs=[ANY] * 3 + [VM],
        scratch_shapes=columns_sems(n_s) + [DMA((n_w * n_s,)), DMA((n_w * n_s,)), DMA],
        compiler_params=params(cid),
        cost_estimate=cost(20),
    )(slots, terms)


def dot(a, b):
    return jnp.dot(a, b, preferred_element_type=f32)


def dot_t(a, b):
    return lax.dot_general(a, b, (((1,), (1,)), ((), ())), preferred_element_type=f32)


def t_dot(a, b):
    return lax.dot_general(a, b, (((0,), (0,)), ((), ())), preferred_element_type=f32)


def turn(v, cosine, sine):
    return v * cosine + pltpu.roll(v, HEAD_DIM // 2, 1) * sine


def allowed_pairs(doc_q, doc_k, length):
    rows = lax.broadcasted_iota(jnp.int32, (length, length), 0)
    cols = lax.broadcasted_iota(jnp.int32, (length, length), 1)
    return (cols <= rows) & (doc_q == doc_k)


def attend_kernel(scale, ql, kl, vl, inv, gq, gk, cos, sin, doc_q, doc_k, att, q_out, k_out, v_out, lse):
    length = cos.shape[0]

    def flat(ref):
        return ref[...].reshape(length, -1)

    scales = flat(inv)
    q = turn(flat(ql) * scales[:, 0:1] * gq[...], cos[...], sin[...]).astype(bf16)
    k = turn(flat(kl) * scales[:, 1:2] * gk[...], cos[...], sin[...]).astype(bf16)
    v = flat(vl).astype(bf16)
    q_out[...] = q.reshape(q_out.shape)
    k_out[...] = k.reshape(k_out.shape)
    v_out[...] = v.reshape(v_out.shape)
    allowed = allowed_pairs(doc_q[0], doc_k[0], length)
    scores = jnp.where(allowed, dot_t(q, k) * scale, masked_value)
    top = jnp.max(scores, 1, keepdims=True)
    e = jnp.exp(scores - top)
    total = jnp.sum(e, 1, keepdims=True)
    probs = (e * (1.0 / total)).astype(bf16)
    att[...] = dot(probs, v).astype(bf16).reshape(att.shape)
    lse[...] = (top + jnp.log(total)).reshape(lse.shape)


def attend_back_kernel(scale, q, k, v, lse, da, cos, sin, doc_q, doc_k, dq_out, dk_out, dv_out):
    length = cos.shape[0]

    def flat(ref):
        return ref[...].reshape(length, -1)

    queries, keys, values, d_att = flat(q), flat(k), flat(v), flat(da)
    allowed = allowed_pairs(doc_q[0], doc_k[0], length)
    scores = jnp.where(allowed, dot_t(queries, keys) * scale, masked_value)
    probs = jnp.exp(scores - flat(lse))
    d_probs = dot_t(d_att, values)
    delta = jnp.sum(probs * d_probs, 1, keepdims=True)
    d_scores = (probs * (d_probs - delta)).astype(bf16)
    d_q = dot(d_scores, keys) * scale
    d_k = t_dot(d_scores, queries) * scale
    dv_out[...] = t_dot(probs.astype(bf16), d_att).astype(bf16).reshape(dv_out.shape)
    dq_out[...] = turn(d_q, cos[...], -sin[...]).reshape(dq_out.shape)
    dk_out[...] = turn(d_k, cos[...], -sin[...]).reshape(dk_out.shape)


def attention_specs(n_s, local, length):
    def tok(first):
        return pl.BlockSpec((n_s, 1, local, HEAD_DIM), lambda m, h: (0, m, 0, first + h))

    gain = pl.BlockSpec((1, HEAD_DIM), lambda m, h: (0, h))
    table = pl.BlockSpec((length, HEAD_DIM), lambda m, h: (0, 0))
    doc_q = pl.BlockSpec((1, length, 1), lambda m, h: (m, 0, 0))
    doc_k = pl.BlockSpec((1, 1, length), lambda m, h: (m, 0, 0))
    col = pl.BlockSpec((1, n_s, 1, local, 1), lambda m, h: (h, 0, m, 0, 0))
    return tok, gain, table, doc_q, doc_k, col


def attend(lin, inv, gains, tables, docs, heads, scale):
    n_s, micro, local, _ = lin.shape
    length = n_s * local
    tok, gain, table, doc_q, doc_k, col = attention_specs(n_s, local, length)
    inv_spec = pl.BlockSpec((n_s, 1, local, 2), lambda m, h: (0, m, 0, 0))
    out = jax.ShapeDtypeStruct((n_s, micro, local, heads * HEAD_DIM), bf16)
    return pl.pallas_call(
        functools.partial(attend_kernel, scale),
        grid=(micro, heads),
        out_shape=[out, out, out, out, jax.ShapeDtypeStruct((heads, n_s, micro, local, 1), f32)],
        in_specs=[tok(0), tok(heads), tok(2 * heads), inv_spec, gain, gain, table, table, doc_q, doc_k],
        out_specs=[tok(0)] * 4 + [col],
        compiler_params=pltpu.CompilerParams(vmem_limit_bytes=48 * 2**20),
    )(lin, lin, lin, inv, gains[0:1], gains[1:2], *tables, docs[:, :, None], docs[:, None, :])


def attend_back(q, k, v, lse, d_att, tables, docs, heads, scale):
    n_s, micro, local, width = q.shape
    length = n_s * local
    tok, gain, table, doc_q, doc_k, col = attention_specs(n_s, local, length)
    return pl.pallas_call(
        functools.partial(attend_back_kernel, scale),
        grid=(micro, heads),
        out_shape=[jax.ShapeDtypeStruct(q.shape, f32)] * 2 + [jax.ShapeDtypeStruct(q.shape, bf16)],
        in_specs=[tok(0)] * 3 + [col, tok(0), table, table, doc_q, doc_k],
        out_specs=[tok(0)] * 3,
        compiler_params=pltpu.CompilerParams(vmem_limit_bytes=48 * 2**20),
    )(q, k, v, lse, d_att, *tables, docs[:, :, None], docs[:, None, :])


def inverse_rms(values):
    return lax.rsqrt(jnp.mean(values * values, axis=-1, keepdims=True) + eps_norm)


def rotation_tables(positions):
    half_dim = HEAD_DIM // 2
    frequency = rope_base ** (-jnp.arange(half_dim, dtype=f32) * 2.0 / HEAD_DIM)
    angles = positions.astype(f32)[:, None] * frequency[None, :]
    cosine, sine = jnp.cos(angles), jnp.sin(angles)
    return jnp.concatenate([cosine, cosine], 1), jnp.concatenate([-sine, sine], 1)


def wide_gather(block):
    return lax.all_gather(block, "wide", axis=0, tiled=True)


def wide_scatter(partial):
    return lax.psum_scatter(partial.astype(bf16), "wide", scatter_dimension=0, tiled=True)


def after(value, *others):
    return lax.optimization_barrier((value, *others))[0]


def on_device(n_w, n_s, inputs, documents, cotangent, query_weight, key_weight, value_weight, output_weight,
              query_gain, key_gain, attention_gain, gate_weight, up_weight, down_weight, feed_gain):
    micro, _, local, width = inputs.shape
    tokens = micro * local
    all_tokens = n_s * tokens
    n_dev = n_w * n_s
    heads = HEADS // n_s
    cols = heads * HEAD_DIM
    row_len = documents.shape[2]
    feed = gate_weight.shape[1]
    feed_block = feed // n_dev
    half = n_w * feed_block
    rows = query_weight.shape[0]
    scale = HEAD_DIM ** (-0.5)
    s_index = lax.axis_index("seq")

    flat = inputs.reshape(tokens, width)
    cot = cotangent.reshape(tokens, width)
    halves = 2 * rows == HEAD_DIM and n_w == 2 * heads

    def head_of(s, i):
        return s // 2 + n_s // 2 * (lax.rem(s, 2) * heads + i) if halves else s * heads + i

    def head_column(i):
        return lambda s: head_of(s, i) * HEAD_DIM

    qkv_plan = [[(head_column(h), HEAD_DIM, i * cols + h * HEAD_DIM) for h in range(heads)] for i in range(3)]
    own_blocks = feed_block % 128 == 0
    moves = [(b, (b % n_w) * n_s + b // n_w) for b in range(n_dev)]
    back_moves = [(b, a) for a, b in moves]
    if own_blocks:
        feed_plan = [[(lambda s, a=a: (a * n_s + s) * feed_block, feed_block, i * half + a * feed_block) for a in range(n_w)] for i in range(2)]
    else:
        feed_plan = [[(lambda s: s * half, half, i * half)] for i in range(2)]

    own_gain = jnp.stack([query_gain, key_gain, attention_gain, feed_gain]).astype(f32)
    own_gain = jnp.pad(own_gain, ((0, 4), (0, 128 - rows)))
    qkv = first_exchange((query_weight, key_weight, value_weight), qkv_plan, 3 * cols, n_s, 0)
    qkv_all = wide_gather(qkv.reshape(n_s * rows, 3 * cols))
    if halves:
        out_halves = wide_gather(after(output_weight, qkv)).reshape(n_w, rows, width)
    else:
        out_all = wide_gather(lax.ppermute(output_weight, ("wide", "seq"), moves))
    x_all, gate_up, gains = second_exchange(after(flat, qkv), (gate_weight, up_weight), own_gain, feed_plan, 2 * half, n_w, n_s, 1)
    x_all = x_all.reshape(all_tokens, width)
    gate_up_all = wide_gather(gate_up.reshape(n_s * rows, 2 * half))
    down_block = after(down_weight, gate_up)
    if not own_blocks:
        down_block = lax.ppermute(down_block, ("wide", "seq"), moves)
    down_all = wide_gather(down_block)

    gains = jnp.swapaxes(gains[:, :4, :rows], 0, 1).reshape(4, width)

    def own_heads(v):
        return jnp.concatenate([lax.dynamic_slice_in_dim(v, head_of(s_index, i) * HEAD_DIM, HEAD_DIM, 1) for i in range(heads)], 1)

    own_gains = own_heads(gains)

    lin = dot(x_all, qkv_all)
    q_lin, k_lin = lin[:, :cols], lin[:, cols : 2 * cols]

    def stack_sums(a, b):
        return jnp.stack([a, b] + [jnp.zeros_like(a)] * 6)

    sums = stack_sums(jnp.sum(q_lin * q_lin, 1), jnp.sum(k_lin * k_lin, 1))
    if halves:
        sums, out_all = sums_exchange(sums, out_halves, False, n_w, n_s, 2)
        out_all = out_all.reshape(cols, width)
    else:
        sums = exchange(sums, n_w, n_s, False, 2)
    inv = lax.rsqrt(jnp.sum(sums, 0)[:2] / width + eps_norm).T
    tables = rotation_tables(jnp.arange(row_len, dtype=jnp.int32))
    docs = documents[:, 0, :]
    shape4 = (n_s, micro, local, -1)
    attended, q, k, v, lse = attend(lin.reshape(shape4), inv.reshape(shape4), own_gains, tables, docs, heads, scale)
    attended = attended.reshape(all_tokens, cols)

    own_f32 = ((tokens, width), f32)
    vec_f32 = ((1, width), f32)
    hidden_all, hidden, mixed_n, mixed_inv = around(
        dot(attended, out_all).astype(bf16), (flat, gains[2:3]), mixed_rows, [own_f32, own_f32, ((tokens, 1), f32)], n_s, 3, False
    )
    hidden_all = hidden_all.reshape(all_tokens, width)
    gate_up_lin = dot(hidden_all, gate_up_all)
    gate_lin, upward = gate_up_lin[:, :half], gate_up_lin[:, half:]
    sigma = jax.nn.sigmoid(gate_lin)
    silu_gate = gate_lin * sigma
    active = (silu_gate * upward).astype(bf16)
    d_down_all, layer_out, feed_term = around(
        dot(active, down_all).astype(bf16), (hidden, cot, gains[3:4]), down_rows, [((tokens, width), bf16), vec_f32], n_s, 4, True
    )
    d_down_all = d_down_all.reshape(all_tokens, width)
    down_part = t_dot(active, d_down_all).astype(bf16)
    down_grad = wide_scatter(down_part)
    d_active = dot_t(after(d_down_all, down_part), down_all)
    d_gate = (d_active * upward * sigma * (1.0 + gate_lin * (1.0 - sigma))).astype(bf16)
    d_up = (d_active * silu_gate).astype(bf16)
    d_gate_up = jnp.concatenate([d_gate, d_up], axis=1)
    mlp_part = t_dot(hidden_all, d_gate_up).astype(bf16)
    mlp_grad = wide_scatter(mlp_part)
    d_mixed_all, d_hidden, attention_term = around(
        dot_t(after(d_gate_up, mlp_part), gate_up_all).astype(bf16), (cot, mixed_n, mixed_inv, gains[2:3]), hidden_rows, [own_f32, vec_f32], n_s, 5, True
    )
    d_mixed_all = d_mixed_all.reshape(all_tokens, width)
    out_part = t_dot(attended, d_mixed_all).astype(bf16)
    d_attended = dot_t(d_mixed_all, out_all).astype(bf16).reshape(shape4)

    d_q, d_k, d_v = attend_back(q, k, v, lse, d_attended, tables, docs, heads, scale)
    d_q, d_k, d_v = (t.reshape(all_tokens, cols) for t in (d_q, d_k, d_v))
    q_n, k_n = q_lin * inv[:, 0:1], k_lin * inv[:, 1:2]
    d_qg, d_kg = d_q * own_gains[0], d_k * own_gains[1]
    mean_sums = stack_sums(jnp.sum(d_qg * q_n, 1), jnp.sum(d_kg * k_n, 1))
    if halves:
        mean_sums, out_part = sums_exchange(mean_sums, out_part.reshape(heads, 2, rows, width), True, n_w, n_s, 6)
    else:
        mean_sums = exchange(mean_sums, n_w, n_s, False, 6)
    means = jnp.sum(mean_sums, 0)[:2].T / width
    query_term = jnp.sum(d_q * q_n, 0)
    key_term = jnp.sum(d_k * k_n, 0)
    d_q_lin = (inv[:, 0:1] * (d_qg - q_n * means[:, 0:1])).astype(bf16)
    d_k_lin = (inv[:, 1:2] * (d_kg - k_n * means[:, 1:2])).astype(bf16)
    d_lin = jnp.concatenate([d_q_lin, d_k_lin, d_v], axis=1)
    qkv_part = t_dot(x_all, d_lin).astype(bf16)
    mlp_grad, down_grad, qkv_part, out_part = lax.optimization_barrier((mlp_grad, down_grad, qkv_part, out_part))
    input_grad = last_sum(dot_t(after(d_lin, qkv_part), qkv_all).astype(bf16), d_hidden, n_s, 7).reshape(inputs.shape)
    qkv_grad = wide_scatter(qkv_part)
    out_grad = wide_scatter(out_part.reshape(cols, width))
    if not halves:
        out_grad = lax.ppermute(out_grad, ("wide", "seq"), back_moves)

    gate_grad, up_grad = columns_back(
        after(mlp_grad, input_grad).reshape(n_s, rows, 2 * half), [(rows, feed)] * 2, feed_plan, n_s, 8
    )
    def spread(term):
        full = jnp.zeros((width,), f32)
        for i in range(heads):
            full = lax.dynamic_update_slice_in_dim(full, term[i * HEAD_DIM : (i + 1) * HEAD_DIM], head_of(s_index, i) * HEAD_DIM, 0)
        return full

    terms = jnp.stack([spread(query_term), spread(key_term), attention_term[0], feed_term[0]])
    terms = jnp.swapaxes(terms.reshape(4, n_dev, rows), 0, 1)
    terms = jnp.pad(terms, ((0, 0), (0, 4), (0, 128 - rows)))
    query_grad, key_grad, value_grad, all_terms = final_exchange(
        after(qkv_grad, gate_grad).reshape(n_s, rows, 3 * cols), terms, width, qkv_plan, n_w, n_s, 9
    )
    gain_grads = jnp.sum(all_terms, 0)[:4, :rows]
    if not own_blocks:
        down_grad = lax.ppermute(down_grad, ("wide", "seq"), back_moves)
    return (layer_out.reshape(inputs.shape), input_grad, *(g.astype(f32) for g in (query_grad, key_grad, value_grad, out_grad)),
            gain_grads[0], gain_grads[1], gain_grads[2], gate_grad.astype(f32), up_grad.astype(f32), down_grad.astype(f32), gain_grads[3])


def solution(mesh):
    tok = P(None, "wide", "seq", None)
    docs = P(None, "wide", None)
    mat = P(("wide", "seq"), None)
    vec = P(("wide", "seq"))

    def body(*args):
        return on_device(mesh.shape["wide"], mesh.shape["seq"], *args)

    return jax.shard_map(
        body,
        mesh=mesh,
        in_specs=(tok, docs, tok, mat, mat, mat, mat, vec, vec, vec, mat, mat, mat, vec),
        out_specs=(tok, tok, mat, mat, mat, mat, vec, vec, vec, mat, mat, mat, vec),
        check_vma=False,
    )
```

time: 1170 us -> 656 us (0.56)
  waiting for transfers between devices: 663 us -> 16.4 us
  Pallas kernels: 0 us -> 474 us
  blocking collectives: 175 us -> 0 us
  local copies, waits for them, and re-layouts: 120 us -> 16.2 us
  matrix products: 122 us -> 93.8 us
  starting transfers between devices: 28.4 us -> 0.94 us
  other arithmetic: 43.5 us -> 29.9 us
    pallas_call x0 -> x12, Pallas kernels: none -> 474 us  [the longest x3 207 us: around(): pl.pallas_call(functools.partial(around_kernel, n_s, chunks, rows_fn, len...]
    all_gather x4 -> x0, waiting for transfers between devices: 165 us -> none  [seq_gather(): return lax.all_gather(block, 'seq', axis=0, tiled=True)]
    reduce_scatter x4 -> x0, waiting for transfers between devices: 125 us -> none  [seq_scatter(): lax.psum_scatter(partial.astype(bf16), 'seq', scatter_dimension=0, tiled=...]
    unnamed x18 -> x8, waiting for transfers between devices: 126 us -> 2 us
    all_gather x4, waiting for transfers between devices: 120 us -> 14.4 us  [wide_gather(): return lax.all_gather(block, 'wide', axis=0, tiled=True)]
    all_to_all x2 -> x0, blocking collectives: 105 us -> none  [the longest x1 81.1 us: on_device(): gate_up = lax.all_to_all(gate_up, 'seq', 0, 0, tiled=True)]
    reduce_scatter x4, waiting for transfers between devices: 102 us -> 0.01 us  [wide_scatter(): lax.psum_scatter(partial.astype(bf16), 'wide', scatter_dimension=0, tiled...]
    all_gather x1 -> x0, blocking collectives: 47.4 us -> none  [on_device(): lax.all_gather(jnp.stack([query_gain, key_gain, attention_gain, feed_gain...]
  transfers between devices with their start and end apart: 21 -> 8, of which waited for: 15 -> 1; matrix products, arithmetic and copies ran while one was open for 18% -> 16% of each run, Pallas kernels for 0% -> 55%
where the time goes in v3:
time: 656 us; the launch traced here: 646 us
  Pallas kernels  474 us (72%)
  matrix products  93.8 us (14%)
  other arithmetic  29.9 us (5%)
  waiting for transfers between devices  16.4 us (2%)
  local copies, waits for them, and re-layouts  16.2 us (2%)
  between operations  15 us (2%)
    pallas_call x3, Pallas kernels, around(): pl.pallas_call(functools.partial(around_kernel, n_s, chunks, rows_fn, len...  207 us
    pallas_call x1, Pallas kernels, second_exchange(): pl.pallas_call(functools.partial(second_kernel, n_w, n_s, chunks, plan),...  83.9 us
    pallas_call x1, Pallas kernels, columns_back(): pl.pallas_call(functools.partial(back_kernel, n_s, plan), out_shape=[jax....  48.5 us
    pallas_call x1, Pallas kernels, last_sum(): pl.pallas_call(functools.partial(last_kernel, n_s, chunks), out_shape=jax...  40.5 us
    dot_general x4, matrix products, dot_t(): lax.dot_general(a, b, (((1,), (1,)), ((), ())), preferred_element_type=f32)  35.6 us
    pallas_call x2, Pallas kernels, sums_exchange(): pl.pallas_call(functools.partial(sums_kernel, n_w, n_s, back), out_shape=...  32.1 us
    dot_general x4, matrix products, dot(): return jnp.dot(a, b, preferred_element_type=f32)  31.3 us
    dot_general x4, matrix products, t_dot(): lax.dot_general(a, b, (((0,), (0,)), ((), ())), preferred_element_type=f32)  26.9 us
  transfers between devices with their start and end apart: 8, of which 1 were waited for; matrix products, arithmetic and copies ran while one was open for 16% of the time, Pallas kernels for 55%

profile of v3, /device:TPU:9, one launch (start us, length us, event | category | flops | bytes accessed | tf_op | source)
XLA Modules:
  0.0 646.5 jit_solution(2051941508264906089)
XLA Ops:
  7.2 21.4 %shard_map.237 = bf16[8,64,768]{2,1,0:T(8,128)(2,1)} custom-call(bf16[64,2048]{1,0:T(8,128)(2,1)} %qw.1, bf16[64,2048]{1,0:T(8,128)(2,1)} %kw.1, bf16[64,2048]{1,0:T(8,128)(2,1)} %vw.1), custom_call_target="tpu_custom_call" | custom-call | bytes 60000000 | tf_op jit(solution)/shard_map/pallas_call | solution.py:509
  29.5 1.3 fusion.17.gain
  30.8 83.9 %shard_map.238 = (bf16[8,128,2048]{2,1,0:T(8,128)(2,1)}, bf16[8,64,2048]{2,1,0:T(8,128)(2,1)}, f32[32,8,128]{2,1,0:T(8,128)}) custom-call(bf16[128,2048]{1,0:T(8,128)(2,1)} %bitcast.109, bf16[64,8192]{1,0:T(8,128)(2,1)} %gw.1, bf16[64,8192]{1,0:T(8,128)(2,1)} %uw.1, f32[8,128]{1,0:T(8,128)} %fusion.17.gain), custom_call_target="tpu_custom_call" | custom-call | bytes 240000000 | tf_op jit(solution)/shard_map/pallas_call | solution.py:544
  115.6 0.9 slice_bitcast_fusion
  117.1 1.0 fusion.3
  118.4 6.1 fusion.23
  124.6 1.7 copy-done.20
  127.3 16.7 %shard_map.239 = (f32[8,8,1024]{2,1,0:T(8,128)}, bf16[2,2,64,2048]{3,2,1,0:T(8,128)(2,1)}) custom-call(f32[8,1024]{1,0:T(8,128)} %maximum_maximum_fusion.x, bf16[4,64,2048]{2,1,0:T(8,128)(2,1)} %bitcast.134), custom_call_target="tpu_custom_call" | custom-call | bytes 30000000 | tf_op jit(solution)/shard_map/pallas_call | solution.py:592
  144.0 1.0 reduce_sum.83
  145.3 7.4 %shard_map.240 = (bf16[8,2,64,256]{3,2,1,0:T(8,128)(2,1)S(1)}, bf16[8,2,64,256]{3,2,1,0:T(8,128)(2,1)S(1)}, bf16[8,2,64,256]{3,2,1,0:T(8,128)(2,1)S(1)}, bf16[8,...) custom-call(f32[8,2,64,768]{3,2,1,0:T(8,128)} %bitcast.124, f32[8,2,64,768]{3,2,1,0:T(8,128)} %bitcast.125, ...), custom_call_target="tpu_custom_call" | custom-call | tf_op jit(solution)/shard_map/pallas_call | solution.py:709
  154.3 3.3 convolution_convert_fusion.2
  157.5 68.0 %shard_map.241 = (bf16[8,128,2048]{2,1,0:T(8,128)(2,1)}, f32[128,2048]{1,0:T(8,128)S(1)}, f32[128,2048]{1,0:T(8,128)S(1)}, f32[128,1]{1,0:T(8,128)S(1)}) custom-call(bf16[8,128,2048]{2,1,0:T(8,128)(2,1)} %bitcast.127, bf16[128,2048]{1,0:T(8,128)(2,1)S(1)} %bitcast.110, f32[1,2048]{1,0:T(1,128)S(1)} %slice.92.refs_2_.refs_4_), custom_call_target="tpu_custom_call" | custom-call | bytes 210000000 | tf_op jit(solution)/shard_map/pallas_call | solution.py:325
  225.6 1.0 copy-done.7
  226.5 12.5 %fusion.24 = f32[1024,2048]{1,0:T(8,128)S(1)} fusion(bf16[1024,2048]{1,0:T(8,128)(2,1)} %bitcast.157, bf16[2048,2048]{1,0:T(8,128)(2,1)} %all-gather.9.cloned.1.call-done), kind=kOutput, calls=%fused_computation.80 | convolution fusion | flops 8589934592 | bytes 20971520 | tf_op jit(solution)/shard_map/dot_general | solution.py:627
  239.0 3.2 copy-done.22
  242.3 2.7 multiply_convert_fusion.2
  245.0 14.4 %all-gather.11.cloned.1.call-done = bf16[1024,2048]{1,0:T(8,128)(2,1)} async-done(((bf16[256,2048]{1,0:T(8,128)(2,1)}), bf16[1024,2048]{1,0:T(8,128)(2,1)}) %all-gather.11.cloned.1.call-update) | async-done | bytes 4194320 | tf_op jit(solution)/shard_map/all_gather | solution.py:746
  259.4 9.4 %convolution_convert_fusion.5 = bf16[1024,2048]{1,0:T(8,128)(2,1)} fusion(bf16[1024,1024]{1,0:T(8,128)(2,1)} %multiply_convert_fusion.2, bf16[1024,2048]{1,0:T(8,128)(2,1)} %all-gather.11.cloned.1.call-done), kind=kOutput, calls=%fused_computation.11 | convolution fusion | flops 4297064448 | bytes 10485760 | tf_op jit(solution)/shard_map/dot_general | solution.py:627
  268.8 68.8 %shard_map.242 = (bf16[8,128,2048]{2,1,0:T(8,128)(2,1)}, bf16[128,2048]{1,0:T(8,128)(2,1)S(1)}, f32[1,2048]{1,0:T(1,128)S(1)}) custom-call(bf16[8,128,2048]{2,1,0:T(8,128)(2,1)} %bitcast.130, f32[128,2048]{1,0:T(8,128)S(1)} %copy-done.8, bf16[128,2048]{1,0:T(8,128)(2,1)S(1)} %bitcast.112, f32[1,2048]{1,0:T(1,128)S(1)} %slice.96.refs_3_), custom_call_target="tpu_custom_call" | custom-call | bytes 210000000 | tf_op jit(solution)/shard_map/pallas_call | solution.py:325
  338.4 8.4 %convolution_convert_fusion.4 = bf16[1024,2048]{1,0:T(8,128)(2,1)} fusion(bf16[1024,1024]{1,0:T(8,128)(2,1)S(1)} %copy-done.23, bf16[1024,2048]{1,0:T(8,128)(2,1)} %bitcast.161), kind=kOutput, calls=%fused_computation.10 | convolution fusion | flops 4297064448 | bytes 10485760 | tf_op jit(solution)/shard_map/dot_general | solution.py:635
  347.1 11.8 %multiply_convert_fusion.1 = (bf16[1024,1024]{1,0:T(8,128)(2,1)S(1)}, bf16[1024,1024]{1,0:T(8,128)(2,1)S(1)}) fusion(f32[1024,2048]{1,0:T(8,128)} %copy-done.22, bf16[1024,2048]{1,0:T(8,128)(2,1)} %bitcast.162, bf16[1024,2048]{1,0:T(8,128)(2,1)} %all-gather.11.cloned.1.call-done), kind=kOutput, calls=%fused_computation.3 | convolution fusion | flops 4308598784 | bytes 20971520 | tf_op jit(solution)/shard_map/dot_general | solution.py:631
  359.0 1.3 copy-done.26
  361.0 11.4 %convolution_convert_fusion = bf16[2048,2048]{1,0:T(8,128)(2,1)} fusion(bf16[1024,2048]{1,0:T(8,128)(2,1)S(1)} %bitcast.158, bf16[1024,1024]{1,0:T(8,128)(2,1)S(1)} %get-tuple-element.136, bf16[1024,1024]{1,0:T(8,128)(2,1)S(1)} %get-tuple-element.135), kind=kOutput, calls=%fused_computation | convolution fusion | flops 8602517504 | bytes 16777216 | tf_op jit(solution)/shard_map/dot_general | solution.py:635
  372.8 2.6 pad_maximum_fusion
  375.5 12.7 %convolution_convert_fusion.1 = bf16[1024,2048]{1,0:T(8,128)(2,1)} fusion(bf16[1024,2048]{1,0:T(8,128)(2,1)S(1)} %pad_maximum_fusion, bf16[2048,2048]{1,0:T(8,128)(2,1)} %all-gather.9.cloned.1.call-done), kind=kOutput, calls=%fused_computation.7 | convolution fusion | flops 8592031744 | bytes 16777216 | tf_op jit(solution)/shard_map/dot_general | solution.py:631
  388.2 70.4 %shard_map.243 = (bf16[8,128,2048]{2,1,0:T(8,128)(2,1)}, f32[128,2048]{1,0:T(8,128)S(1)}, f32[1,2048]{1,0:T(1,128)S(1)}) custom-call(bf16[8,128,2048]{2,1,0:T(8,128)(2,1)} %bitcast.129, bf16[128,2048]{1,0:T(8,128)(2,1)S(1)} %bitcast.113, f32[128,2048]{1,0:T(8,128)S(1)} %get-tuple-element.75.refs_2_, f32[128,1]{1,0:T(8,128)S(1)} %get-tuple-element.76.refs_3_, ...), custom_call_target="tpu_custom_call" | custom-call | bytes 210000000 | tf_op jit(solution)/shard_map/pallas_call | solution.py:325
  458.6 4.0 convolution_convert_fusion.8
  462.7 7.1 %shard_map.244 = (f32[8,2,64,256]{3,2,1,0:T(8,128)S(1)}, f32[8,2,64,256]{3,2,1,0:T(8,128)S(1)}, bf16[8,2,64,256]{3,2,1,0:T(8,128)(2,1)S(1)}) custom-call(bf16[8,2,64,256]{3,2,1,0:T(8,128)(2,1)S(1)} %copy-done.10, bf16[8,2,64,256]{3,2,1,0:T(8,128)(2,1)S(1)} %copy-done.12, bf16[8,2,64,256]{3,2,1,0:T(8,128)(2,1)S(1)} %copy-done.14, ...), custom_call_target="tpu_custom_call" | custom-call | tf_op jit(solution)/shard_map/pallas_call | solution.py:723
  469.8 0.9 fusion.2
  471.4 2.2 convolution_convert_fusion.7
  473.6 15.4 %shard_map.245 = (f32[8,8,1024]{2,1,0:T(8,128)}, bf16[4,64,2048]{2,1,0:T(8,128)(2,1)}) custom-call(f32[8,1024]{1,0:T(8,128)} %maximum_maximum_fusion.1.x, bf16[2,2,64,2048]{3,2,1,0:T(8,128)(2,1)} %bitcast.136), custom_call_target="tpu_custom_call" | custom-call | bytes 30000000 | tf_op jit(solution)/shard_map/pallas_call | solution.py:592
  489.1 1.0 reduce_sum.86
  490.1 2.3 multiply_convert_fusion.4
  493.2 4.9 convolution_convert_fusion.6
  499.9 7.1 %convolution_convert_fusion.3 = bf16[1024,2048]{1,0:T(8,128)(2,1)} fusion(bf16[1024,768]{1,0:T(8,128)(2,1)S(1)} %pad_maximum_fusion.1, bf16[2048,768]{1,0:T(8,128)(2,1)} %all-gather.5.cloned.1.call-done), kind=kOutput, calls=%fused_computation.9 | convolution fusion | flops 3223322624 | bytes 8912896 | tf_op jit(solution)/shard_map/dot_general | solution.py:631
  507.0 40.5 %shard_map.246 = f32[128,2048]{1,0:T(8,128)S(1)} custom-call(bf16[8,128,2048]{2,1,0:T(8,128)(2,1)} %bitcast.128, f32[128,2048]{1,0:T(8,128)S(1)} %copy-done.6), custom_call_target="tpu_custom_call" | custom-call | bytes 120000000 | tf_op jit(solution)/shard_map/pallas_call | solution.py:352
  547.5 48.5 %shard_map.247 = (bf16[64,8192]{1,0:T(8,128)(2,1)}, bf16[64,8192]{1,0:T(8,128)(2,1)}) custom-call(bf16[8,64,2048]{2,1,0:T(8,128)(2,1)} %bitcast.133), custom_call_target="tpu_custom_call" | custom-call | bytes 120000000 | tf_op jit(solution)/shard_map/pallas_call | solution.py:568
  596.0 2.7 convert_element_type.100
  598.7 2.7 convert_element_type.101
  601.4 1.6 convert_element_type.102
  602.9 1.8 convert_element_type.99
  604.7 26.1 %shard_map.248 = (bf16[64,2048]{1,0:T(8,128)(2,1)}, bf16[64,2048]{1,0:T(8,128)(2,1)}, bf16[64,2048]{1,0:T(8,128)(2,1)}, f32[32,8,128]{2,1,0:T(8,128)}) custom-call(bf16[8,64,768]{2,1,0:T(8,128)(2,1)} %bitcast.139, f32[32,8,128]{2,1,0:T(8,128)} %pad.12.terms), custom_call_target="tpu_custom_call" | custom-call | bytes 60000000 | tf_op jit(solution)/shard_map/pallas_call | solution.py:615
  630.8 1.8 convert_element_type.96
  632.6 1.8 convert_element_type.97
  634.4 1.8 convert_element_type.98
  636.2 0.9 reduce_sum.89
  637.6 0.8 copy.54
  638.4 1.0 copy.55
  (123 shorter events, 11.5 us)
Async XLA Ops:
  7.2 109.4 %copy-start.19 = (s32[2,1,512]{2,1,0:T(1,128)S(1)}, s32[2,1,512]{2,1,0:T(1,128)}, u32[]{:S(2)}) copy-start(s32[2,1,512]{2,1,0:T(1,128)} %doc_k.3) | copy-start | bytes 12292
  7.2 111.2 %all-gather.5.cloned.1.call-start = ((), (), s32[]{:S(2)}) async-start(), calls=%async_computation.4 | async-start | bytes 3932160 | tf_op jit(solution)/shard_map/all_gather | solution.py:746
  28.7 98.6 %all-gather.7.cloned.1.call-start = ((), (), s32[]{:S(2)}) async-start(), calls=%async_computation.5 | async-start | bytes 1310720 | tf_op jit(solution)/shard_map/all_gather | solution.py:746
  29.5 197.1 %all-gather.9.cloned.1.call-start = ((), (), s32[]{:S(2)}) async-start(), calls=%async_computation.6 | async-start | bytes 10485760 | tf_op jit(solution)/shard_map/all_gather | solution.py:746
  114.7 144.6 %all-gather.11.cloned.1.call-start = ((), (), s32[]{:S(2)}) async-start(), calls=%async_computation.7 | async-start | bytes 5242880 | tf_op jit(solution)/shard_map/all_gather | solution.py:746
  115.3 382.7 %reduce-scatter.7.cloned.1.call-start = ((), (), s32[]{:S(2)}) async-start(), calls=%async_computation.9 | async-start | bytes 5242880 | tf_op jit(solution)/shard_map/reduce_scatter | solution.py:750
  124.6 1.7 copy-start.20
  145.3 9.0 %copy-start.29 = (bf16[2,2,64,2048]{3,2,1,0:T(8,128)(2,1)S(1)}, bf16[2,2,64,2048]{3,2,1,0:T(8,128)(2,1)}, u32[]{:S(2)}) copy-start(bf16[2,2,64,2048]{3,2,1,0:T(8,128)(2,1)} %get-tuple-element.62) | copy-start | bytes 3145732
  152.7 0.8 copy-start.9
  153.5 0.8 copy-start.2
  153.5 4.1 copy-start.4
  153.5 4.1 copy-start.11
  153.5 4.1 copy-start.13
  153.5 4.1 copy-start
  225.6 1.0 copy-start.7
  239.0 3.2 copy-start.22
  245.0 23.8 %copy-start.1 = (bf16[2,1,64,2048]{3,2,1,0:T(8,128)(2,1)S(1)}, bf16[2,1,64,2048]{3,2,1,0:T(8,128)(2,1)}, u32[]{:S(2)}) copy-start(bf16[2,1,64,2048]{3,2,1,0:T(8,128)(2,1)} %param.16) | copy-start | bytes 1572868
  259.4 9.4 %copy-start.8 = (f32[128,2048]{1,0:T(8,128)S(1)}, f32[128,2048]{1,0:T(8,128)}, u32[]{:S(2)}) copy-start(f32[128,2048]{1,0:T(8,128)} %copy-done.7) | copy-start | bytes 3145732
  268.8 69.7 %copy-start.23 = (bf16[1024,1024]{1,0:T(8,128)(2,1)S(1)}, bf16[1024,1024]{1,0:T(8,128)(2,1)}, u32[]{:S(2)}) copy-start(bf16[1024,1024]{1,0:T(8,128)(2,1)} %multiply_convert_fusion.2) | copy-start | bytes 6291460
  337.6 0.8 copy-start.15
  346.9 151.2 %reduce-scatter.5.cloned.1.call-start = ((), (), s32[]{:S(2)}) async-start(), calls=%async_computation.8 | async-start | bytes 10485760 | tf_op jit(solution)/shard_map/reduce_scatter | solution.py:750
  347.1 13.8 %copy-start.32 = (bf16[8,128,2048]{2,1,0:T(8,128)(2,1)S(1)}, bf16[8,128,2048]{2,1,0:T(8,128)(2,1)}, u32[]{:S(2)}) copy-start(bf16[8,128,2048]{2,1,0:T(8,128)(2,1)} %get-tuple-element.63) | copy-start | bytes 12582916
  358.9 1.3 copy-start.26
  359.0 2.0 copy-start.27
  372.3 230.6 %reduce-scatter.11.cloned.1.call-start = ((), (), s32[]{:S(2)}) async-start(), calls=%async_computation.11 | async-start | bytes 1310720 | tf_op jit(solution)/shard_map/reduce_scatter | solution.py:750
  388.2 70.4 %copy-start.30 = (bf16[2,2,64,2048]{3,2,1,0:T(8,128)(2,1)S(1)}, bf16[2,2,64,2048]{3,2,1,0:T(8,128)(2,1)}, u32[]{:S(2)}) copy-start(bf16[2,2,64,2048]{3,2,1,0:T(8,128)(2,1)} %get-tuple-element.62) | copy-start | bytes 3145732
  458.6 4.0 copy-start.5
  458.6 4.0 copy-start.10
  458.6 4.0 copy-start.12
  458.6 4.0 copy-start.14
  462.6 7.2 %copy-start.21 = (f32[1024,768]{1,0:T(8,128)S(1)}, f32[1024,768]{1,0:T(8,128)}, u32[]{:S(2)}) copy-start(f32[1024,768]{1,0:T(8,128)} %copy-done.20) | copy-start | bytes 9437188
  462.6 8.7 %copy-start.3 = (bf16[8,2,64,256]{3,2,1,0:T(8,128)(2,1)S(1)}, bf16[8,2,64,256]{3,2,1,0:T(8,128)(2,1)}, u32[]{:S(2)}) copy-start(bf16[8,2,64,256]{3,2,1,0:T(8,128)(2,1)} %copy-done.2) | copy-start | bytes 1572868
  462.7 8.7 %copy-start.33 = (bf16[8,128,2048]{2,1,0:T(8,128)(2,1)S(1)}, bf16[8,128,2048]{2,1,0:T(8,128)(2,1)}, u32[]{:S(2)}) copy-start(bf16[8,128,2048]{2,1,0:T(8,128)(2,1)} %get-tuple-element.77) | copy-start | bytes 12582916
  469.8 3.8 copy-start.17
  473.6 19.5 %copy-start.18 = (bf16[8,2,64,256]{3,2,1,0:T(8,128)(2,1)S(1)}, bf16[8,2,64,256]{3,2,1,0:T(8,128)(2,1)}, u32[]{:S(2)}) copy-start(bf16[8,2,64,256]{3,2,1,0:T(8,128)(2,1)} %copy-done.17) | copy-start | bytes 1572868
  490.0 3.1 copy-start.31
  492.4 0.8 copy-start.24
  498.0 1.7 copy-start.25
  498.1 106.6 %reduce-scatter.9.cloned.1.call-start = ((), (), s32[]{:S(2)}) async-start(), calls=%async_computation.10 | async-start | bytes 3932160 | tf_op jit(solution)/shard_map/reduce_scatter | solution.py:750
  499.9 7.1 %copy-start.6 = (f32[128,2048]{1,0:T(8,128)S(1)}, f32[128,2048]{1,0:T(8,128)}, u32[]{:S(2)}) copy-start(f32[128,2048]{1,0:T(8,128)} %copy-done.5) | copy-start | bytes 3145732
  547.5 53.9 %copy-start.28 = (bf16[256,2048]{1,0:T(8,128)(2,1)S(1)}, bf16[256,2048]{1,0:T(8,128)(2,1)}, u32[]{:S(2)}) copy-start(bf16[256,2048]{1,0:T(8,128)(2,1)} %reduce-scatter.7.cloned.1.call-done) | copy-start | bytes 3145732
  601.4 36.3 %copy-start.16 = (bf16[128,2048]{1,0:T(8,128)(2,1)S(1)}, bf16[128,2048]{1,0:T(8,128)(2,1)}, u32[]{:S(2)}) copy-start(bf16[128,2048]{1,0:T(8,128)(2,1)} %copy-done.15) | copy-start | bytes 1572868
Sparse Core Ops, SparseCore 0:
  28.8 45.0 all-gather.4
  75.8 26.4 all-gather.6
  114.9 90.0 all-gather.8
  206.6 52.6 all-gather.10
  347.0 54.9 reduce-scatter.6
  405.2 86.3 reduce-scatter.4
  498.2 26.8 reduce-scatter.10
  528.4 43.9 reduce-scatter.8

commit v4 on v3

--- a/solution.py
+++ b/solution.py
@@ -32,6 +32,10 @@
     return pl.CostEstimate(flops=0, transcendentals=0, bytes_accessed=int(microseconds * 3e6))
 
 
+def far_first(n_s):
+    return sorted(range(n_s), key=lambda k: -min(k, n_s - k))
+
+
 def remote(src, dst, send, recv, device):
     return pltpu.make_async_remote_copy(src, dst, send, recv, device_id=device, device_id_type=MESH)
 
@@ -283,9 +287,10 @@
     return d.astype(bf16), jnp.sum(grad * n, axis=0, keepdims=True)
 
 
-def run_slots(scatter, use, gather=None):
+def run_slots(scatter, use, gather=None, work=None):
     steps, groups = scatter.steps, scatter.groups
-    for t in range(steps * (groups + (1 if gather else 0)) + 1):
+    slots = steps * (groups + (1 if gather else 0)) + 1
+    for t in range(slots):
         if t < steps * (groups + 1):
             scatter.slot(t)
         if gather:
@@ -298,12 +303,34 @@
                 scatter.total(k, lambda total: use(k, total))
                 if gather:
                     gather.start(k)
-
-
-def around_kernel(n_s, chunks, rows_fn, n_in, n_out, adds, *refs):
+        if work:
+            work(t, slots)
+
+
+def product_work(left, right, out):
+    size = 128
+    count = out.shape[0] // size
+
+    def work(t, slots):
+        for i in range(count * t // slots, count * (t + 1) // slots):
+            rs = pl.ds(i * size, size)
+            out[rs] = lax.dot_general(left[:, rs], right[...], (((0,), (0,)), ((), ())), preferred_element_type=f32).astype(bf16)
+
+    return work
+
+
+def around_kernel(n_s, chunks, rows_fn, n_in, n_out, adds, with_work, *refs):
     part, extra = refs[0], refs[1 : 1 + n_in]
-    gathered, outs = refs[1 + n_in], refs[2 + n_in : 2 + n_in + n_out]
-    low, local, from_mate, run, *sems = refs[2 + n_in + n_out :]
+    refs = refs[1 + n_in :]
+    work = None
+    if with_work:
+        left, right, gathered, *outs, made = refs[: 4 + n_out]
+        work = product_work(left, right, made)
+        refs = refs[4 + n_out :]
+    else:
+        gathered, *outs = refs[: 1 + n_out]
+        refs = refs[1 + n_out :]
+    low, local, from_mate, run, *sems = refs
     line = Line(n_s)
     scatter = Scatter(line, part, from_mate, run, chunks, *sems[:4])
     gather = Gather(line, low, gathered, chunks, *sems[4:])
@@ -312,7 +339,7 @@
         scatter.start(k)
     if adds:
         outs[-1][...] = jnp.zeros_like(outs[-1])
-    run_slots(scatter, lambda k, total: rows_fn(scatter.span(k), total, *extra, *outs, low), gather)
+    run_slots(scatter, lambda k, total: rows_fn(scatter.span(k), total, *extra, *outs, low), gather, work)
     own = pltpu.make_async_copy(low, gathered.at[line.s], local)
     own.start()
     gather.finish()
@@ -320,17 +347,18 @@
     own.wait()
 
 
-def around(terms, extra, rows_fn, outs, n_s, cid, adds, chunks=CHUNKS):
+def around(terms, extra, rows_fn, outs, n_s, cid, adds, pair=(), chunks=CHUNKS):
     rows, width = terms.shape[0] // n_s, terms.shape[1]
+    shapes = [((n_s, rows, width), bf16), *outs] + ([((pair[0].shape[1], pair[1].shape[1]), bf16)] if pair else [])
     return pl.pallas_call(
-        functools.partial(around_kernel, n_s, chunks, rows_fn, len(extra), len(outs), adds),
-        out_shape=[jax.ShapeDtypeStruct((n_s, rows, width), bf16)] + [jax.ShapeDtypeStruct(*o) for o in outs],
-        in_specs=[VM] * (1 + len(extra)),
-        out_specs=[ANY] + [VM] * len(outs),
+        functools.partial(around_kernel, n_s, chunks, rows_fn, len(extra), len(outs), adds, bool(pair)),
+        out_shape=[jax.ShapeDtypeStruct(*o) for o in shapes],
+        in_specs=[VM] * (1 + len(extra) + len(pair)),
+        out_specs=[ANY] + [VM] * (len(shapes) - 1),
         scratch_shapes=[pltpu.VMEM((rows, width), bf16), DMA] + scatter_scratch(n_s, rows, width, chunks) + line_sems(n_s // 2, chunks),
         compiler_params=params(cid, 48),
         cost_estimate=cost(70),
-    )(terms.reshape(n_s, rows, width), *extra)
+    )(terms.reshape(n_s, rows, width), *extra, *pair)
 
 
 def last_kernel(n_s, chunks, part, d_hidden, out, from_mate, run, *sems):
@@ -380,7 +408,7 @@
                     yield array.at[:, pl.ds(pl.multiple_of(first(there), 128), width)], self.slots.at[self.s, :, at]
 
     def start(self):
-        for k in range(1, self.n_s):
+        for k in far_first(self.n_s)[:-1]:
             for src, dst in self.pieces(k):
                 remote(src, dst, self.send.at[k], self.recv.at[k], {"seq": self.place(k)}).start()
         for src, dst in self.pieces(0):
@@ -409,7 +437,7 @@
         self.n_w, self.n_s, self.whole = n_w, n_s, whole
         self.x, self.out, self.send, self.recv, self.local = x, out, send, recv, local
         self.w, self.s = lax.axis_index("wide"), lax.axis_index("seq")
-        self.steps = [(a, b) for a in (range(n_w) if whole else (0,)) for b in range(n_s) if a or b]
+        self.steps = [(a, b) for b in far_first(n_s) for a in (range(n_w) if whole else (0,)) if a or b]
 
     def at(self, a, b):
         return lax.rem(self.w + a, self.n_w), lax.rem(self.s + b, self.n_s)
@@ -556,23 +584,22 @@
     )(x, *weights, gain)
 
 
-def back_kernel(n_s, plan, *refs):
-    slots, arrays, sems = refs[0], refs[1 : 1 + len(plan)], refs[1 + len(plan) :]
-    columns = Columns(n_s, plan, arrays, slots, True, *sems)
-    greet(seq_others(n_s))
-    columns.start()
-    columns.finish()
-
-
-def columns_back(slots, shapes, plan, n_s, cid):
+def unpack_kernel(n_s, plan, slots, *outs):
+    for out, pieces in zip(outs, plan):
+        for first, width, column in pieces:
+            for s in range(n_s):
+                out[:, first(s) : first(s) + width] = slots[s, :, column : column + width].astype(f32)
+
+
+def unpack(slots, width, plan):
+    n_s, rows, _ = slots.shape
     return pl.pallas_call(
-        functools.partial(back_kernel, n_s, plan),
-        out_shape=[jax.ShapeDtypeStruct(s, bf16) for s in shapes],
-        in_specs=[ANY],
-        out_specs=[ANY] * len(shapes),
-        scratch_shapes=columns_sems(n_s),
-        compiler_params=params(cid),
-        cost_estimate=cost(40),
+        functools.partial(unpack_kernel, n_s, plan),
+        out_shape=[jax.ShapeDtypeStruct((rows, width), f32)] * len(plan),
+        in_specs=[VM],
+        out_specs=[VM] * len(plan),
+        compiler_params=pltpu.CompilerParams(vmem_limit_bytes=40 * 2**20),
+        cost_estimate=cost(4),
     )(slots)
 
 
@@ -600,27 +627,25 @@
     )(x, given)
 
 
-def final_kernel(n_w, n_s, plan, slots, terms, q, k, v, all_terms, *sems):
-    columns = Columns(n_s, plan, (q, k, v), slots, True, *sems[:3])
-    share = Share(n_w, n_s, True, terms, all_terms, *sems[3:])
-    greet(share.others())
-    share.start()
-    columns.start()
-    share.finish()
-    columns.finish()
-
-
-def final_exchange(slots, terms, width, plan, n_w, n_s, cid):
-    mat = jax.ShapeDtypeStruct((slots.shape[1], width), bf16)
+def final_kernel(n_w, n_s, qkv, terms, qkv_own, all_terms, *sems):
+    shares = [Share(n_w, n_s, True, terms, all_terms, *sems[:3]), Share(n_w, n_s, False, qkv, qkv_own, *sems[3:])]
+    greet(shares[0].others())
+    for share in shares:
+        share.start()
+    for share in shares:
+        share.finish()
+
+
+def final_exchange(qkv, terms, n_w, n_s, cid):
     return pl.pallas_call(
-        functools.partial(final_kernel, n_w, n_s, plan),
-        out_shape=[mat, mat, mat, jax.ShapeDtypeStruct(terms.shape, terms.dtype)],
+        functools.partial(final_kernel, n_w, n_s),
+        out_shape=[jax.ShapeDtypeStruct(v.shape, v.dtype) for v in (qkv, terms)],
         in_specs=[ANY, VM],
-        out_specs=[ANY] * 3 + [VM],
-        scratch_shapes=columns_sems(n_s) + [DMA((n_w * n_s,)), DMA((n_w * n_s,)), DMA],
+        out_specs=[ANY, VM],
+        scratch_shapes=[DMA((n_w * n_s,)), DMA((n_w * n_s,)), DMA, DMA((n_s,)), DMA((n_s,)), DMA],
         compiler_params=params(cid),
         cost_estimate=cost(20),
-    )(slots, terms)
+    )(qkv, terms)
 
 
 def dot(a, b):
@@ -775,7 +800,7 @@
     halves = 2 * rows == HEAD_DIM and n_w == 2 * heads
 
     def head_of(s, i):
-        return s // 2 + n_s // 2 * (lax.rem(s, 2) * heads + i) if halves else s * heads + i
+        return s // 2 + n_s // 2 * (s % 2 * heads + i) if halves else s * heads + i
 
     def head_column(i):
         return lambda s: head_of(s, i) * HEAD_DIM
@@ -800,7 +825,7 @@
     x_all, gate_up, gains = second_exchange(after(flat, qkv), (gate_weight, up_weight), own_gain, feed_plan, 2 * half, n_w, n_s, 1)
     x_all = x_all.reshape(all_tokens, width)
     gate_up_all = wide_gather(gate_up.reshape(n_s * rows, 2 * half))
-    down_block = after(down_weight, gate_up)
+    down_block = down_weight
     if not own_blocks:
         down_block = lax.ppermute(down_block, ("wide", "seq"), moves)
     down_all = wide_gather(down_block)
@@ -846,17 +871,19 @@
         dot(active, down_all).astype(bf16), (hidden, cot, gains[3:4]), down_rows, [((tokens, width), bf16), vec_f32], n_s, 4, True
     )
     d_down_all = d_down_all.reshape(all_tokens, width)
-    down_part = t_dot(active, d_down_all).astype(bf16)
-    down_grad = wide_scatter(down_part)
-    d_active = dot_t(after(d_down_all, down_part), down_all)
+    d_active = dot_t(d_down_all, down_all)
     d_gate = (d_active * upward * sigma * (1.0 + gate_lin * (1.0 - sigma))).astype(bf16)
     d_up = (d_active * silu_gate).astype(bf16)
     d_gate_up = jnp.concatenate([d_gate, d_up], axis=1)
     mlp_part = t_dot(hidden_all, d_gate_up).astype(bf16)
     mlp_grad = wide_scatter(mlp_part)
-    d_mixed_all, d_hidden, attention_term = around(
-        dot_t(after(d_gate_up, mlp_part), gate_up_all).astype(bf16), (cot, mixed_n, mixed_inv, gains[2:3]), hidden_rows, [own_f32, vec_f32], n_s, 5, True
+    d_mixed_all, d_hidden, attention_term, down_part = around(
+        dot_t(after(d_gate_up, mlp_part), gate_up_all).astype(bf16), (cot, mixed_n, mixed_inv, gains[2:3]), hidden_rows, [own_f32, vec_f32],
+        n_s, 5, True, (active, d_down_all),
     )
+    mlp_grad, d_mixed_all, down_part = lax.optimization_barrier((mlp_grad, d_mixed_all, down_part))
+    down_grad = wide_scatter(down_part)
+    mlp_grad = lax.all_to_all(mlp_grad, "seq", 0, 0, tiled=True)
     d_mixed_all = d_mixed_all.reshape(all_tokens, width)
     out_part = t_dot(attended, d_mixed_all).astype(bf16)
     d_attended = dot_t(d_mixed_all, out_all).astype(bf16).reshape(shape4)
@@ -870,6 +897,7 @@
         mean_sums, out_part = sums_exchange(mean_sums, out_part.reshape(heads, 2, rows, width), True, n_w, n_s, 6)
     else:
         mean_sums = exchange(mean_sums, n_w, n_s, False, 6)
+    mean_sums, mlp_grad = lax.optimization_barrier((mean_sums, mlp_grad))
     means = jnp.sum(mean_sums, 0)[:2].T / width
     query_term = jnp.sum(d_q * q_n, 0)
     key_term = jnp.sum(d_k * k_n, 0)
@@ -877,16 +905,13 @@
     d_k_lin = (inv[:, 1:2] * (d_kg - k_n * means[:, 1:2])).astype(bf16)
     d_lin = jnp.concatenate([d_q_lin, d_k_lin, d_v], axis=1)
     qkv_part = t_dot(x_all, d_lin).astype(bf16)
-    mlp_grad, down_grad, qkv_part, out_part = lax.optimization_barrier((mlp_grad, down_grad, qkv_part, out_part))
+    down_grad, qkv_part = lax.optimization_barrier((down_grad, qkv_part))
     input_grad = last_sum(dot_t(after(d_lin, qkv_part), qkv_all).astype(bf16), d_hidden, n_s, 7).reshape(inputs.shape)
     qkv_grad = wide_scatter(qkv_part)
-    out_grad = wide_scatter(out_part.reshape(cols, width))
+    out_grad = wide_scatter(after(out_part, qkv_grad, input_grad).reshape(cols, width))
     if not halves:
         out_grad = lax.ppermute(out_grad, ("wide", "seq"), back_moves)
 
-    gate_grad, up_grad = columns_back(
-        after(mlp_grad, input_grad).reshape(n_s, rows, 2 * half), [(rows, feed)] * 2, feed_plan, n_s, 8
-    )
     def spread(term):
         full = jnp.zeros((width,), f32)
         for i in range(heads):
@@ -896,14 +921,14 @@
     terms = jnp.stack([spread(query_term), spread(key_term), attention_term[0], feed_term[0]])
     terms = jnp.swapaxes(terms.reshape(4, n_dev, rows), 0, 1)
     terms = jnp.pad(terms, ((0, 0), (0, 4), (0, 128 - rows)))
-    query_grad, key_grad, value_grad, all_terms = final_exchange(
-        after(qkv_grad, gate_grad).reshape(n_s, rows, 3 * cols), terms, width, qkv_plan, n_w, n_s, 9
-    )
+    qkv_grad, all_terms = final_exchange(qkv_grad.reshape(n_s, rows, 3 * cols), after(terms, input_grad), n_w, n_s, 8)
+    gate_grad, up_grad = unpack(mlp_grad.reshape(n_s, rows, 2 * half), feed, feed_plan)
+    query_grad, key_grad, value_grad = unpack(qkv_grad, width, qkv_plan)
     gain_grads = jnp.sum(all_terms, 0)[:4, :rows]
     if not own_blocks:
         down_grad = lax.ppermute(down_grad, ("wide", "seq"), back_moves)
-    return (layer_out.reshape(inputs.shape), input_grad, *(g.astype(f32) for g in (query_grad, key_grad, value_grad, out_grad)),
-            gain_grads[0], gain_grads[1], gain_grads[2], gate_grad.astype(f32), up_grad.astype(f32), down_grad.astype(f32), gain_grads[3])
+    return (layer_out.reshape(inputs.shape), input_grad, query_grad, key_grad, value_grad, out_grad.astype(f32),
+            gain_grads[0], gain_grads[1], gain_grads[2], gate_grad, up_grad, down_grad.astype(f32), gain_grads[3])
 
 
 def solution(mesh):

time: 656 us -> 627 us (0.956)
  Pallas kernels: 474 us -> 452 us
  matrix products: 93.8 us -> 85 us
  starting transfers between devices: 0.94 us -> 9.36 us
    pallas_call x2 -> x3, Pallas kernels: 74.6 us -> 29.2 us  [the longest x1 25.8 us: final_exchange(): pl.pallas_call(functools.partial(final_kernel, n_w, n_s), out_shape=[jax....]
    pallas_call x2, Pallas kernels: 32.1 us -> 52.6 us  [sums_exchange(): pl.pallas_call(functools.partial(sums_kernel, n_w, n_s, back), out_shape=...]
    convert_element_type x6 -> x1, other arithmetic: 12.5 us -> 1.78 us  [on_device(): out_grad.astype(f32)]
    all_to_all x0 -> x1, starting transfers between devices: none -> 8.68 us  [on_device(): mlp_grad = lax.all_to_all(mlp_grad, 'seq', 0, 0, tiled=True)]
    dot_general x4 -> x3, matrix products: 26.9 us -> 18.8 us  [t_dot(): lax.dot_general(a, b, (((0,), (0,)), ((), ())), preferred_element_type=f32)]
    unnamed x70 -> x76, local copies, waits for them, and re-layouts: 12.9 us -> 13.7 us
  transfers between devices with their start and end apart: 8 -> 9, of which waited for: 1 -> 1; matrix products, arithmetic and copies ran while one was open for 16% -> 13% of each run, Pallas kernels for 55% -> 59%
where the time goes in v4:
time: 627 us; the launch traced here: 618 us
  Pallas kernels  452 us (72%)
  matrix products  85 us (14%)
  other arithmetic  25.2 us (4%)
  local copies, waits for them, and re-layouts  16.9 us (3%)
  between operations  15 us (2%)
  waiting for transfers between devices  14.9 us (2%)
  starting transfers between devices  9.36 us (1%)
    pallas_call x3, Pallas kernels, around(): pl.pallas_call(functools.partial(around_kernel, n_s, chunks, rows_fn, len...  210 us
    pallas_call x1, Pallas kernels, second_exchange(): pl.pallas_call(functools.partial(second_kernel, n_w, n_s, chunks, plan),...  83.4 us
    pallas_call x2, Pallas kernels, sums_exchange(): pl.pallas_call(functools.partial(sums_kernel, n_w, n_s, back), out_shape=...  52.6 us
    pallas_call x1, Pallas kernels, last_sum(): pl.pallas_call(functools.partial(last_kernel, n_s, chunks), out_shape=jax...  40.9 us
    dot_general x4, matrix products, dot_t(): lax.dot_general(a, b, (((1,), (1,)), ((), ())), preferred_element_type=f32)  33.8 us
    dot_general x4, matrix products, dot(): return jnp.dot(a, b, preferred_element_type=f32)  32.4 us
    pallas_call x1, Pallas kernels, final_exchange(): pl.pallas_call(functools.partial(final_kernel, n_w, n_s), out_shape=[jax....  25.8 us
    pallas_call x1, Pallas kernels, first_exchange(): pl.pallas_call(functools.partial(first_kernel, n_s, plan), out_shape=jax....  21.4 us
  transfers between devices with their start and end apart: 9, of which 1 were waited for; matrix products, arithmetic and copies ran while one was open for 13% of the time, Pallas kernels for 59%

profile of v4, /device:TPU:9, one launch (start us, length us, event | category | flops | bytes accessed | tf_op | source)
XLA Modules:
  0.0 618.2 jit_solution(504658300954710255)
XLA Ops:
  7.2 21.4 %shard_map.237 = bf16[8,64,768]{2,1,0:T(8,128)(2,1)} custom-call(bf16[64,2048]{1,0:T(8,128)(2,1)} %qw.1, bf16[64,2048]{1,0:T(8,128)(2,1)} %kw.1, bf16[64,2048]{1,0:T(8,128)(2,1)} %vw.1), custom_call_target="tpu_custom_call" | custom-call | bytes 60000000 | tf_op jit(solution)/shard_map/pallas_call | solution.py:537
  29.5 1.3 fusion.17.gain
  30.8 83.4 %shard_map.238 = (bf16[8,128,2048]{2,1,0:T(8,128)(2,1)}, bf16[8,64,2048]{2,1,0:T(8,128)(2,1)}, f32[32,8,128]{2,1,0:T(8,128)}) custom-call(bf16[128,2048]{1,0:T(8,128)(2,1)} %bitcast.109, bf16[64,8192]{1,0:T(8,128)(2,1)} %gw.1, bf16[64,8192]{1,0:T(8,128)(2,1)} %uw.1, f32[8,128]{1,0:T(8,128)} %fusion.17.gain), custom_call_target="tpu_custom_call" | custom-call | bytes 240000000 | tf_op jit(solution)/shard_map/pallas_call | solution.py:572
  114.9 0.9 slice_bitcast_fusion
  116.6 1.0 fusion.3
  117.9 8.3 %fusion.23 = f32[1024,768]{1,0:T(8,128)} fusion(bf16[1024,2048]{1,0:T(8,128)(2,1)} %bitcast.154, bf16[2048,768]{1,0:T(8,128)(2,1)} %all-gather.5.cloned.1.call-done), kind=kOutput, calls=%fused_computation.78 | convolution fusion | flops 3221225472 | bytes 10485760 | tf_op jit(solution)/shard_map/dot_general | solution.py:652
  126.2 2.2 multiply_reduce_fusion.3
  129.1 16.7 %shard_map.239 = (f32[8,8,1024]{2,1,0:T(8,128)}, bf16[2,2,64,2048]{3,2,1,0:T(8,128)(2,1)}) custom-call(f32[8,1024]{1,0:T(8,128)} %maximum_maximum_fusion.x, bf16[4,64,2048]{2,1,0:T(8,128)(2,1)} %bitcast.133), custom_call_target="tpu_custom_call" | custom-call | bytes 30000000 | tf_op jit(solution)/shard_map/pallas_call | solution.py:619
  145.8 1.0 reduce_sum.83
  147.0 7.4 %shard_map.240 = (bf16[8,2,64,256]{3,2,1,0:T(8,128)(2,1)S(1)}, bf16[8,2,64,256]{3,2,1,0:T(8,128)(2,1)S(1)}, bf16[8,2,64,256]{3,2,1,0:T(8,128)(2,1)S(1)}, bf16[8,...) custom-call(f32[8,2,64,768]{3,2,1,0:T(8,128)} %bitcast.7.ql.kl.vl, f32[8,2,64,768]{3,2,1,0:T(8,128)} %bitcast.7.ql.kl.vl, ...), custom_call_target="tpu_custom_call" | custom-call | tf_op jit(solution)/shard_map/pallas_call | solution.py:734
  155.2 3.3 convolution_convert_fusion.2
  158.5 67.9 %shard_map.241 = (bf16[8,128,2048]{2,1,0:T(8,128)(2,1)}, f32[128,2048]{1,0:T(8,128)S(1)}, f32[128,2048]{1,0:T(8,128)S(1)}, f32[128,1]{1,0:T(8,128)S(1)}) custom-call(bf16[8,128,2048]{2,1,0:T(8,128)(2,1)} %bitcast.124, bf16[128,2048]{1,0:T(8,128)(2,1)S(1)} %bitcast.110, f32[1,2048]{1,0:T(1,128)S(1)} %slice.92.refs_2_.refs_4_), custom_call_target="tpu_custom_call" | custom-call | bytes 210000000 | tf_op jit(solution)/shard_map/pallas_call | solution.py:353
  226.5 1.0 copy-done.12
  227.4 1.0 copy-done.14
  228.4 12.5 %fusion.24 = f32[1024,2048]{1,0:T(8,128)S(1)} fusion(bf16[1024,2048]{1,0:T(8,128)(2,1)} %bitcast.158, bf16[2048,2048]{1,0:T(8,128)(2,1)} %all-gather.9.cloned.1.call-done), kind=kOutput, calls=%fused_computation.79 | convolution fusion | flops 8589934592 | bytes 20971520 | tf_op jit(solution)/shard_map/dot_general | solution.py:652
  240.9 3.2 copy-done.28
  244.1 1.4 multiply_convert_fusion.2.refs_5_
  245.6 13.5 %all-gather.11.cloned.1.call-done = bf16[1024,2048]{1,0:T(8,128)(2,1)} async-done(((bf16[256,2048]{1,0:T(8,128)(2,1)}), bf16[1024,2048]{1,0:T(8,128)(2,1)}) %all-gather.11.cloned.1.call-update) | async-done | bytes 4194320 | tf_op jit(solution)/shard_map/all_gather | solution.py:771
  259.1 8.4 %convolution_convert_fusion.4 = bf16[1024,2048]{1,0:T(8,128)(2,1)} fusion(bf16[1024,1024]{1,0:T(8,128)(2,1)S(1)} %multiply_convert_fusion.2.refs_5_, bf16[1024,2048]{1,0:T(8,128)(2,1)} %all-gather.11.cloned.1.call-done), kind=kOutput, calls=%fused_computation.10 | convolution fusion | flops 4297064448 | bytes 10485760 | tf_op jit(solution)/shard_map/dot_general | solution.py:652
  267.5 68.7 %shard_map.242 = (bf16[8,128,2048]{2,1,0:T(8,128)(2,1)}, bf16[128,2048]{1,0:T(8,128)(2,1)S(1)}, f32[1,2048]{1,0:T(1,128)S(1)}) custom-call(bf16[8,128,2048]{2,1,0:T(8,128)(2,1)} %bitcast.126, f32[128,2048]{1,0:T(8,128)S(1)} %copy-done.13, bf16[128,2048]{1,0:T(8,128)(2,1)S(1)} %bitcast.112, f32[1,2048]{1,0:T(1,128)S(1)} %slice.96.refs_3_), custom_call_target="tpu_custom_call" | custom-call | bytes 210000000 | tf_op jit(solution)/shard_map/pallas_call | solution.py:353
  336.2 9.5 %multiply_convert_fusion.1 = (bf16[1024,1024]{1,0:T(8,128)(2,1)S(1)}, bf16[1024,1024]{1,0:T(8,128)(2,1)S(1)}) fusion(f32[1024,2048]{1,0:T(8,128)S(1)} %copy-done.29, bf16[1024,2048]{1,0:T(8,128)(2,1)} %bitcast.127, bf16[1024,2048]{1,0:T(8,128)(2,1)} %all-gather.11.cloned.1.call-done), kind=kOutput, calls=%fused_computation.3 | convolution fusion | flops 4308598784 | bytes 20971520 | tf_op jit(solution)/shard_map/dot_general | solution.py:656
  345.7 1.3 copy-done.31
  347.7 11.6 %convolution_convert_fusion = bf16[2048,2048]{1,0:T(8,128)(2,1)} fusion(bf16[1024,2048]{1,0:T(8,128)(2,1)S(1)} %bitcast.159, bf16[1024,1024]{1,0:T(8,128)(2,1)S(1)} %get-tuple-element.142, bf16[1024,1024]{1,0:T(8,128)(2,1)S(1)} %get-tuple-element.141), kind=kOutput, calls=%fused_computation | convolution fusion | flops 8602517504 | bytes 16777216 | tf_op jit(solution)/shard_map/dot_general | solution.py:660
  359.8 2.6 pad_maximum_fusion
  362.4 12.8 %convolution_convert_fusion.1 = bf16[1024,2048]{1,0:T(8,128)(2,1)} fusion(bf16[1024,2048]{1,0:T(8,128)(2,1)S(1)} %pad_maximum_fusion, bf16[2048,2048]{1,0:T(8,128)(2,1)} %all-gather.9.cloned.1.call-done), kind=kOutput, calls=%fused_computation.7 | convolution fusion | flops 8592031744 | bytes 16777216 | tf_op jit(solution)/shard_map/dot_general | solution.py:656
  375.2 73.1 %shard_map.243 = (bf16[8,128,2048]{2,1,0:T(8,128)(2,1)}, f32[128,2048]{1,0:T(8,128)S(1)}, f32[1,2048]{1,0:T(1,128)S(1)}, bf16[1024,2048]{1,0:T(8,128)(2,1)}) custom-call(bf16[8,128,2048]{2,1,0:T(8,128)(2,1)} %bitcast.129, bf16[128,2048]{1,0:T(8,128)(2,1)S(1)} %bitcast.113, f32[128,2048]{1,0:T(8,128)S(1)} %copy-done.15, ...), custom_call_target="tpu_custom_call" | custom-call | bytes 210000000 | tf_op jit(solution)/shard_map/pallas_call | solution.py:353
  448.3 1.0 copy-done.10
  449.3 8.7 %all-to-all-start = ((bf16[8,64,2048]{2,1,0:T(8,128)(2,1)}), bf16[8,64,2048]{2,1,0:T(8,128)(2,1)S(1)}, u32[]{:S(2)}, u32[]{:S(2)}) async-start(bf16[8,64,2048]{2,1,0:T(8,128)(2,1)} %bitcast.132), calls=%async_computation.1 | async-start | bytes 4194304 | tf_op jit(solution)/shard_map/all_to_all | solution.py:886
  458.0 4.6 convolution_convert_fusion.7
  462.7 7.1 %shard_map.244 = (f32[8,2,64,256]{3,2,1,0:T(8,128)S(1)}, f32[8,2,64,256]{3,2,1,0:T(8,128)S(1)}, bf16[8,2,64,256]{3,2,1,0:T(8,128)(2,1)S(1)}) custom-call(bf16[8,2,64,256]{3,2,1,0:T(8,128)(2,1)S(1)} %copy-done.18, bf16[8,2,64,256]{3,2,1,0:T(8,128)(2,1)S(1)} %copy-done.20, bf16[8,2,64,256]{3,2,1,0:T(8,128)(2,1)S(1)} %copy-done.22, ...), custom_call_target="tpu_custom_call" | custom-call | tf_op jit(solution)/shard_map/pallas_call | solution.py:748
  469.9 3.5 fusion.2
  474.0 2.2 convolution_convert_fusion.6
  476.3 35.9 %shard_map.245 = (f32[8,8,1024]{2,1,0:T(8,128)}, bf16[4,64,2048]{2,1,0:T(8,128)(2,1)}) custom-call(f32[8,1024]{1,0:T(8,128)} %maximum_maximum_fusion.1.x, bf16[2,2,64,2048]{3,2,1,0:T(8,128)(2,1)} %bitcast.135), custom_call_target="tpu_custom_call" | custom-call | bytes 30000000 | tf_op jit(solution)/shard_map/pallas_call | solution.py:619
  512.2 1.0 reduce_sum.86
  513.2 2.8 multiply_convert_fusion.4
  516.8 5.0 convolution_convert_fusion.5
  521.8 1.1 pad_maximum_fusion.1
  523.0 7.0 %convolution_convert_fusion.3 = bf16[1024,2048]{1,0:T(8,128)(2,1)} fusion(bf16[1024,768]{1,0:T(8,128)(2,1)S(1)} %pad_maximum_fusion.1, bf16[2048,768]{1,0:T(8,128)(2,1)} %all-gather.5.cloned.1.call-done), kind=kOutput, calls=%fused_computation.9 | convolution fusion | flops 3223322624 | bytes 8912896 | tf_op jit(solution)/shard_map/dot_general | solution.py:656
  530.0 40.9 %shard_map.246 = f32[128,2048]{1,0:T(8,128)S(1)} custom-call(bf16[8,128,2048]{2,1,0:T(8,128)(2,1)} %bitcast.125, f32[128,2048]{1,0:T(8,128)S(1)} %copy-done.11), custom_call_target="tpu_custom_call" | custom-call | bytes 120000000 | tf_op jit(solution)/shard_map/pallas_call | solution.py:380
  570.9 1.0 copy-done.2
  572.9 2.2 shard_map.249
  575.1 2.9 convert_element_type.78
  578.0 25.8 %shard_map.247 = (bf16[8,64,768]{2,1,0:T(8,128)(2,1)}, f32[32,8,128]{2,1,0:T(8,128)}) custom-call(bf16[8,64,768]{2,1,0:T(8,128)(2,1)} %bitcast.138, f32[32,8,128]{2,1,0:T(8,128)} %pad.12.terms), custom_call_target="tpu_custom_call" | custom-call | bytes 60000000 | tf_op jit(solution)/shard_map/pallas_call | solution.py:640
  603.8 1.1 copy-done.16
  604.9 1.2 shard_map.248
  606.1 0.9 reduce_sum.89
  607.6 1.8 convert_element_type.77
  610.2 1.0 copy.55
  (126 shorter events, 9.3 us)
Async XLA Ops:
  7.2 108.9 %copy-start.27 = (s32[2,1,512]{2,1,0:T(1,128)S(1)}, s32[2,1,512]{2,1,0:T(1,128)}, u32[]{:S(2)}) copy-start(s32[2,1,512]{2,1,0:T(1,128)} %doc_k.3) | copy-start | bytes 12292
  7.2 110.7 %all-gather.5.cloned.1.call-start = ((), (), s32[]{:S(2)}) async-start(), calls=%async_computation.5 | async-start | bytes 3932160 | tf_op jit(solution)/shard_map/all_gather | solution.py:771
  28.7 100.4 %all-gather.7.cloned.1.call-start = ((), (), s32[]{:S(2)}) async-start(), calls=%async_computation.6 | async-start | bytes 1310720 | tf_op jit(solution)/shard_map/all_gather | solution.py:771
  29.4 199.0 %all-gather.9.cloned.1.call-start = ((), (), s32[]{:S(2)}) async-start(), calls=%async_computation.7 | async-start | bytes 10485760 | tf_op jit(solution)/shard_map/all_gather | solution.py:771
  114.2 144.9 %all-gather.11.cloned.1.call-start = ((), (), s32[]{:S(2)}) async-start(), calls=%async_computation.8 | async-start | bytes 5242880 | tf_op jit(solution)/shard_map/all_gather | solution.py:771
  114.8 334.5 %reduce-scatter.5.cloned.1.call-start = ((), (), s32[]{:S(2)}) async-start(), calls=%async_computation.9 | async-start | bytes 10485760 | tf_op jit(solution)/shard_map/reduce_scatter | solution.py:775
  147.0 8.2 %copy-start.33 = (bf16[2,2,64,2048]{3,2,1,0:T(8,128)(2,1)S(1)}, bf16[2,2,64,2048]{3,2,1,0:T(8,128)(2,1)}, u32[]{:S(2)}) copy-start(bf16[2,2,64,2048]{3,2,1,0:T(8,128)(2,1)} %get-tuple-element.65) | copy-start | bytes 3145732
  154.4 0.8 copy-start.7
  154.4 4.0 copy-start.19
  154.5 4.0 copy-start.21
  154.5 72.0 %copy-start.9 = (f32[2,8,2,64,1]{4,3,2,1,0:T(8,128)}, f32[2,8,2,64,1]{4,3,2,1,0:T(8,128)S(1)}, u32[]{:S(2)}) copy-start(f32[2,8,2,64,1]{4,3,2,1,0:T(8,128)S(1)} %get-tuple-element.73.lse) | copy-start | bytes 24580
  154.5 72.0 %copy-start.17 = (bf16[8,2,64,256]{3,2,1,0:T(8,128)(2,1)}, bf16[8,2,64,256]{3,2,1,0:T(8,128)(2,1)S(1)}, u32[]{:S(2)}) copy-start(bf16[8,2,64,256]{3,2,1,0:T(8,128)(2,1)S(1)} %get-tuple-element.70.q) | copy-start | bytes 1572868
  154.5 4.0 copy-start.4
  226.4 1.0 copy-start.12
  227.4 1.0 copy-start.14
  240.9 3.3 copy-start.28
  259.1 8.4 %copy-start.5 = (bf16[2,1,64,2048]{3,2,1,0:T(8,128)(2,1)S(1)}, bf16[2,1,64,2048]{3,2,1,0:T(8,128)(2,1)}, u32[]{:S(2)}) copy-start(bf16[2,1,64,2048]{3,2,1,0:T(8,128)(2,1)} %param.16) | copy-start | bytes 1572868
  259.1 8.4 %copy-start.13 = (f32[128,2048]{1,0:T(8,128)S(1)}, f32[128,2048]{1,0:T(8,128)}, u32[]{:S(2)}) copy-start(f32[128,2048]{1,0:T(8,128)} %copy-done.12) | copy-start | bytes 3145732
  259.1 77.1 %copy-start.29 = (f32[1024,2048]{1,0:T(8,128)S(1)}, f32[1024,2048]{1,0:T(8,128)}, u32[]{:S(2)}) copy-start(f32[1024,2048]{1,0:T(8,128)} %copy-done.28) | copy-start | bytes 25165828
  336.2 9.5 %copy-start.23 = (bf16[128,2048]{1,0:T(8,128)(2,1)}, bf16[128,2048]{1,0:T(8,128)(2,1)S(1)}, u32[]{:S(2)}) copy-start(bf16[128,2048]{1,0:T(8,128)(2,1)S(1)} %get-tuple-element.69) | copy-start | bytes 1572868
  336.2 11.5 %copy-start.36 = (bf16[8,128,2048]{2,1,0:T(8,128)(2,1)S(1)}, bf16[8,128,2048]{2,1,0:T(8,128)(2,1)}, u32[]{:S(2)}) copy-start(bf16[8,128,2048]{2,1,0:T(8,128)(2,1)} %get-tuple-element.66) | copy-start | bytes 12582916
  345.7 1.3 copy-start.31
  345.7 2.0 copy-start.32
  359.3 162.5 %reduce-scatter.7.cloned.1.call-start = ((), (), s32[]{:S(2)}) async-start(), calls=%async_computation.10 | async-start | bytes 5242880 | tf_op jit(solution)/shard_map/reduce_scatter | solution.py:775
  362.4 12.8 %copy-start.6 = (bf16[2,1,64,2048]{3,2,1,0:T(8,128)(2,1)S(1)}, bf16[2,1,64,2048]{3,2,1,0:T(8,128)(2,1)}, u32[]{:S(2)}) copy-start(bf16[2,1,64,2048]{3,2,1,0:T(8,128)(2,1)} %param.16) | copy-start | bytes 1572868
  362.4 12.8 %copy-start.15 = (f32[128,2048]{1,0:T(8,128)S(1)}, f32[128,2048]{1,0:T(8,128)}, u32[]{:S(2)}) copy-start(f32[128,2048]{1,0:T(8,128)} %copy-done.14) | copy-start | bytes 3145732
  448.3 1.0 copy-start.10
  449.3 62.9 %all-to-all-start = ((bf16[8,64,2048]{2,1,0:T(8,128)(2,1)}), bf16[8,64,2048]{2,1,0:T(8,128)(2,1)S(1)}, u32[]{:S(2)}, u32[]{:S(2)}) async-start(bf16[8,64,2048]{2,1,0:T(8,128)(2,1)} %bitcast.132), calls=%async_computation.1 | async-start | bytes 4194304 | tf_op jit(solution)/shard_map/all_to_all | solution.py:886
  458.0 113.9 %reduce-scatter.9.cloned.1.call-start = ((), (), s32[]{:S(2)}) async-start(), calls=%async_computation.11 | async-start | bytes 3932160 | tf_op jit(solution)/shard_map/reduce_scatter | solution.py:775
  458.0 4.6 copy-start.18
  458.0 4.6 copy-start.20
  458.0 4.6 copy-start.22
  462.6 11.4 %copy-start.8 = (bf16[8,2,64,256]{3,2,1,0:T(8,128)(2,1)S(1)}, bf16[8,2,64,256]{3,2,1,0:T(8,128)(2,1)}, u32[]{:S(2)}) copy-start(bf16[8,2,64,256]{3,2,1,0:T(8,128)(2,1)} %copy-done.7) | copy-start | bytes 1572868
  462.7 11.4 %copy-start.35 = (bf16[8,128,2048]{2,1,0:T(8,128)(2,1)S(1)}, bf16[8,128,2048]{2,1,0:T(8,128)(2,1)}, u32[]{:S(2)}) copy-start(bf16[8,128,2048]{2,1,0:T(8,128)(2,1)} %get-tuple-element.80) | copy-start | bytes 12582916
  469.8 6.5 %copy-start = (f32[8,2,64,256]{3,2,1,0:T(8,128)}, f32[8,2,64,256]{3,2,1,0:T(8,128)S(1)}, u32[]{:S(2)}) copy-start(f32[8,2,64,256]{3,2,1,0:T(8,128)S(1)} %get-tuple-element.81) | copy-start | bytes 3145732
  469.8 6.5 %copy-start.1 = (f32[8,2,64,256]{3,2,1,0:T(8,128)}, f32[8,2,64,256]{3,2,1,0:T(8,128)S(1)}, u32[]{:S(2)}) copy-start(f32[8,2,64,256]{3,2,1,0:T(8,128)S(1)} %get-tuple-element.82) | copy-start | bytes 3145732
  469.8 6.5 %copy-start.25 = (bf16[8,2,64,256]{3,2,1,0:T(8,128)(2,1)}, bf16[8,2,64,256]{3,2,1,0:T(8,128)(2,1)S(1)}, u32[]{:S(2)}) copy-start(bf16[8,2,64,256]{3,2,1,0:T(8,128)(2,1)S(1)} %get-tuple-element.86) | copy-start | bytes 1572868
  476.3 40.5 %copy-start.26 = (bf16[8,2,64,256]{3,2,1,0:T(8,128)(2,1)S(1)}, bf16[8,2,64,256]{3,2,1,0:T(8,128)(2,1)}, u32[]{:S(2)}) copy-start(bf16[8,2,64,256]{3,2,1,0:T(8,128)(2,1)} %copy-done.25) | copy-start | bytes 1572868
  513.2 3.6 copy-start.34
  516.0 0.8 copy-start.30
  521.8 85.8 %reduce-scatter.11.cloned.1.call-start = ((), (), s32[]{:S(2)}) async-start(), calls=%async_computation.12 | async-start | bytes 1310720 | tf_op jit(solution)/shard_map/reduce_scatter | solution.py:775
  523.0 7.0 %copy-start.11 = (f32[128,2048]{1,0:T(8,128)S(1)}, f32[128,2048]{1,0:T(8,128)}, u32[]{:S(2)}) copy-start(f32[128,2048]{1,0:T(8,128)} %copy-done.10) | copy-start | bytes 3145732
  570.9 1.0 copy-start.2
  572.0 37.4 %copy-start.24 = (bf16[128,2048]{1,0:T(8,128)(2,1)S(1)}, bf16[128,2048]{1,0:T(8,128)(2,1)}, u32[]{:S(2)}) copy-start(bf16[128,2048]{1,0:T(8,128)(2,1)} %copy-done.23) | copy-start | bytes 1572868
  575.1 35.1 %copy-start.3 = (f32[128,2048]{1,0:T(8,128)S(1)}, f32[128,2048]{1,0:T(8,128)}, u32[]{:S(2)}) copy-start(f32[128,2048]{1,0:T(8,128)} %copy-done.2) | copy-start | bytes 3145732
  603.8 1.1 copy-start.16
Sparse Core Ops, SparseCore 0:
  28.8 44.9 all-gather.4
  75.6 26.4 all-gather.6
  114.4 90.2 all-gather.8
  206.4 52.6 all-gather.10
  359.4 88.5 reduce-scatter.4
  451.2 54.1 reduce-scatter.6
  521.9 41.8 reduce-scatter.8
  572.0 26.7 reduce-scatter.10

commit v5 on v4

--- a/solution.py
+++ b/solution.py
@@ -361,31 +361,35 @@
     )(terms.reshape(n_s, rows, width), *extra, *pair)
 
 
-def last_kernel(n_s, chunks, part, d_hidden, out, from_mate, run, *sems):
+def last_kernel(n_w, n_s, chunks, part, d_hidden, terms, out, all_terms, from_mate, run, *sems):
     line = Line(n_s)
-    scatter = Scatter(line, part, from_mate, run, chunks, *sems)
-    greet(line.neighbours())
+    scatter = Scatter(line, part, from_mate, run, chunks, *sems[:4])
+    share = Share(n_w, n_s, True, terms, all_terms, *sems[4:])
+    greet(share.others())
     for k in range(chunks):
         scatter.start(k)
 
     def use(k, total):
         out[scatter.span(k)] = d_hidden[scatter.span(k)] + total
 
+    share.start()
     run_slots(scatter, use)
     scatter.finish()
-
-
-def last_sum(terms, d_hidden, n_s, cid, chunks=CHUNKS):
-    rows, width = terms.shape[0] // n_s, terms.shape[1]
-    return pl.pallas_call(
-        functools.partial(last_kernel, n_s, chunks),
-        out_shape=jax.ShapeDtypeStruct((rows, width), f32),
-        in_specs=[VM, VM],
-        out_specs=VM,
-        scratch_shapes=scatter_scratch(n_s, rows, width, chunks),
+    share.finish()
+
+
+def last_sum(part, d_hidden, terms, n_w, n_s, cid, chunks=CHUNKS):
+    rows, width = part.shape[0] // n_s, part.shape[1]
+    count = n_w * n_s
+    return pl.pallas_call(
+        functools.partial(last_kernel, n_w, n_s, chunks),
+        out_shape=[jax.ShapeDtypeStruct((rows, width), f32), jax.ShapeDtypeStruct(terms.shape, terms.dtype)],
+        in_specs=[VM] * 3,
+        out_specs=[VM] * 2,
+        scratch_shapes=scatter_scratch(n_s, rows, width, chunks) + [DMA((count,)), DMA((count,)), DMA],
         compiler_params=params(cid, 48),
         cost_estimate=cost(40),
-    )(terms.reshape(n_s, rows, width), d_hidden)
+    )(part.reshape(n_s, rows, width), d_hidden, terms)
 
 
 class Columns:
@@ -495,30 +499,22 @@
 
 
 class Halves:
-    def __init__(self, n_w, natural, heads, back, send, recv, local):
+    def __init__(self, n_w, natural, heads, send, recv, local):
         s = lax.axis_index("seq")
         c = lax.rem(s, 2)
-        self.back, self.count = back, n_w // 2
-        self.send, self.recv, self.local = send, recv, local
         mate = {"seq": s + 1 - 2 * c}
-        self.away, self.stay = [], []
-        for i in range(self.count):
-            mine, his = c * self.count + i, (1 - c) * self.count + i
-            if back:
-                pair = heads.at[i, 1 - c], natural.at[mine]
-                own = heads.at[i, c], natural.at[mine]
-            else:
-                pair = natural.at[his], heads.at[i, c]
-                own = natural.at[mine], heads.at[i, c]
-            self.away.append(remote(*pair, send.at[i], recv.at[i], mate))
-            self.stay.append(pltpu.make_async_copy(*own, local.at[i]))
+        self.copies = []
+        for i in range(n_w // 2):
+            there = natural.at[c * (n_w // 2) + i]
+            self.copies.append(remote(heads.at[i, 1 - c], there, send.at[i], recv.at[i], mate))
+            self.copies.append(pltpu.make_async_copy(heads.at[i, c], there, local.at[i]))
 
     def start(self):
-        for copy in self.away + self.stay:
+        for copy in self.copies:
             copy.start()
 
     def finish(self):
-        for copy in self.away + self.stay:
+        for copy in self.copies:
             copy.wait()
 
 
@@ -545,43 +541,103 @@
     )(*weights)
 
 
-def second_kernel(n_w, n_s, chunks, plan, x, gw, uw, gain, x_all, slots, gains, own_sem, *sems):
+class Heads:
+    def __init__(self, n_w, block, heads, send, recv, local):
+        w, s = lax.axis_index("wide"), lax.axis_index("seq")
+        half = n_w // 2
+        c = lax.rem(s, 2)
+        core = w // half
+        self.lane = core == c
+        dst = heads.at[lax.rem(w, half), c]
+        self.sends = []
+        for k in range(n_w):
+            device = {"wide": lax.rem(w + k, n_w), "seq": s - c + core}
+            self.sends.append(remote(block, dst, send.at[k], recv.at[lax.rem(w, half), c], device))
+        self.stay = pltpu.make_async_copy(block, dst, local)
+        self.arrivals = []
+        for i in range(half):
+            for there in range(2):
+                own = self.lane & (lax.rem(w, half) == i) & (c == there)
+                ref = heads.at[i, there]
+                self.arrivals.append((jnp.logical_not(own), remote(ref, ref, send.at[0], recv.at[i, there], {"seq": s + 1 - 2 * c})))
+
+    def start(self):
+        for copy in self.sends[1:]:
+            copy.start()
+
+        @pl.when(self.lane)
+        def _():
+            self.stay.start()
+
+        @pl.when(jnp.logical_not(self.lane))
+        def _():
+            self.sends[0].start()
+
+    def finish(self):
+        for come, copy in self.arrivals:
+
+            @pl.when(come)
+            def _():
+                copy.wait_recv()
+
+        for copy in self.sends[1:]:
+            copy.wait_send()
+
+        @pl.when(self.lane)
+        def _():
+            self.stay.wait()
+
+        @pl.when(jnp.logical_not(self.lane))
+        def _():
+            self.sends[0].wait_send()
+
+
+def second_kernel(n_w, n_s, chunks, plan, heads, x, gw, uw, gain, *refs):
+    if heads:
+        out_block, x_all, slots, gains, out_heads, own_sem, *sems = refs
+    else:
+        x_all, slots, gains, own_sem, *sems = refs
     line = Line(n_s)
     gather = Gather(line, x, x_all, chunks, *sems[:4])
-    columns = Columns(n_s, plan, (gw, uw), slots, False, *sems[4:7])
-    share = Share(n_w, n_s, True, gain, gains, *sems[7:])
-    greet(share.others())
+    others = [Share(n_w, n_s, True, gain, gains, *sems[4:7])]
+    if heads:
+        others.append(Heads(n_w, out_block, out_heads, *sems[7:10]))
+    others.append(Columns(n_s, plan, (gw, uw), slots, False, *sems[-3:]))
+    greet(others[0].others())
     own = pltpu.make_async_copy(x, x_all.at[line.s], own_sem)
     for k in range(chunks):
         gather.start(k)
     own.start()
-    share.start()
-    columns.start()
+    for other in others:
+        other.start()
     for d in range(1, line.nz):
         for k in range(chunks):
             gather.pass_on(d, k)
     gather.finish()
     own.wait()
-    share.finish()
-    columns.finish()
-
-
-def second_exchange(x, weights, gain, plan, cols, n_w, n_s, cid, chunks=2):
+    for other in others:
+        other.finish()
+
+
+def second_exchange(x, weights, gain, out_block, plan, cols, n_w, n_s, cid, chunks=2):
     rows, width = x.shape
     count = n_w * n_s
-    return pl.pallas_call(
-        functools.partial(second_kernel, n_w, n_s, chunks, plan),
-        out_shape=[
-            jax.ShapeDtypeStruct((n_s, rows, width), bf16),
-            jax.ShapeDtypeStruct((n_s, weights[0].shape[0], cols), bf16),
-            jax.ShapeDtypeStruct((count, *gain.shape), gain.dtype),
-        ],
-        in_specs=[ANY] * 3 + [VM],
-        out_specs=[ANY, ANY, VM],
-        scratch_shapes=[DMA] + line_sems(n_s // 2, chunks) + columns_sems(n_s) + [DMA((count,)), DMA((count,)), DMA],
+    shapes = [((n_s, rows, width), bf16), ((n_s, weights[0].shape[0], cols), bf16), ((count, *gain.shape), gain.dtype)]
+    sems = [DMA] + line_sems(n_s // 2, chunks) + [DMA((count,)), DMA((count,)), DMA]
+    extra = []
+    if out_block is not None:
+        extra = [out_block]
+        shapes.append(((n_w // 2, 2, *out_block.shape), bf16))
+        sems += [DMA((n_w,)), DMA((n_w // 2, 2)), DMA]
+    return pl.pallas_call(
+        functools.partial(second_kernel, n_w, n_s, chunks, plan, bool(extra)),
+        out_shape=[jax.ShapeDtypeStruct(*o) for o in shapes],
+        in_specs=[ANY] * 3 + [VM] + [ANY] * len(extra),
+        out_specs=[ANY, ANY, VM] + [ANY] * len(extra),
+        scratch_shapes=sems + columns_sems(n_s),
         compiler_params=params(cid),
         cost_estimate=cost(80),
-    )(x, *weights, gain)
+    )(x, *weights, gain, *extra)
 
 
 def unpack_kernel(n_s, plan, slots, *outs):
@@ -603,9 +659,9 @@
     )(slots)
 
 
-def sums_kernel(n_w, n_s, back, x, given, all_x, made, *sems):
+def sums_kernel(n_w, n_s, x, heads, all_x, natural, *sems):
     share = Share(n_w, n_s, False, x, all_x, *sems[:3])
-    halves = Halves(n_w, *((made, given) if back else (given, made)), back, *sems[3:])
+    halves = Halves(n_w, natural, heads, *sems[3:])
     greet(share.others())
     share.start()
     halves.start()
@@ -613,39 +669,125 @@
     halves.finish()
 
 
-def sums_exchange(x, given, back, n_w, n_s, cid):
-    rows, width = given.shape[-2:]
-    made = (n_w, rows, width) if back else (n_w // 2, 2, rows, width)
-    return pl.pallas_call(
-        functools.partial(sums_kernel, n_w, n_s, back),
-        out_shape=[jax.ShapeDtypeStruct((n_s, *x.shape), x.dtype), jax.ShapeDtypeStruct(made, bf16)],
+def sums_exchange(x, heads, n_w, n_s, cid):
+    return pl.pallas_call(
+        functools.partial(sums_kernel, n_w, n_s),
+        out_shape=[jax.ShapeDtypeStruct((n_s, *x.shape), x.dtype), jax.ShapeDtypeStruct((n_w, *heads.shape[2:]), bf16)],
         in_specs=[VM, VM],
         out_specs=[VM, VM],
         scratch_shapes=[DMA((n_s,)), DMA((n_s,)), DMA] + halves_sems(n_w),
         compiler_params=params(cid),
         cost_estimate=cost(10),
-    )(x, given)
-
-
-def final_kernel(n_w, n_s, qkv, terms, qkv_own, all_terms, *sems):
-    shares = [Share(n_w, n_s, True, terms, all_terms, *sems[:3]), Share(n_w, n_s, False, qkv, qkv_own, *sems[3:])]
-    greet(shares[0].others())
-    for share in shares:
-        share.start()
-    for share in shares:
-        share.finish()
-
-
-def final_exchange(qkv, terms, n_w, n_s, cid):
+    )(x, heads)
+
+
+def final_kernel(n_w, n_s, qkv, qkv_own, *sems):
+    share = Share(n_w, n_s, False, qkv, qkv_own, *sems)
+    greet(seq_others(n_s))
+    share.start()
+    share.finish()
+
+
+def final_exchange(qkv, n_w, n_s, cid):
     return pl.pallas_call(
         functools.partial(final_kernel, n_w, n_s),
-        out_shape=[jax.ShapeDtypeStruct(v.shape, v.dtype) for v in (qkv, terms)],
-        in_specs=[ANY, VM],
-        out_specs=[ANY, VM],
-        scratch_shapes=[DMA((n_w * n_s,)), DMA((n_w * n_s,)), DMA, DMA((n_s,)), DMA((n_s,)), DMA],
+        out_shape=jax.ShapeDtypeStruct(qkv.shape, qkv.dtype),
+        in_specs=[ANY],
+        out_specs=ANY,
+        scratch_shapes=[DMA((n_s,)), DMA((n_s,)), DMA],
         compiler_params=params(cid),
         cost_estimate=cost(20),
-    )(qkv, terms)
+    )(qkv)
+
+
+def feed_kernel(hidden, gate_w, up_w, active, slope, swish):
+    rows = hidden.shape[0] // 4
+    for i in range(4):
+        rs = pl.ds(i * rows, rows)
+        gate, up = dot(hidden[rs], gate_w[...]), dot(hidden[rs], up_w[...])
+        sigma = jax.nn.sigmoid(gate)
+        silu = gate * sigma
+        active[rs] = (silu * up).astype(bf16)
+        slope[rs] = (up * sigma * (1.0 + gate * (1.0 - sigma))).astype(bf16)
+        swish[rs] = silu.astype(bf16)
+
+
+def feed_forward(hidden, weights, tile=256):
+    tokens, width = hidden.shape
+    half = weights.shape[1] // 2
+    steps = half // tile
+    out = pl.BlockSpec((tokens, tile), lambda j: (0, j))
+    return pl.pallas_call(
+        feed_kernel,
+        grid=(steps,),
+        out_shape=[jax.ShapeDtypeStruct((tokens, half), bf16)] * 3,
+        in_specs=[
+            pl.BlockSpec((tokens, width), lambda j: (0, 0)),
+            pl.BlockSpec((width, tile), lambda j: (0, j)),
+            pl.BlockSpec((width, tile), lambda j: (0, j + steps)),
+        ],
+        out_specs=[out] * 3,
+        compiler_params=pltpu.CompilerParams(vmem_limit_bytes=48 * 2**20),
+        cost_estimate=pl.CostEstimate(flops=4 * tokens * width * half, transcendentals=0, bytes_accessed=2 * (tokens * width + 2 * width * half)),
+    )(hidden, weights, weights)
+
+
+def feed_back_kernel(d_down, down_w, slope, swish, out):
+    tile = down_w.shape[0]
+    half = out.shape[1] // 2
+    d_active = dot_t(d_down[...], down_w[...])
+    at = pl.multiple_of(pl.program_id(0) * tile, tile)
+    out[:, pl.ds(at, tile)] = (d_active * slope[...].astype(f32)).astype(bf16)
+    out[:, pl.ds(pl.multiple_of(at + half, tile), tile)] = (d_active * swish[...].astype(f32)).astype(bf16)
+
+
+def feed_back(d_down, down_w, slope, swish, tile=256):
+    tokens, width = d_down.shape
+    half = down_w.shape[0]
+    cols = pl.BlockSpec((tokens, tile), lambda j: (0, j))
+    return pl.pallas_call(
+        feed_back_kernel,
+        grid=(half // tile,),
+        out_shape=jax.ShapeDtypeStruct((tokens, 2 * half), bf16),
+        in_specs=[pl.BlockSpec((tokens, width), lambda j: (0, 0)), pl.BlockSpec((tile, width), lambda j: (j, 0)), cols, cols],
+        out_specs=pl.BlockSpec((tokens, 2 * half), lambda j: (0, 0)),
+        compiler_params=pltpu.CompilerParams(vmem_limit_bytes=48 * 2**20),
+        cost_estimate=pl.CostEstimate(flops=2 * tokens * width * half, transcendentals=0, bytes_accessed=2 * (tokens * width + width * half)),
+    )(d_down, down_w, slope, swish)
+
+
+def rows_kernel(a, b, out):
+    out[...] = lax.dot_general(a[...], b[...], (((1,), (1,)), ((), ())), preferred_element_type=f32).astype(bf16)
+
+
+def columns_product(a, b, tile=512):
+    (m, k), n = a.shape, b.shape[0]
+    return pl.pallas_call(
+        rows_kernel,
+        grid=(n // tile,),
+        out_shape=jax.ShapeDtypeStruct((m, n), bf16),
+        in_specs=[pl.BlockSpec((m, k), lambda j: (0, 0)), pl.BlockSpec((tile, k), lambda j: (j, 0))],
+        out_specs=pl.BlockSpec((m, tile), lambda j: (0, j)),
+        compiler_params=pltpu.CompilerParams(vmem_limit_bytes=48 * 2**20),
+        cost_estimate=pl.CostEstimate(flops=2 * m * n * k, transcendentals=0, bytes_accessed=2 * (m * k + k * n + m * n)),
+    )(a, b)
+
+
+def terms_kernel(a, b, out):
+    out[...] = lax.dot_general(a[...], b[...], (((0,), (0,)), ((), ())), preferred_element_type=f32).astype(bf16)
+
+
+def weight_product(a, b, tile=512):
+    (k, m), n = a.shape, b.shape[1]
+    return pl.pallas_call(
+        terms_kernel,
+        grid=(m // tile,),
+        out_shape=jax.ShapeDtypeStruct((m, n), bf16),
+        in_specs=[pl.BlockSpec((k, tile), lambda i: (0, i)), pl.BlockSpec((k, n), lambda i: (0, 0))],
+        out_specs=pl.BlockSpec((tile, n), lambda i: (i, 0)),
+        compiler_params=pltpu.CompilerParams(vmem_limit_bytes=48 * 2**20),
+        cost_estimate=pl.CostEstimate(flops=2 * m * n * k, transcendentals=0, bytes_accessed=2 * (m * k + k * n + m * n)),
+    )(a, b)
 
 
 def dot(a, b):
@@ -818,11 +960,13 @@
     own_gain = jnp.pad(own_gain, ((0, 4), (0, 128 - rows)))
     qkv = first_exchange((query_weight, key_weight, value_weight), qkv_plan, 3 * cols, n_s, 0)
     qkv_all = wide_gather(qkv.reshape(n_s * rows, 3 * cols))
+    if not halves:
+        out_all = wide_gather(lax.ppermute(output_weight, ("wide", "seq"), moves))
+    x_all, gate_up, gains, *out_heads = second_exchange(
+        after(flat, qkv), (gate_weight, up_weight), own_gain, output_weight if halves else None, feed_plan, 2 * half, n_w, n_s, 1
+    )
     if halves:
-        out_halves = wide_gather(after(output_weight, qkv)).reshape(n_w, rows, width)
-    else:
-        out_all = wide_gather(lax.ppermute(output_weight, ("wide", "seq"), moves))
-    x_all, gate_up, gains = second_exchange(after(flat, qkv), (gate_weight, up_weight), own_gain, feed_plan, 2 * half, n_w, n_s, 1)
+        out_all = out_heads[0].reshape(cols, width)
     x_all = x_all.reshape(all_tokens, width)
     gate_up_all = wide_gather(gate_up.reshape(n_s * rows, 2 * half))
     down_block = down_weight
@@ -837,18 +981,14 @@
 
     own_gains = own_heads(gains)
 
+    x_all, down_all = lax.optimization_barrier((x_all, down_all))
     lin = dot(x_all, qkv_all)
     q_lin, k_lin = lin[:, :cols], lin[:, cols : 2 * cols]
 
     def stack_sums(a, b):
         return jnp.stack([a, b] + [jnp.zeros_like(a)] * 6)
 
-    sums = stack_sums(jnp.sum(q_lin * q_lin, 1), jnp.sum(k_lin * k_lin, 1))
-    if halves:
-        sums, out_all = sums_exchange(sums, out_halves, False, n_w, n_s, 2)
-        out_all = out_all.reshape(cols, width)
-    else:
-        sums = exchange(sums, n_w, n_s, False, 2)
+    sums = exchange(stack_sums(jnp.sum(q_lin * q_lin, 1), jnp.sum(k_lin * k_lin, 1)), n_w, n_s, False, 2)
     inv = lax.rsqrt(jnp.sum(sums, 0)[:2] / width + eps_norm).T
     tables = rotation_tables(jnp.arange(row_len, dtype=jnp.int32))
     docs = documents[:, 0, :]
@@ -862,19 +1002,12 @@
         dot(attended, out_all).astype(bf16), (flat, gains[2:3]), mixed_rows, [own_f32, own_f32, ((tokens, 1), f32)], n_s, 3, False
     )
     hidden_all = hidden_all.reshape(all_tokens, width)
-    gate_up_lin = dot(hidden_all, gate_up_all)
-    gate_lin, upward = gate_up_lin[:, :half], gate_up_lin[:, half:]
-    sigma = jax.nn.sigmoid(gate_lin)
-    silu_gate = gate_lin * sigma
-    active = (silu_gate * upward).astype(bf16)
+    active, slope, swish = feed_forward(hidden_all, gate_up_all)
     d_down_all, layer_out, feed_term = around(
         dot(active, down_all).astype(bf16), (hidden, cot, gains[3:4]), down_rows, [((tokens, width), bf16), vec_f32], n_s, 4, True
     )
     d_down_all = d_down_all.reshape(all_tokens, width)
-    d_active = dot_t(d_down_all, down_all)
-    d_gate = (d_active * upward * sigma * (1.0 + gate_lin * (1.0 - sigma))).astype(bf16)
-    d_up = (d_active * silu_gate).astype(bf16)
-    d_gate_up = jnp.concatenate([d_gate, d_up], axis=1)
+    d_gate_up = feed_back(d_down_all, down_all, slope, swish)
     mlp_part = t_dot(hidden_all, d_gate_up).astype(bf16)
     mlp_grad = wide_scatter(mlp_part)
     d_mixed_all, d_hidden, attention_term, down_part = around(
@@ -883,7 +1016,6 @@
     )
     mlp_grad, d_mixed_all, down_part = lax.optimization_barrier((mlp_grad, d_mixed_all, down_part))
     down_grad = wide_scatter(down_part)
-    mlp_grad = lax.all_to_all(mlp_grad, "seq", 0, 0, tiled=True)
     d_mixed_all = d_mixed_all.reshape(all_tokens, width)
     out_part = t_dot(attended, d_mixed_all).astype(bf16)
     d_attended = dot_t(d_mixed_all, out_all).astype(bf16).reshape(shape4)
@@ -894,10 +1026,11 @@
     d_qg, d_kg = d_q * own_gains[0], d_k * own_gains[1]
     mean_sums = stack_sums(jnp.sum(d_qg * q_n, 1), jnp.sum(d_kg * k_n, 1))
     if halves:
-        mean_sums, out_part = sums_exchange(mean_sums, out_part.reshape(heads, 2, rows, width), True, n_w, n_s, 6)
+        mean_sums, out_part = sums_exchange(mean_sums, out_part.reshape(heads, 2, rows, width), n_w, n_s, 6)
     else:
         mean_sums = exchange(mean_sums, n_w, n_s, False, 6)
     mean_sums, mlp_grad = lax.optimization_barrier((mean_sums, mlp_grad))
+    mlp_grad = lax.all_to_all(mlp_grad, "seq", 0, 0, tiled=True)
     means = jnp.sum(mean_sums, 0)[:2].T / width
     query_term = jnp.sum(d_q * q_n, 0)
     key_term = jnp.sum(d_k * k_n, 0)
@@ -905,13 +1038,7 @@
     d_k_lin = (inv[:, 1:2] * (d_kg - k_n * means[:, 1:2])).astype(bf16)
     d_lin = jnp.concatenate([d_q_lin, d_k_lin, d_v], axis=1)
     qkv_part = t_dot(x_all, d_lin).astype(bf16)
-    down_grad, qkv_part = lax.optimization_barrier((down_grad, qkv_part))
-    input_grad = last_sum(dot_t(after(d_lin, qkv_part), qkv_all).astype(bf16), d_hidden, n_s, 7).reshape(inputs.shape)
-    qkv_grad = wide_scatter(qkv_part)
-    out_grad = wide_scatter(after(out_part, qkv_grad, input_grad).reshape(cols, width))
-    if not halves:
-        out_grad = lax.ppermute(out_grad, ("wide", "seq"), back_moves)
-
+    d_hidden, down_grad = lax.optimization_barrier((d_hidden, down_grad))
     def spread(term):
         full = jnp.zeros((width,), f32)
         for i in range(heads):
@@ -921,7 +1048,14 @@
     terms = jnp.stack([spread(query_term), spread(key_term), attention_term[0], feed_term[0]])
     terms = jnp.swapaxes(terms.reshape(4, n_dev, rows), 0, 1)
     terms = jnp.pad(terms, ((0, 0), (0, 4), (0, 128 - rows)))
-    qkv_grad, all_terms = final_exchange(qkv_grad.reshape(n_s, rows, 3 * cols), after(terms, input_grad), n_w, n_s, 8)
+    input_grad, all_terms = last_sum(dot_t(after(d_lin, qkv_part), qkv_all).astype(bf16), d_hidden, terms, n_w, n_s, 7)
+    input_grad = input_grad.reshape(inputs.shape)
+    qkv_grad = wide_scatter(qkv_part)
+    out_grad = wide_scatter(after(out_part, qkv_grad, input_grad).reshape(cols, width))
+    if not halves:
+        out_grad = lax.ppermute(out_grad, ("wide", "seq"), back_moves)
+
+    qkv_grad = final_exchange(after(qkv_grad, input_grad).reshape(n_s, rows, 3 * cols), n_w, n_s, 8)
     gate_grad, up_grad = unpack(mlp_grad.reshape(n_s, rows, 2 * half), feed, feed_plan)
     query_grad, key_grad, value_grad = unpack(qkv_grad, width, qkv_plan)
     gain_grads = jnp.sum(all_terms, 0)[:4, :rows]

time: 627 us -> 594 us (0.947)
  matrix products: 85 us -> 60.7 us
  Pallas kernels: 452 us -> 472 us
  waiting for transfers between devices: 14.9 us -> 2.7 us
  other arithmetic: 25.2 us -> 15.3 us
    pallas_call x5 -> x7, Pallas kernels: 203 us -> 221 us  [the longest x1 83.2 us: second_exchange(): pl.pallas_call(functools.partial(second_kernel, n_w, n_s, chunks, plan, b...]
    dot_general x4 -> x3, matrix products: 32.4 us -> 15.5 us  [dot(): return jnp.dot(a, b, preferred_element_type=f32)]
    all_gather x4 -> x3, waiting for transfers between devices: 13.6 us -> 0.04 us  [wide_gather(): return lax.all_gather(block, 'wide', axis=0, tiled=True)]
    dot_general x4 -> x3, matrix products: 33.8 us -> 24.7 us  [dot_t(): lax.dot_general(a, b, (((1,), (1,)), ((), ())), preferred_element_type=f32)]
    unnamed x76 -> x70, local copies, waits for them, and re-layouts: 13.7 us -> 12.2 us
  transfers between devices with their start and end apart: 9 -> 8, of which waited for: 1 -> 1; matrix products, arithmetic and copies ran while one was open for 13% -> 10% of each run, Pallas kernels for 59% -> 64%
where the time goes in v5:
time: 594 us; the launch traced here: 585 us
  Pallas kernels  472 us (79%)
  matrix products  60.7 us (10%)
  other arithmetic  15.3 us (3%)
  between operations  15.1 us (3%)
  local copies, waits for them, and re-layouts  14.9 us (3%)
    pallas_call x3, Pallas kernels, around(): pl.pallas_call(functools.partial(around_kernel, n_s, chunks, rows_fn, len...  211 us
    pallas_call x1, Pallas kernels, second_exchange(): pl.pallas_call(functools.partial(second_kernel, n_w, n_s, chunks, plan, b...  83.2 us
    pallas_call x1, Pallas kernels, last_sum(): pl.pallas_call(functools.partial(last_kernel, n_w, n_s, chunks), out_shap...  62.2 us
    dot_general x3, matrix products, dot_t(): lax.dot_general(a, b, (((1,), (1,)), ((), ())), preferred_element_type=f32)  24.7 us
    pallas_call x1, Pallas kernels, first_exchange(): pl.pallas_call(functools.partial(first_kernel, n_s, plan), out_shape=jax....  21.7 us
    pallas_call x1, Pallas kernels, final_exchange(): pl.pallas_call(functools.partial(final_kernel, n_w, n_s), out_shape=jax.S...  20.8 us
    dot_general x3, matrix products, t_dot(): lax.dot_general(a, b, (((0,), (0,)), ((), ())), preferred_element_type=f32)  20.5 us
    pallas_call x1, Pallas kernels, sums_exchange(): pl.pallas_call(functools.partial(sums_kernel, n_w, n_s), out_shape=[jax.S...  15.6 us
  transfers between devices with their start and end apart: 8, of which 1 were waited for; matrix products, arithmetic and copies ran while one was open for 10% of the time, Pallas kernels for 64%

profile of v5, /device:TPU:9, one launch (start us, length us, event | category | flops | bytes accessed | tf_op | source)
XLA Modules:
  0.0 585.3 jit_solution(5682254147477180645)
XLA Ops:
  8.0 21.7 %shard_map.237 = bf16[8,64,768]{2,1,0:T(8,128)(2,1)} custom-call(bf16[64,2048]{1,0:T(8,128)(2,1)} %qw.1, bf16[64,2048]{1,0:T(8,128)(2,1)} %kw.1, bf16[64,2048]{1,0:T(8,128)(2,1)} %vw.1), custom_call_target="tpu_custom_call" | custom-call | bytes 60000000 | tf_op jit(solution)/shard_map/pallas_call | solution.py:533
  29.7 1.3 fusion.16.gain
  31.1 83.2 %shard_map.238 = (bf16[8,128,2048]{2,1,0:T(8,128)(2,1)}, bf16[8,64,2048]{2,1,0:T(8,128)(2,1)}, f32[32,8,128]{2,1,0:T(8,128)}, bf16[2,2,64,2048]{3,2,1,0:T(8,128)(2,1)}) custom-call(bf16[128,2048]{1,0:T(8,128)(2,1)} %bitcast.103, bf16[64,8192]{1,0:T(8,128)(2,1)} %gw.1, bf16[64,8192]{1,0:T(8,128)(2,1)} %uw.1, f32[8,128]{1,0:T(8,128)} %fusion.16.gain, ...), custom_call_target="tpu_custom_call" | custom-call | bytes 240000000 | tf_op jit(solution)/shard_map/pallas_call | solution.py:632
  114.4 0.9 slice_bitcast_fusion
  116.1 1.0 fusion.2
  117.4 6.1 %fusion.22 = f32[1024,768]{1,0:T(8,128)S(1)} fusion(bf16[1024,2048]{1,0:T(8,128)(2,1)} %bitcast.150, bf16[2048,768]{1,0:T(8,128)(2,1)} %all-gather.6.cloned.1.call-done), kind=kOutput, calls=%fused_computation.72 | convolution fusion | flops 3221225472 | bytes 10485760 | tf_op jit(solution)/shard_map/dot_general | solution.py:794
  123.6 1.6 copy-done.25
  126.3 15.1 %shard_map.239 = f32[8,8,1024]{2,1,0:T(8,128)} custom-call(f32[8,1024]{1,0:T(8,128)} %maximum_maximum_fusion.x_ref), custom_call_target="tpu_custom_call" | custom-call | bytes 30000000 | tf_op jit(solution)/shard_map/pallas_call | solution.py:490
  141.4 1.0 reduce_sum.83
  142.7 7.4 %shard_map.240 = (bf16[8,2,64,256]{3,2,1,0:T(8,128)(2,1)S(1)}, bf16[8,2,64,256]{3,2,1,0:T(8,128)(2,1)S(1)}, bf16[8,2,64,256]{3,2,1,0:T(8,128)(2,1)S(1)}, bf16[8,...) custom-call(f32[8,2,64,768]{3,2,1,0:T(8,128)} %bitcast.118, f32[8,2,64,768]{3,2,1,0:T(8,128)} %bitcast.119, ...), custom_call_target="tpu_custom_call" | custom-call | tf_op jit(solution)/shard_map/pallas_call | solution.py:876
  150.1 0.8 copy-done.14
  150.9 0.8 copy-done.5
  151.6 3.3 convolution_convert_fusion.2
  154.9 66.6 %shard_map.241 = (bf16[8,128,2048]{2,1,0:T(8,128)(2,1)}, f32[128,2048]{1,0:T(8,128)S(1)}, f32[128,2048]{1,0:T(8,128)S(1)}, f32[128,1]{1,0:T(8,128)S(1)}) custom-call(bf16[8,128,2048]{2,1,0:T(8,128)(2,1)} %bitcast.121, bf16[128,2048]{1,0:T(8,128)(2,1)S(1)} %bitcast.104, f32[1,2048]{1,0:T(1,128)S(1)} %slice.86.refs_2_.refs_4_), custom_call_target="tpu_custom_call" | custom-call | bytes 210000000 | tf_op jit(solution)/shard_map/pallas_call | solution.py:353
  221.6 1.0 copy-done.10
  222.6 1.0 copy-done.12
  223.5 14.0 %shard_map.242 = (bf16[1024,1024]{1,0:T(8,128)(2,1)S(1)}, bf16[1024,1024]{1,0:T(8,128)(2,1)S(1)}, bf16[1024,1024]{1,0:T(8,128)(2,1)}) custom-call(bf16[1024,2048]{1,0:T(8,128)(2,1)} %bitcast.154, bf16[2048,2048]{1,0:T(8,128)(2,1)} %all-gather.8.cloned.1.call-done.gate_w.up_w, bf16[2048,2048]{1,0:T(8,128)(2,1)} %all-gather.8.cloned.1.call-done.gate_w.up_w), custom_call_target="tpu_custom_call" | custom-call | flops 8589934592 | bytes 12582912 | tf_op jit(solution)/shard_map/pallas_call | solution.py:720
  237.5 6.1 %convolution_convert_fusion.4 = bf16[1024,2048]{1,0:T(8,128)(2,1)} fusion(bf16[1024,1024]{1,0:T(8,128)(2,1)S(1)} %get-tuple-element.70.refs_5_, bf16[1024,2048]{1,0:T(8,128)(2,1)S(1)} %copy-done.27), kind=kOutput, calls=%fused_computation.4 | convolution fusion | flops 4297064448 | bytes 10485760 | tf_op jit(solution)/shard_map/dot_general | solution.py:794
  243.6 70.6 %shard_map.243 = (bf16[8,128,2048]{2,1,0:T(8,128)(2,1)}, bf16[128,2048]{1,0:T(8,128)(2,1)S(1)}, f32[1,2048]{1,0:T(1,128)S(1)}) custom-call(bf16[8,128,2048]{2,1,0:T(8,128)(2,1)} %bitcast.125, f32[128,2048]{1,0:T(8,128)S(1)} %copy-done.11, bf16[128,2048]{1,0:T(8,128)(2,1)S(1)} %bitcast.105, f32[1,2048]{1,0:T(1,128)S(1)} %slice.88.refs_3_), custom_call_target="tpu_custom_call" | custom-call | bytes 210000000 | tf_op jit(solution)/shard_map/pallas_call | solution.py:353
  314.2 10.5 %shard_map.244 = bf16[1024,2048]{1,0:T(8,128)(2,1)} custom-call(bf16[1024,2048]{1,0:T(8,128)(2,1)} %bitcast.122, bf16[1024,2048]{1,0:T(8,128)(2,1)} %all-gather.4.cloned.1.call-done.down_w, bf16[1024,1024]{1,0:T(8,128)(2,1)S(1)} %get-tuple-element.79.slope, bf16[1024,1024]{1,0:T(8,128)(2,1)S(1)} %copy-done.2), custom_call_target="tpu_custom_call" | custom-call | flops 4294967296 | bytes 8388608 | tf_op jit(solution)/shard_map/pallas_call | solution.py:748
  324.7 13.3 %convolution_convert_fusion = bf16[2048,2048]{1,0:T(8,128)(2,1)} fusion(bf16[1024,2048]{1,0:T(8,128)(2,1)S(1)} %bitcast.155, bf16[1024,2048]{1,0:T(8,128)(2,1)} %shard_map.244), kind=kOutput, calls=%fused_computation | convolution fusion | flops 8594128896 | bytes 16777216 | tf_op jit(solution)/shard_map/dot_general | solution.py:802
  338.2 14.0 %convolution_convert_fusion.1 = bf16[1024,2048]{1,0:T(8,128)(2,1)} fusion(bf16[1024,2048]{1,0:T(8,128)(2,1)} %shard_map.244, bf16[2048,2048]{1,0:T(8,128)(2,1)} %all-gather.8.cloned.1.call-done.gate_w.up_w), kind=kOutput, calls=%fused_computation.1 | convolution fusion | flops 8592031744 | bytes 16777216 | tf_op jit(solution)/shard_map/dot_general | solution.py:798
  352.2 73.9 %shard_map.245 = (bf16[8,128,2048]{2,1,0:T(8,128)(2,1)}, f32[128,2048]{1,0:T(8,128)S(1)}, f32[1,2048]{1,0:T(1,128)S(1)}, bf16[1024,2048]{1,0:T(8,128)(2,1)}) custom-call(bf16[8,128,2048]{2,1,0:T(8,128)(2,1)} %bitcast.126, bf16[128,2048]{1,0:T(8,128)(2,1)S(1)} %bitcast.106, f32[128,2048]{1,0:T(8,128)S(1)} %copy-done.13, ...), custom_call_target="tpu_custom_call" | custom-call | bytes 210000000 | tf_op jit(solution)/shard_map/pallas_call | solution.py:353
  426.1 1.0 copy-done.8
  427.1 1.1 copy-done.30
  428.3 3.7 convolution_convert_fusion.7
  432.0 7.1 %shard_map.246 = (f32[8,2,64,256]{3,2,1,0:T(8,128)S(1)}, f32[8,2,64,256]{3,2,1,0:T(8,128)S(1)}, bf16[8,2,64,256]{3,2,1,0:T(8,128)(2,1)S(1)}) custom-call(bf16[8,2,64,256]{3,2,1,0:T(8,128)(2,1)S(1)} %copy-done.15, bf16[8,2,64,256]{3,2,1,0:T(8,128)(2,1)S(1)} %copy-done.17, bf16[8,2,64,256]{3,2,1,0:T(8,128)(2,1)S(1)} %copy-done.19, ...), custom_call_target="tpu_custom_call" | custom-call | tf_op jit(solution)/shard_map/pallas_call | solution.py:890
  439.1 0.9 fusion.1
  440.7 2.2 convolution_convert_fusion.6
  443.0 15.6 %shard_map.247 = (f32[8,8,1024]{2,1,0:T(8,128)}, bf16[4,64,2048]{2,1,0:T(8,128)(2,1)}) custom-call(f32[8,1024]{1,0:T(8,128)} %maximum_maximum_fusion.1.x, bf16[2,2,64,2048]{3,2,1,0:T(8,128)(2,1)} %bitcast.131), custom_call_target="tpu_custom_call" | custom-call | bytes 30000000 | tf_op jit(solution)/shard_map/pallas_call | solution.py:673
  458.6 1.0 reduce_sum.86
  459.6 2.3 multiply_convert_fusion.1
  461.9 0.8 copy-done.28
  462.7 5.0 convolution_convert_fusion.5
  467.7 3.9 all-to-all-start
  472.2 1.1 pad_maximum_fusion
  473.3 7.0 %convolution_convert_fusion.3 = bf16[1024,2048]{1,0:T(8,128)(2,1)} fusion(bf16[1024,768]{1,0:T(8,128)(2,1)S(1)} %pad_maximum_fusion, bf16[2048,768]{1,0:T(8,128)(2,1)} %all-gather.6.cloned.1.call-done), kind=kOutput, calls=%fused_computation.3 | convolution fusion | flops 3223322624 | bytes 8912896 | tf_op jit(solution)/shard_map/dot_general | solution.py:798
  480.3 1.9 reduce-scatter.7.cloned.1.call-done
  482.2 1.2 copy-done.9
  483.4 62.2 %shard_map.248 = (f32[128,2048]{1,0:T(8,128)S(1)}, f32[32,8,128]{2,1,0:T(8,128)S(1)}) custom-call(bf16[8,128,2048]{2,1,0:T(8,128)(2,1)} %bitcast.124, f32[128,2048]{1,0:T(8,128)S(1)} %copy-done.9, f32[32,8,128]{2,1,0:T(8,128)S(1)} %pad.12.terms), custom_call_target="tpu_custom_call" | custom-call | bytes 120000000 | tf_op jit(solution)/shard_map/pallas_call | solution.py:384
  545.7 2.2 shard_map.251
  547.9 20.8 %shard_map.249.slots = bf16[8,64,768]{2,1,0:T(8,128)(2,1)} custom-call(bf16[8,64,768]{2,1,0:T(8,128)(2,1)} %bitcast.134), custom_call_target="tpu_custom_call" | custom-call | bytes 60000000 | tf_op jit(solution)/shard_map/pallas_call | solution.py:692
  568.8 1.1 copy-done
  569.9 1.2 shard_map.250
  571.1 2.8 convert_element_type.66
  574.5 1.8 convert_element_type.65
  576.3 0.8 copy.49
  577.1 1.0 copy.50
  (115 shorter events, 5.3 us)
Async XLA Ops:
  7.2 108.4 %copy-start.24 = (s32[2,1,512]{2,1,0:T(1,128)S(1)}, s32[2,1,512]{2,1,0:T(1,128)}, u32[]{:S(2)}) copy-start(s32[2,1,512]{2,1,0:T(1,128)} %doc_k.3) | copy-start | bytes 12292
  7.2 110.2 %all-gather.4.cloned.1.call-start = ((), (), s32[]{:S(2)}) async-start(), calls=%async_computation.5 | async-start | bytes 5242880 | tf_op jit(solution)/shard_map/all_gather | solution.py:913
  7.9 109.5 %all-gather.6.cloned.1.call-start = ((), (), s32[]{:S(2)}) async-start(), calls=%async_computation.6 | async-start | bytes 3932160 | tf_op jit(solution)/shard_map/all_gather | solution.py:913
  29.7 193.8 %all-gather.8.cloned.1.call-start = ((), (), s32[]{:S(2)}) async-start(), calls=%async_computation.7 | async-start | bytes 10485760 | tf_op jit(solution)/shard_map/all_gather | solution.py:913
  114.3 312.7 %reduce-scatter.5.cloned.1.call-start = ((), (), s32[]{:S(2)}) async-start(), calls=%async_computation.8 | async-start | bytes 10485760 | tf_op jit(solution)/shard_map/reduce_scatter | solution.py:917
  123.6 1.6 copy-start.25
  142.6 9.0 %copy-start.29 = (bf16[2,2,64,2048]{3,2,1,0:T(8,128)(2,1)S(1)}, bf16[2,2,64,2048]{3,2,1,0:T(8,128)(2,1)}, u32[]{:S(2)}) copy-start(bf16[2,2,64,2048]{3,2,1,0:T(8,128)(2,1)} %get-tuple-element.67) | copy-start | bytes 3145732
  150.0 0.8 copy-start.14
  150.8 0.8 copy-start.5
  150.8 4.1 copy-start.7
  150.8 4.1 copy-start.16
  150.8 70.7 %copy-start.18 = (bf16[8,2,64,256]{3,2,1,0:T(8,128)(2,1)}, bf16[8,2,64,256]{3,2,1,0:T(8,128)(2,1)S(1)}, u32[]{:S(2)}) copy-start(bf16[8,2,64,256]{3,2,1,0:T(8,128)(2,1)S(1)} %get-tuple-element.76.v) | copy-start | bytes 1572868
  150.9 4.1 copy-start.1
  221.6 1.0 copy-start.10
  222.6 1.0 copy-start.12
  223.5 14.0 %copy-start.27 = (bf16[1024,2048]{1,0:T(8,128)(2,1)S(1)}, bf16[1024,2048]{1,0:T(8,128)(2,1)}, u32[]{:S(2)}) copy-start(bf16[1024,2048]{1,0:T(8,128)(2,1)} %all-gather.4.cloned.1.call-done.down_w) | copy-start | bytes 12582916
  237.5 6.1 %copy-start.3 = (bf16[2,1,64,2048]{3,2,1,0:T(8,128)(2,1)S(1)}, bf16[2,1,64,2048]{3,2,1,0:T(8,128)(2,1)}, u32[]{:S(2)}) copy-start(bf16[2,1,64,2048]{3,2,1,0:T(8,128)(2,1)} %param.16) | copy-start | bytes 1572868
  237.5 6.1 %copy-start.11 = (f32[128,2048]{1,0:T(8,128)S(1)}, f32[128,2048]{1,0:T(8,128)}, u32[]{:S(2)}) copy-start(f32[128,2048]{1,0:T(8,128)} %copy-done.10) | copy-start | bytes 3145732
  243.6 70.6 %copy-start.2 = (bf16[1024,1024]{1,0:T(8,128)(2,1)S(1)}, bf16[1024,1024]{1,0:T(8,128)(2,1)}, u32[]{:S(2)}) copy-start(bf16[1024,1024]{1,0:T(8,128)(2,1)} %get-tuple-element.80.swish) | copy-start | bytes 6291460
  314.2 10.5 %copy-start.20 = (bf16[128,2048]{1,0:T(8,128)(2,1)}, bf16[128,2048]{1,0:T(8,128)(2,1)S(1)}, u32[]{:S(2)}) copy-start(bf16[128,2048]{1,0:T(8,128)(2,1)S(1)} %get-tuple-element.73) | copy-start | bytes 1572868
  314.2 10.5 %copy-start.33 = (bf16[8,128,2048]{2,1,0:T(8,128)(2,1)S(1)}, bf16[8,128,2048]{2,1,0:T(8,128)(2,1)}, u32[]{:S(2)}) copy-start(bf16[8,128,2048]{2,1,0:T(8,128)(2,1)} %get-tuple-element.68) | copy-start | bytes 12582916
  338.1 144.1 %reduce-scatter.7.cloned.1.call-start = ((), (), s32[]{:S(2)}) async-start(), calls=%async_computation.9 | async-start | bytes 5242880 | tf_op jit(solution)/shard_map/reduce_scatter | solution.py:917
  338.1 14.1 %copy-start.4 = (bf16[2,1,64,2048]{3,2,1,0:T(8,128)(2,1)S(1)}, bf16[2,1,64,2048]{3,2,1,0:T(8,128)(2,1)}, u32[]{:S(2)}) copy-start(bf16[2,1,64,2048]{3,2,1,0:T(8,128)(2,1)} %param.16) | copy-start | bytes 1572868
  338.1 14.0 %copy-start.13 = (f32[128,2048]{1,0:T(8,128)S(1)}, f32[128,2048]{1,0:T(8,128)}, u32[]{:S(2)}) copy-start(f32[128,2048]{1,0:T(8,128)} %copy-done.12) | copy-start | bytes 3145732
  426.1 1.0 copy-start.8
  427.0 1.2 copy-start.30
  427.1 118.6 %reduce-scatter.9.cloned.1.call-start = ((), (), s32[]{:S(2)}) async-start(), calls=%async_computation.10 | async-start | bytes 3932160 | tf_op jit(solution)/shard_map/reduce_scatter | solution.py:917
  428.2 3.7 copy-start.15
  428.3 3.7 copy-start.17
  428.3 3.7 copy-start.19
  431.9 7.2 %copy-start.26 = (f32[1024,768]{1,0:T(8,128)S(1)}, f32[1024,768]{1,0:T(8,128)}, u32[]{:S(2)}) copy-start(f32[1024,768]{1,0:T(8,128)} %copy-done.25) | copy-start | bytes 9437188
  432.0 8.8 %copy-start.6 = (bf16[8,2,64,256]{3,2,1,0:T(8,128)(2,1)S(1)}, bf16[8,2,64,256]{3,2,1,0:T(8,128)(2,1)}, u32[]{:S(2)}) copy-start(bf16[8,2,64,256]{3,2,1,0:T(8,128)(2,1)} %copy-done.5) | copy-start | bytes 1572868
  432.0 8.8 %copy-start.32 = (bf16[8,128,2048]{2,1,0:T(8,128)(2,1)S(1)}, bf16[8,128,2048]{2,1,0:T(8,128)(2,1)}, u32[]{:S(2)}) copy-start(bf16[8,128,2048]{2,1,0:T(8,128)(2,1)} %get-tuple-element.86) | copy-start | bytes 12582916
  439.1 3.9 copy-start.22
  443.0 19.7 %copy-start.23 = (bf16[8,2,64,256]{3,2,1,0:T(8,128)(2,1)S(1)}, bf16[8,2,64,256]{3,2,1,0:T(8,128)(2,1)}, u32[]{:S(2)}) copy-start(bf16[8,2,64,256]{3,2,1,0:T(8,128)(2,1)} %copy-done.22) | copy-start | bytes 1572868
  459.6 3.1 copy-start.31
  461.9 0.8 copy-start.28
  467.7 78.0 %all-to-all-start = ((bf16[8,64,2048]{2,1,0:T(8,128)(2,1)}), bf16[8,64,2048]{2,1,0:T(8,128)(2,1)S(1)}, u32[]{:S(2)}, u32[]{:S(2)}) async-start(bf16[8,64,2048]{2,1,0:T(8,128)(2,1)} %bitcast.129), calls=%async_computation.4 | async-start | bytes 4194304 | tf_op jit(solution)/shard_map/all_to_all | solution.py:1033
  471.6 102.9 %reduce-scatter.11.cloned.1.call-start = ((), (), s32[]{:S(2)}) async-start(), calls=%async_computation.11 | async-start | bytes 1310720 | tf_op jit(solution)/shard_map/reduce_scatter | solution.py:917
  482.2 1.2 copy-start.9
  547.9 28.4 %copy-start.21 = (bf16[128,2048]{1,0:T(8,128)(2,1)S(1)}, bf16[128,2048]{1,0:T(8,128)(2,1)}, u32[]{:S(2)}) copy-start(bf16[128,2048]{1,0:T(8,128)(2,1)} %copy-done.20) | copy-start | bytes 1572868
  568.8 1.1 copy-start
Sparse Core Ops, SparseCore 0:
  9.9 62.5 all-gather.3
  74.3 42.8 all-gather.5
  119.0 87.5 all-gather.7
  338.2 87.9 reduce-scatter.4
  429.3 52.8 reduce-scatter.6
  485.0 44.9 reduce-scatter.8
  545.8 25.5 reduce-scatter.10

commit v6 on v5

--- a/solution.py
+++ b/solution.py
@@ -619,7 +619,7 @@
         other.finish()
 
 
-def second_exchange(x, weights, gain, out_block, plan, cols, n_w, n_s, cid, chunks=2):
+def second_exchange(x, weights, gain, out_block, plan, cols, n_w, n_s, cid, chunks=4):
     rows, width = x.shape
     count = n_w * n_s
     shapes = [((n_s, rows, width), bf16), ((n_s, weights[0].shape[0], cols), bf16), ((count, *gain.shape), gain.dtype)]
@@ -741,7 +741,7 @@
     out[:, pl.ds(pl.multiple_of(at + half, tile), tile)] = (d_active * swish[...].astype(f32)).astype(bf16)
 
 
-def feed_back(d_down, down_w, slope, swish, tile=256):
+def feed_back(d_down, down_w, slope, swish, tile=512):
     tokens, width = d_down.shape
     half = down_w.shape[0]
     cols = pl.BlockSpec((tokens, tile), lambda j: (0, j))
@@ -986,10 +986,10 @@
     q_lin, k_lin = lin[:, :cols], lin[:, cols : 2 * cols]
 
     def stack_sums(a, b):
-        return jnp.stack([a, b] + [jnp.zeros_like(a)] * 6)
+        return jnp.stack([a, b]).reshape(-1, 128)
 
     sums = exchange(stack_sums(jnp.sum(q_lin * q_lin, 1), jnp.sum(k_lin * k_lin, 1)), n_w, n_s, False, 2)
-    inv = lax.rsqrt(jnp.sum(sums, 0)[:2] / width + eps_norm).T
+    inv = lax.rsqrt(jnp.sum(sums, 0).reshape(2, all_tokens) / width + eps_norm).T
     tables = rotation_tables(jnp.arange(row_len, dtype=jnp.int32))
     docs = documents[:, 0, :]
     shape4 = (n_s, micro, local, -1)
@@ -1031,7 +1031,7 @@
         mean_sums = exchange(mean_sums, n_w, n_s, False, 6)
     mean_sums, mlp_grad = lax.optimization_barrier((mean_sums, mlp_grad))
     mlp_grad = lax.all_to_all(mlp_grad, "seq", 0, 0, tiled=True)
-    means = jnp.sum(mean_sums, 0)[:2].T / width
+    means = jnp.sum(mean_sums, 0).reshape(2, all_tokens).T / width
     query_term = jnp.sum(d_q * q_n, 0)
     key_term = jnp.sum(d_k * k_n, 0)
     d_q_lin = (inv[:, 0:1] * (d_qg - q_n * means[:, 0:1])).astype(bf16)

time: 594 us -> 588 us (0.990)
  Pallas kernels: 472 us -> 461 us
    pallas_call x1, Pallas kernels: 15.1 us -> 8.84 us  [exchange(): pl.pallas_call(functools.partial(share_kernel, n_w, n_s, whole), out_shap...]
    unnamed x70 -> x68, local copies, waits for them, and re-layouts: 12.2 us -> 13 us
  transfers between devices with their start and end apart: 8 -> 8, of which waited for: 1 -> 2; matrix products, arithmetic and copies ran while one was open for 10% -> 10% of each run, Pallas kernels for 64% -> 63%
where the time goes in v6:
time: 588 us; the launch traced here: 579 us
  Pallas kernels  461 us (78%)
  matrix products  63.3 us (11%)
  local copies, waits for them, and re-layouts  16.7 us (3%)
  between operations  15.1 us (3%)
  other arithmetic  13.7 us (2%)
    pallas_call x3, Pallas kernels, around(): pl.pallas_call(functools.partial(around_kernel, n_s, chunks, rows_fn, len...  212 us
    pallas_call x1, Pallas kernels, second_exchange(): pl.pallas_call(functools.partial(second_kernel, n_w, n_s, chunks, plan, b...  81.6 us
    pallas_call x1, Pallas kernels, last_sum(): pl.pallas_call(functools.partial(last_kernel, n_w, n_s, chunks), out_shap...  62.2 us
    dot_general x3, matrix products, dot_t(): lax.dot_general(a, b, (((1,), (1,)), ((), ())), preferred_element_type=f32)  24.7 us
    dot_general x3, matrix products, t_dot(): lax.dot_general(a, b, (((0,), (0,)), ((), ())), preferred_element_type=f32)  23 us
    pallas_call x1, Pallas kernels, first_exchange(): pl.pallas_call(functools.partial(first_kernel, n_s, plan), out_shape=jax....  21.7 us
    pallas_call x1, Pallas kernels, final_exchange(): pl.pallas_call(functools.partial(final_kernel, n_w, n_s), out_shape=jax.S...  20.8 us
    dot_general x3, matrix products, dot(): return jnp.dot(a, b, preferred_element_type=f32)  15.5 us
  transfers between devices with their start and end apart: 8, of which 2 were waited for; matrix products, arithmetic and copies ran while one was open for 10% of the time, Pallas kernels for 63%

profile of v6, /device:TPU:9, one launch (start us, length us, event | category | flops | bytes accessed | tf_op | source)
XLA Modules:
  0.0 579.2 jit_solution(5641209290252950244)
XLA Ops:
  8.0 21.7 %shard_map.237 = bf16[8,64,768]{2,1,0:T(8,128)(2,1)} custom-call(bf16[64,2048]{1,0:T(8,128)(2,1)} %qw.1, bf16[64,2048]{1,0:T(8,128)(2,1)} %kw.1, bf16[64,2048]{1,0:T(8,128)(2,1)} %vw.1), custom_call_target="tpu_custom_call" | custom-call | bytes 60000000 | tf_op jit(solution)/shard_map/pallas_call | solution.py:533
  29.7 1.3 fusion.12.gain
  31.1 81.6 %shard_map.238 = (bf16[8,128,2048]{2,1,0:T(8,128)(2,1)}, bf16[8,64,2048]{2,1,0:T(8,128)(2,1)}, f32[32,8,128]{2,1,0:T(8,128)}, bf16[2,2,64,2048]{3,2,1,0:T(8,128)(2,1)}) custom-call(bf16[128,2048]{1,0:T(8,128)(2,1)} %bitcast.101, bf16[64,8192]{1,0:T(8,128)(2,1)} %gw.1, bf16[64,8192]{1,0:T(8,128)(2,1)} %uw.1, f32[8,128]{1,0:T(8,128)} %fusion.12.gain, ...), custom_call_target="tpu_custom_call" | custom-call | bytes 240000000 | tf_op jit(solution)/shard_map/pallas_call | solution.py:632
  112.8 0.9 slice_bitcast_fusion
  114.4 1.0 fusion.2
  115.7 1.5 all-gather.6.cloned.1.call-done
  117.2 6.1 %fusion.18 = f32[1024,768]{1,0:T(8,128)S(1)} fusion(bf16[1024,2048]{1,0:T(8,128)(2,1)} %bitcast.151, bf16[2048,768]{1,0:T(8,128)(2,1)} %all-gather.6.cloned.1.call-done), kind=kOutput, calls=%fused_computation.68 | convolution fusion | flops 3221225472 | bytes 10485760 | tf_op jit(solution)/shard_map/dot_general | solution.py:794
  123.3 1.6 copy-done.25
  126.0 8.8 %shard_map.239 = f32[8,16,128]{2,1,0:T(8,128)} custom-call(f32[16,128]{1,0:T(8,128)} %reshape.150.x_ref), custom_call_target="tpu_custom_call" | custom-call | bytes 30000000 | tf_op jit(solution)/shard_map/pallas_call | solution.py:490
  134.8 0.9 reduce_sum.83
  135.9 7.4 %shard_map.240 = (bf16[8,2,64,256]{3,2,1,0:T(8,128)(2,1)S(1)}, bf16[8,2,64,256]{3,2,1,0:T(8,128)(2,1)S(1)}, bf16[8,2,64,256]{3,2,1,0:T(8,128)(2,1)S(1)}, bf16[8,...) custom-call(f32[8,2,64,768]{3,2,1,0:T(8,128)} %bitcast.116, f32[8,2,64,768]{3,2,1,0:T(8,128)} %bitcast.117, ...), custom_call_target="tpu_custom_call" | custom-call | tf_op jit(solution)/shard_map/pallas_call | solution.py:876
  143.3 0.8 copy-done.14
  144.9 3.3 convolution_convert_fusion.2
  148.2 67.4 %shard_map.241 = (bf16[8,128,2048]{2,1,0:T(8,128)(2,1)}, f32[128,2048]{1,0:T(8,128)S(1)}, f32[128,2048]{1,0:T(8,128)S(1)}, f32[128,1]{1,0:T(8,128)S(1)}) custom-call(bf16[8,128,2048]{2,1,0:T(8,128)(2,1)} %bitcast.119, bf16[128,2048]{1,0:T(8,128)(2,1)S(1)} %bitcast.102, f32[1,2048]{1,0:T(1,128)S(1)} %slice.79.refs_2_.refs_4_), custom_call_target="tpu_custom_call" | custom-call | bytes 210000000 | tf_op jit(solution)/shard_map/pallas_call | solution.py:353
  215.6 1.0 copy-done.10
  216.6 1.0 copy-done.12
  217.6 14.0 %shard_map.242 = (bf16[1024,1024]{1,0:T(8,128)(2,1)S(1)}, bf16[1024,1024]{1,0:T(8,128)(2,1)S(1)}, bf16[1024,1024]{1,0:T(8,128)(2,1)}) custom-call(bf16[1024,2048]{1,0:T(8,128)(2,1)} %bitcast.155, bf16[2048,2048]{1,0:T(8,128)(2,1)} %all-gather.8.cloned.1.call-done.gate_w.up_w, bf16[2048,2048]{1,0:T(8,128)(2,1)} %all-gather.8.cloned.1.call-done.gate_w.up_w), custom_call_target="tpu_custom_call" | custom-call | flops 8589934592 | bytes 12582912 | tf_op jit(solution)/shard_map/pallas_call | solution.py:720
  231.6 6.1 %convolution_convert_fusion.4 = bf16[1024,2048]{1,0:T(8,128)(2,1)} fusion(bf16[1024,1024]{1,0:T(8,128)(2,1)S(1)} %get-tuple-element.70.refs_5_, bf16[1024,2048]{1,0:T(8,128)(2,1)S(1)} %copy-done.27), kind=kOutput, calls=%fused_computation.4 | convolution fusion | flops 4297064448 | bytes 10485760 | tf_op jit(solution)/shard_map/dot_general | solution.py:794
  237.7 70.5 %shard_map.243 = (bf16[8,128,2048]{2,1,0:T(8,128)(2,1)}, bf16[128,2048]{1,0:T(8,128)(2,1)S(1)}, f32[1,2048]{1,0:T(1,128)S(1)}) custom-call(bf16[8,128,2048]{2,1,0:T(8,128)(2,1)} %bitcast.123, f32[128,2048]{1,0:T(8,128)S(1)} %copy-done.11, bf16[128,2048]{1,0:T(8,128)(2,1)S(1)} %bitcast.103, f32[1,2048]{1,0:T(1,128)S(1)} %slice.81.refs_3_), custom_call_target="tpu_custom_call" | custom-call | bytes 210000000 | tf_op jit(solution)/shard_map/pallas_call | solution.py:353
  308.2 10.1 %shard_map.244 = bf16[1024,2048]{1,0:T(8,128)(2,1)} custom-call(bf16[1024,2048]{1,0:T(8,128)(2,1)} %bitcast.120, bf16[1024,2048]{1,0:T(8,128)(2,1)} %all-gather.4.cloned.1.call-done.down_w, bf16[1024,1024]{1,0:T(8,128)(2,1)S(1)} %get-tuple-element.79.slope, bf16[1024,1024]{1,0:T(8,128)(2,1)S(1)} %copy-done.2), custom_call_target="tpu_custom_call" | custom-call | flops 4294967296 | bytes 8388608 | tf_op jit(solution)/shard_map/pallas_call | solution.py:748
  318.4 13.4 %convolution_convert_fusion = bf16[2048,2048]{1,0:T(8,128)(2,1)} fusion(bf16[1024,2048]{1,0:T(8,128)(2,1)S(1)} %bitcast.156, bf16[1024,2048]{1,0:T(8,128)(2,1)} %shard_map.244), kind=kOutput, calls=%fused_computation | convolution fusion | flops 8594128896 | bytes 16777216 | tf_op jit(solution)/shard_map/dot_general | solution.py:802
  331.9 14.0 %convolution_convert_fusion.1 = bf16[1024,2048]{1,0:T(8,128)(2,1)} fusion(bf16[1024,2048]{1,0:T(8,128)(2,1)} %shard_map.244, bf16[2048,2048]{1,0:T(8,128)(2,1)} %all-gather.8.cloned.1.call-done.gate_w.up_w), kind=kOutput, calls=%fused_computation.1 | convolution fusion | flops 8592031744 | bytes 16777216 | tf_op jit(solution)/shard_map/dot_general | solution.py:798
  345.9 73.9 %shard_map.245 = (bf16[8,128,2048]{2,1,0:T(8,128)(2,1)}, f32[128,2048]{1,0:T(8,128)S(1)}, f32[1,2048]{1,0:T(1,128)S(1)}, bf16[1024,2048]{1,0:T(8,128)(2,1)}) custom-call(bf16[8,128,2048]{2,1,0:T(8,128)(2,1)} %bitcast.124, bf16[128,2048]{1,0:T(8,128)(2,1)S(1)} %bitcast.104, f32[128,2048]{1,0:T(8,128)S(1)} %copy-done.13, ...), custom_call_target="tpu_custom_call" | custom-call | bytes 210000000 | tf_op jit(solution)/shard_map/pallas_call | solution.py:353
  419.8 1.0 copy-done.8
  420.9 1.1 copy-done.30
  422.0 3.6 convolution_convert_fusion.7
  425.6 7.1 %shard_map.246 = (f32[8,2,64,256]{3,2,1,0:T(8,128)S(1)}, f32[8,2,64,256]{3,2,1,0:T(8,128)S(1)}, bf16[8,2,64,256]{3,2,1,0:T(8,128)(2,1)S(1)}) custom-call(bf16[8,2,64,256]{3,2,1,0:T(8,128)(2,1)S(1)} %copy-done.15, bf16[8,2,64,256]{3,2,1,0:T(8,128)(2,1)S(1)} %copy-done.17, bf16[8,2,64,256]{3,2,1,0:T(8,128)(2,1)S(1)} %copy-done.19, ...), custom_call_target="tpu_custom_call" | custom-call | tf_op jit(solution)/shard_map/pallas_call | solution.py:890
  432.8 0.8 copy-done.22
  433.6 0.9 fusion.1
  435.1 4.7 convolution_convert_fusion.6
  439.8 11.5 %shard_map.247 = (f32[8,16,128]{2,1,0:T(8,128)}, bf16[4,64,2048]{2,1,0:T(8,128)(2,1)}) custom-call(f32[16,128]{1,0:T(8,128)} %reshape.167.x, bf16[2,2,64,2048]{3,2,1,0:T(8,128)(2,1)} %bitcast.129), custom_call_target="tpu_custom_call" | custom-call | bytes 30000000 | tf_op jit(solution)/shard_map/pallas_call | solution.py:673
  451.3 0.9 reduce_sum.86
  452.2 2.3 multiply_convert_fusion.1
  455.3 4.9 convolution_convert_fusion.5
  460.3 5.3 all-to-all-start
  466.0 1.1 pad_maximum_fusion
  467.2 7.1 %convolution_convert_fusion.3 = bf16[1024,2048]{1,0:T(8,128)(2,1)} fusion(bf16[1024,768]{1,0:T(8,128)(2,1)S(1)} %pad_maximum_fusion, bf16[2048,768]{1,0:T(8,128)(2,1)} %all-gather.6.cloned.1.call-done), kind=kOutput, calls=%fused_computation.3 | convolution fusion | flops 3223322624 | bytes 8912896 | tf_op jit(solution)/shard_map/dot_general | solution.py:798
  474.3 1.8 reduce-scatter.7.cloned.1.call-done
  476.1 1.2 copy-done.9
  477.4 62.2 %shard_map.248 = (f32[128,2048]{1,0:T(8,128)S(1)}, f32[32,8,128]{2,1,0:T(8,128)S(1)}) custom-call(bf16[8,128,2048]{2,1,0:T(8,128)(2,1)} %bitcast.122, f32[128,2048]{1,0:T(8,128)S(1)} %copy-done.9, f32[32,8,128]{2,1,0:T(8,128)S(1)} %pad.12.terms), custom_call_target="tpu_custom_call" | custom-call | bytes 120000000 | tf_op jit(solution)/shard_map/pallas_call | solution.py:384
  539.6 2.2 shard_map.251
  541.8 20.8 %shard_map.249.slots = bf16[8,64,768]{2,1,0:T(8,128)(2,1)} custom-call(bf16[8,64,768]{2,1,0:T(8,128)(2,1)} %bitcast.132), custom_call_target="tpu_custom_call" | custom-call | bytes 60000000 | tf_op jit(solution)/shard_map/pallas_call | solution.py:692
  562.6 1.1 copy-done
  563.8 1.2 shard_map.250
  565.0 2.8 convert_element_type.66
  568.4 1.8 convert_element_type.65
  570.1 0.8 copy.49
  570.9 1.0 copy.50
  (113 shorter events, 6.6 us)
Async XLA Ops:
  7.2 106.6 %copy-start.24 = (s32[2,1,512]{2,1,0:T(1,128)S(1)}, s32[2,1,512]{2,1,0:T(1,128)}, u32[]{:S(2)}) copy-start(s32[2,1,512]{2,1,0:T(1,128)} %doc_k.3) | copy-start | bytes 12292
  7.2 108.5 %all-gather.4.cloned.1.call-start = ((), (), s32[]{:S(2)}) async-start(), calls=%async_computation.5 | async-start | bytes 5242880 | tf_op jit(solution)/shard_map/all_gather | solution.py:913
  7.9 109.3 %all-gather.6.cloned.1.call-start = ((), (), s32[]{:S(2)}) async-start(), calls=%async_computation.6 | async-start | bytes 3932160 | tf_op jit(solution)/shard_map/all_gather | solution.py:913
  29.7 187.9 %all-gather.8.cloned.1.call-start = ((), (), s32[]{:S(2)}) async-start(), calls=%async_computation.7 | async-start | bytes 10485760 | tf_op jit(solution)/shard_map/all_gather | solution.py:913
  112.7 308.1 %reduce-scatter.5.cloned.1.call-start = ((), (), s32[]{:S(2)}) async-start(), calls=%async_computation.8 | async-start | bytes 10485760 | tf_op jit(solution)/shard_map/reduce_scatter | solution.py:917
  123.3 1.7 copy-start.25
  135.9 9.0 %copy-start.29 = (bf16[2,2,64,2048]{3,2,1,0:T(8,128)(2,1)S(1)}, bf16[2,2,64,2048]{3,2,1,0:T(8,128)(2,1)}, u32[]{:S(2)}) copy-start(bf16[2,2,64,2048]{3,2,1,0:T(8,128)(2,1)} %get-tuple-element.67) | copy-start | bytes 3145732
  143.3 0.8 copy-start.14
  144.1 0.8 copy-start.5
  144.1 4.1 copy-start.7
  144.1 4.1 copy-start.16
  144.1 71.5 %copy-start.18 = (bf16[8,2,64,256]{3,2,1,0:T(8,128)(2,1)}, bf16[8,2,64,256]{3,2,1,0:T(8,128)(2,1)S(1)}, u32[]{:S(2)}) copy-start(bf16[8,2,64,256]{3,2,1,0:T(8,128)(2,1)S(1)} %get-tuple-element.76.v) | copy-start | bytes 1572868
  144.1 4.1 copy-start.1
  215.6 1.0 copy-start.10
  216.6 1.0 copy-start.12
  217.6 14.0 %copy-start.27 = (bf16[1024,2048]{1,0:T(8,128)(2,1)S(1)}, bf16[1024,2048]{1,0:T(8,128)(2,1)}, u32[]{:S(2)}) copy-start(bf16[1024,2048]{1,0:T(8,128)(2,1)} %all-gather.4.cloned.1.call-done.down_w) | copy-start | bytes 12582916
  231.5 6.1 %copy-start.3 = (bf16[2,1,64,2048]{3,2,1,0:T(8,128)(2,1)S(1)}, bf16[2,1,64,2048]{3,2,1,0:T(8,128)(2,1)}, u32[]{:S(2)}) copy-start(bf16[2,1,64,2048]{3,2,1,0:T(8,128)(2,1)} %param.16) | copy-start | bytes 1572868
  231.6 6.1 %copy-start.11 = (f32[128,2048]{1,0:T(8,128)S(1)}, f32[128,2048]{1,0:T(8,128)}, u32[]{:S(2)}) copy-start(f32[128,2048]{1,0:T(8,128)} %copy-done.10) | copy-start | bytes 3145732
  237.7 70.5 %copy-start.2 = (bf16[1024,1024]{1,0:T(8,128)(2,1)S(1)}, bf16[1024,1024]{1,0:T(8,128)(2,1)}, u32[]{:S(2)}) copy-start(bf16[1024,1024]{1,0:T(8,128)(2,1)} %get-tuple-element.80.swish) | copy-start | bytes 6291460
  308.2 10.2 %copy-start.20 = (bf16[128,2048]{1,0:T(8,128)(2,1)}, bf16[128,2048]{1,0:T(8,128)(2,1)S(1)}, u32[]{:S(2)}) copy-start(bf16[128,2048]{1,0:T(8,128)(2,1)S(1)} %get-tuple-element.73) | copy-start | bytes 1572868
  308.2 10.2 %copy-start.32 = (bf16[8,128,2048]{2,1,0:T(8,128)(2,1)S(1)}, bf16[8,128,2048]{2,1,0:T(8,128)(2,1)}, u32[]{:S(2)}) copy-start(bf16[8,128,2048]{2,1,0:T(8,128)(2,1)} %get-tuple-element.68) | copy-start | bytes 12582916
  331.8 144.3 %reduce-scatter.7.cloned.1.call-start = ((), (), s32[]{:S(2)}) async-start(), calls=%async_computation.9 | async-start | bytes 5242880 | tf_op jit(solution)/shard_map/reduce_scatter | solution.py:917
  331.8 14.0 %copy-start.4 = (bf16[2,1,64,2048]{3,2,1,0:T(8,128)(2,1)S(1)}, bf16[2,1,64,2048]{3,2,1,0:T(8,128)(2,1)}, u32[]{:S(2)}) copy-start(bf16[2,1,64,2048]{3,2,1,0:T(8,128)(2,1)} %param.16) | copy-start | bytes 1572868
  331.9 14.0 %copy-start.13 = (f32[128,2048]{1,0:T(8,128)S(1)}, f32[128,2048]{1,0:T(8,128)}, u32[]{:S(2)}) copy-start(f32[128,2048]{1,0:T(8,128)} %copy-done.12) | copy-start | bytes 3145732
  419.8 1.0 copy-start.8
  420.8 1.2 copy-start.30
  420.8 118.7 %reduce-scatter.9.cloned.1.call-start = ((), (), s32[]{:S(2)}) async-start(), calls=%async_computation.10 | async-start | bytes 3932160 | tf_op jit(solution)/shard_map/reduce_scatter | solution.py:917
  422.0 3.6 copy-start.15
  422.0 3.6 copy-start.17
  422.0 3.6 copy-start.19
  425.6 8.0 %copy-start.26 = (f32[1024,768]{1,0:T(8,128)S(1)}, f32[1024,768]{1,0:T(8,128)}, u32[]{:S(2)}) copy-start(f32[1024,768]{1,0:T(8,128)} %copy-done.25) | copy-start | bytes 9437188
  432.8 0.8 copy-start.22
  433.6 1.5 copy-start.6
  439.8 15.5 %copy-start.23 = (bf16[8,2,64,256]{3,2,1,0:T(8,128)(2,1)S(1)}, bf16[8,2,64,256]{3,2,1,0:T(8,128)(2,1)}, u32[]{:S(2)}) copy-start(bf16[8,2,64,256]{3,2,1,0:T(8,128)(2,1)} %copy-done.22) | copy-start | bytes 1572868
  452.2 3.1 copy-start.31
  454.5 0.8 copy-start.28
  460.3 79.3 %all-to-all-start = ((bf16[8,64,2048]{2,1,0:T(8,128)(2,1)}), bf16[8,64,2048]{2,1,0:T(8,128)(2,1)S(1)}, u32[]{:S(2)}, u32[]{:S(2)}) async-start(bf16[8,64,2048]{2,1,0:T(8,128)(2,1)} %bitcast.127), calls=%async_computation.4 | async-start | bytes 4194304 | tf_op jit(solution)/shard_map/all_to_all | solution.py:1033
  465.5 102.9 %reduce-scatter.11.cloned.1.call-start = ((), (), s32[]{:S(2)}) async-start(), calls=%async_computation.11 | async-start | bytes 1310720 | tf_op jit(solution)/shard_map/reduce_scatter | solution.py:917
  476.1 1.2 copy-start.9
  541.8 28.3 %copy-start.21 = (bf16[128,2048]{1,0:T(8,128)(2,1)S(1)}, bf16[128,2048]{1,0:T(8,128)(2,1)}, u32[]{:S(2)}) copy-start(bf16[128,2048]{1,0:T(8,128)(2,1)} %copy-done.20) | copy-start | bytes 1572868
  562.6 1.1 copy-start
Sparse Core Ops, SparseCore 0:
  9.9 62.5 all-gather.3
  74.3 42.8 all-gather.5
  119.0 87.5 all-gather.7
  331.9 88.2 reduce-scatter.4
  423.3 52.7 reduce-scatter.6
  479.0 45.0 reduce-scatter.8
  539.7 25.4 reduce-scatter.10

commit v7 on v6

--- a/solution.py
+++ b/solution.py
@@ -608,11 +608,13 @@
     for k in range(chunks):
         gather.start(k)
     own.start()
-    for other in others:
+    for other in others[:-1]:
         other.start()
     for d in range(1, line.nz):
         for k in range(chunks):
             gather.pass_on(d, k)
+            if (d, k) == (1, chunks // 2 - 1):
+                others[-1].start()
     gather.finish()
     own.wait()
     for other in others:

time: 588 us -> 588 us (level)
  no operation moved by 1% of the time
where the time goes in v7:
time: 588 us; the launch traced here: 579 us
  Pallas kernels  460 us (78%)
  matrix products  63.2 us (11%)
  local copies, waits for them, and re-layouts  16.7 us (3%)
  between operations  15.1 us (3%)
  other arithmetic  13.7 us (2%)
    pallas_call x3, Pallas kernels, around(): pl.pallas_call(functools.partial(around_kernel, n_s, chunks, rows_fn, len...  212 us
    pallas_call x1, Pallas kernels, second_exchange(): pl.pallas_call(functools.partial(second_kernel, n_w, n_s, chunks, plan, b...  81.7 us
    pallas_call x1, Pallas kernels, last_sum(): pl.pallas_call(functools.partial(last_kernel, n_w, n_s, chunks), out_shap...  62.1 us
    dot_general x3, matrix products, dot_t(): lax.dot_general(a, b, (((1,), (1,)), ((), ())), preferred_element_type=f32)  24.7 us
    dot_general x3, matrix products, t_dot(): lax.dot_general(a, b, (((0,), (0,)), ((), ())), preferred_element_type=f32)  23 us
    pallas_call x1, Pallas kernels, first_exchange(): pl.pallas_call(functools.partial(first_kernel, n_s, plan), out_shape=jax....  21.7 us
    pallas_call x1, Pallas kernels, final_exchange(): pl.pallas_call(functools.partial(final_kernel, n_w, n_s), out_shape=jax.S...  20.8 us
    dot_general x3, matrix products, dot(): return jnp.dot(a, b, preferred_element_type=f32)  15.5 us
  transfers between devices with their start and end apart: 8, of which 2 were waited for; matrix products, arithmetic and copies ran while one was open for 10% of the time, Pallas kernels for 63%

profile of v7, /device:TPU:9, one launch (start us, length us, event | category | flops | bytes accessed | tf_op | source)
XLA Modules:
  0.0 579.2 jit_solution(12118200761662240656)
XLA Ops:
  8.0 21.7 %shard_map.237 = bf16[8,64,768]{2,1,0:T(8,128)(2,1)} custom-call(bf16[64,2048]{1,0:T(8,128)(2,1)} %qw.1, bf16[64,2048]{1,0:T(8,128)(2,1)} %kw.1, bf16[64,2048]{1,0:T(8,128)(2,1)} %vw.1), custom_call_target="tpu_custom_call" | custom-call | bytes 60000000 | tf_op jit(solution)/shard_map/pallas_call | solution.py:533
  29.7 1.3 fusion.12.gain
  31.1 81.7 %shard_map.238 = (bf16[8,128,2048]{2,1,0:T(8,128)(2,1)}, bf16[8,64,2048]{2,1,0:T(8,128)(2,1)}, f32[32,8,128]{2,1,0:T(8,128)}, bf16[2,2,64,2048]{3,2,1,0:T(8,128)(2,1)}) custom-call(bf16[128,2048]{1,0:T(8,128)(2,1)} %bitcast.101, bf16[64,8192]{1,0:T(8,128)(2,1)} %gw.1, bf16[64,8192]{1,0:T(8,128)(2,1)} %uw.1, f32[8,128]{1,0:T(8,128)} %fusion.12.gain, ...), custom_call_target="tpu_custom_call" | custom-call | bytes 240000000 | tf_op jit(solution)/shard_map/pallas_call | solution.py:634
  112.8 0.9 slice_bitcast_fusion
  114.4 1.0 fusion.2
  115.7 1.5 all-gather.6.cloned.1.call-done
  117.2 6.1 %fusion.18 = f32[1024,768]{1,0:T(8,128)S(1)} fusion(bf16[1024,2048]{1,0:T(8,128)(2,1)} %bitcast.151, bf16[2048,768]{1,0:T(8,128)(2,1)} %all-gather.6.cloned.1.call-done), kind=kOutput, calls=%fused_computation.68 | convolution fusion | flops 3221225472 | bytes 10485760 | tf_op jit(solution)/shard_map/dot_general | solution.py:796
  123.3 1.6 copy-done.25
  125.9 8.9 %shard_map.239 = f32[8,16,128]{2,1,0:T(8,128)} custom-call(f32[16,128]{1,0:T(8,128)} %reshape.150.x_ref), custom_call_target="tpu_custom_call" | custom-call | bytes 30000000 | tf_op jit(solution)/shard_map/pallas_call | solution.py:490
  134.8 0.9 reduce_sum.83
  135.9 7.4 %shard_map.240 = (bf16[8,2,64,256]{3,2,1,0:T(8,128)(2,1)S(1)}, bf16[8,2,64,256]{3,2,1,0:T(8,128)(2,1)S(1)}, bf16[8,2,64,256]{3,2,1,0:T(8,128)(2,1)S(1)}, bf16[8,...) custom-call(f32[8,2,64,768]{3,2,1,0:T(8,128)} %bitcast.116, f32[8,2,64,768]{3,2,1,0:T(8,128)} %bitcast.117, ...), custom_call_target="tpu_custom_call" | custom-call | tf_op jit(solution)/shard_map/pallas_call | solution.py:878
  143.3 0.8 copy-done.14
  144.9 3.3 convolution_convert_fusion.2
  148.2 67.3 %shard_map.241 = (bf16[8,128,2048]{2,1,0:T(8,128)(2,1)}, f32[128,2048]{1,0:T(8,128)S(1)}, f32[128,2048]{1,0:T(8,128)S(1)}, f32[128,1]{1,0:T(8,128)S(1)}) custom-call(bf16[8,128,2048]{2,1,0:T(8,128)(2,1)} %bitcast.119, bf16[128,2048]{1,0:T(8,128)(2,1)S(1)} %bitcast.102, f32[1,2048]{1,0:T(1,128)S(1)} %slice.79.refs_2_.refs_4_), custom_call_target="tpu_custom_call" | custom-call | bytes 210000000 | tf_op jit(solution)/shard_map/pallas_call | solution.py:353
  215.6 1.0 copy-done.10
  216.5 1.0 copy-done.12
  217.5 14.0 %shard_map.242 = (bf16[1024,1024]{1,0:T(8,128)(2,1)S(1)}, bf16[1024,1024]{1,0:T(8,128)(2,1)S(1)}, bf16[1024,1024]{1,0:T(8,128)(2,1)}) custom-call(bf16[1024,2048]{1,0:T(8,128)(2,1)} %bitcast.155, bf16[2048,2048]{1,0:T(8,128)(2,1)} %all-gather.8.cloned.1.call-done.gate_w.up_w, bf16[2048,2048]{1,0:T(8,128)(2,1)} %all-gather.8.cloned.1.call-done.gate_w.up_w), custom_call_target="tpu_custom_call" | custom-call | flops 8589934592 | bytes 12582912 | tf_op jit(solution)/shard_map/pallas_call | solution.py:722
  231.5 6.1 %convolution_convert_fusion.4 = bf16[1024,2048]{1,0:T(8,128)(2,1)} fusion(bf16[1024,1024]{1,0:T(8,128)(2,1)S(1)} %get-tuple-element.70.refs_5_, bf16[1024,2048]{1,0:T(8,128)(2,1)S(1)} %copy-done.27), kind=kOutput, calls=%fused_computation.4 | convolution fusion | flops 4297064448 | bytes 10485760 | tf_op jit(solution)/shard_map/dot_general | solution.py:796
  237.6 70.6 %shard_map.243 = (bf16[8,128,2048]{2,1,0:T(8,128)(2,1)}, bf16[128,2048]{1,0:T(8,128)(2,1)S(1)}, f32[1,2048]{1,0:T(1,128)S(1)}) custom-call(bf16[8,128,2048]{2,1,0:T(8,128)(2,1)} %bitcast.123, f32[128,2048]{1,0:T(8,128)S(1)} %copy-done.11, bf16[128,2048]{1,0:T(8,128)(2,1)S(1)} %bitcast.103, f32[1,2048]{1,0:T(1,128)S(1)} %slice.81.refs_3_), custom_call_target="tpu_custom_call" | custom-call | bytes 210000000 | tf_op jit(solution)/shard_map/pallas_call | solution.py:353
  308.2 10.1 %shard_map.244 = bf16[1024,2048]{1,0:T(8,128)(2,1)} custom-call(bf16[1024,2048]{1,0:T(8,128)(2,1)} %bitcast.120, bf16[1024,2048]{1,0:T(8,128)(2,1)} %all-gather.4.cloned.1.call-done.down_w, bf16[1024,1024]{1,0:T(8,128)(2,1)S(1)} %get-tuple-element.79.slope, bf16[1024,1024]{1,0:T(8,128)(2,1)S(1)} %copy-done.2), custom_call_target="tpu_custom_call" | custom-call | flops 4294967296 | bytes 8388608 | tf_op jit(solution)/shard_map/pallas_call | solution.py:750
  318.3 13.4 %convolution_convert_fusion = bf16[2048,2048]{1,0:T(8,128)(2,1)} fusion(bf16[1024,2048]{1,0:T(8,128)(2,1)S(1)} %bitcast.156, bf16[1024,2048]{1,0:T(8,128)(2,1)} %shard_map.244), kind=kOutput, calls=%fused_computation | convolution fusion | flops 8594128896 | bytes 16777216 | tf_op jit(solution)/shard_map/dot_general | solution.py:804
  331.8 14.0 %convolution_convert_fusion.1 = bf16[1024,2048]{1,0:T(8,128)(2,1)} fusion(bf16[1024,2048]{1,0:T(8,128)(2,1)} %shard_map.244, bf16[2048,2048]{1,0:T(8,128)(2,1)} %all-gather.8.cloned.1.call-done.gate_w.up_w), kind=kOutput, calls=%fused_computation.1 | convolution fusion | flops 8592031744 | bytes 16777216 | tf_op jit(solution)/shard_map/dot_general | solution.py:800
  345.9 74.0 %shard_map.245 = (bf16[8,128,2048]{2,1,0:T(8,128)(2,1)}, f32[128,2048]{1,0:T(8,128)S(1)}, f32[1,2048]{1,0:T(1,128)S(1)}, bf16[1024,2048]{1,0:T(8,128)(2,1)}) custom-call(bf16[8,128,2048]{2,1,0:T(8,128)(2,1)} %bitcast.124, bf16[128,2048]{1,0:T(8,128)(2,1)S(1)} %bitcast.104, f32[128,2048]{1,0:T(8,128)S(1)} %copy-done.13, ...), custom_call_target="tpu_custom_call" | custom-call | bytes 210000000 | tf_op jit(solution)/shard_map/pallas_call | solution.py:353
  419.8 1.0 copy-done.8
  420.9 1.1 copy-done.30
  422.0 3.6 convolution_convert_fusion.7
  425.7 7.1 %shard_map.246 = (f32[8,2,64,256]{3,2,1,0:T(8,128)S(1)}, f32[8,2,64,256]{3,2,1,0:T(8,128)S(1)}, bf16[8,2,64,256]{3,2,1,0:T(8,128)(2,1)S(1)}) custom-call(bf16[8,2,64,256]{3,2,1,0:T(8,128)(2,1)S(1)} %copy-done.15, bf16[8,2,64,256]{3,2,1,0:T(8,128)(2,1)S(1)} %copy-done.17, bf16[8,2,64,256]{3,2,1,0:T(8,128)(2,1)S(1)} %copy-done.19, ...), custom_call_target="tpu_custom_call" | custom-call | tf_op jit(solution)/shard_map/pallas_call | solution.py:892
  432.8 0.8 copy-done.22
  433.6 0.9 fusion.1
  435.1 4.7 convolution_convert_fusion.6
  439.8 11.4 %shard_map.247 = (f32[8,16,128]{2,1,0:T(8,128)}, bf16[4,64,2048]{2,1,0:T(8,128)(2,1)}) custom-call(f32[16,128]{1,0:T(8,128)} %reshape.167.x, bf16[2,2,64,2048]{3,2,1,0:T(8,128)(2,1)} %bitcast.129), custom_call_target="tpu_custom_call" | custom-call | bytes 30000000 | tf_op jit(solution)/shard_map/pallas_call | solution.py:675
  451.3 0.9 reduce_sum.86
  452.2 2.3 multiply_convert_fusion.1
  455.3 4.9 convolution_convert_fusion.5
  460.2 5.3 all-to-all-start
  466.0 1.1 pad_maximum_fusion
  467.2 7.1 %convolution_convert_fusion.3 = bf16[1024,2048]{1,0:T(8,128)(2,1)} fusion(bf16[1024,768]{1,0:T(8,128)(2,1)S(1)} %pad_maximum_fusion, bf16[2048,768]{1,0:T(8,128)(2,1)} %all-gather.6.cloned.1.call-done), kind=kOutput, calls=%fused_computation.3 | convolution fusion | flops 3223322624 | bytes 8912896 | tf_op jit(solution)/shard_map/dot_general | solution.py:800
  474.3 1.9 reduce-scatter.7.cloned.1.call-done
  476.2 1.2 copy-done.9
  477.4 62.1 %shard_map.248 = (f32[128,2048]{1,0:T(8,128)S(1)}, f32[32,8,128]{2,1,0:T(8,128)S(1)}) custom-call(bf16[8,128,2048]{2,1,0:T(8,128)(2,1)} %bitcast.122, f32[128,2048]{1,0:T(8,128)S(1)} %copy-done.9, f32[32,8,128]{2,1,0:T(8,128)S(1)} %pad.12.terms), custom_call_target="tpu_custom_call" | custom-call | bytes 120000000 | tf_op jit(solution)/shard_map/pallas_call | solution.py:384
  539.6 2.2 shard_map.251
  541.8 20.8 %shard_map.249.slots = bf16[8,64,768]{2,1,0:T(8,128)(2,1)} custom-call(bf16[8,64,768]{2,1,0:T(8,128)(2,1)} %bitcast.132), custom_call_target="tpu_custom_call" | custom-call | bytes 60000000 | tf_op jit(solution)/shard_map/pallas_call | solution.py:694
  562.6 1.1 copy-done
  563.7 1.2 shard_map.250
  565.0 2.8 convert_element_type.66
  568.3 1.8 convert_element_type.65
  570.1 0.8 copy.49
  570.9 1.0 copy.50
  (113 shorter events, 6.6 us)
Async XLA Ops:
  7.2 106.7 %copy-start.24 = (s32[2,1,512]{2,1,0:T(1,128)S(1)}, s32[2,1,512]{2,1,0:T(1,128)}, u32[]{:S(2)}) copy-start(s32[2,1,512]{2,1,0:T(1,128)} %doc_k.3) | copy-start | bytes 12292
  7.2 108.5 %all-gather.4.cloned.1.call-start = ((), (), s32[]{:S(2)}) async-start(), calls=%async_computation.5 | async-start | bytes 5242880 | tf_op jit(solution)/shard_map/all_gather | solution.py:915
  7.9 109.3 %all-gather.6.cloned.1.call-start = ((), (), s32[]{:S(2)}) async-start(), calls=%async_computation.6 | async-start | bytes 3932160 | tf_op jit(solution)/shard_map/all_gather | solution.py:915
  29.7 187.8 %all-gather.8.cloned.1.call-start = ((), (), s32[]{:S(2)}) async-start(), calls=%async_computation.7 | async-start | bytes 10485760 | tf_op jit(solution)/shard_map/all_gather | solution.py:915
  112.7 308.1 %reduce-scatter.5.cloned.1.call-start = ((), (), s32[]{:S(2)}) async-start(), calls=%async_computation.8 | async-start | bytes 10485760 | tf_op jit(solution)/shard_map/reduce_scatter | solution.py:919
  123.3 1.7 copy-start.25
  135.9 9.0 %copy-start.29 = (bf16[2,2,64,2048]{3,2,1,0:T(8,128)(2,1)S(1)}, bf16[2,2,64,2048]{3,2,1,0:T(8,128)(2,1)}, u32[]{:S(2)}) copy-start(bf16[2,2,64,2048]{3,2,1,0:T(8,128)(2,1)} %get-tuple-element.67) | copy-start | bytes 3145732
  143.3 0.8 copy-start.14
  144.1 0.8 copy-start.5
  144.1 4.1 copy-start.7
  144.1 4.1 copy-start.16
  144.1 71.4 %copy-start.18 = (bf16[8,2,64,256]{3,2,1,0:T(8,128)(2,1)}, bf16[8,2,64,256]{3,2,1,0:T(8,128)(2,1)S(1)}, u32[]{:S(2)}) copy-start(bf16[8,2,64,256]{3,2,1,0:T(8,128)(2,1)S(1)} %get-tuple-element.76.v) | copy-start | bytes 1572868
  144.1 4.1 copy-start.1
  215.5 1.0 copy-start.10
  216.5 1.0 copy-start.12
  217.5 14.0 %copy-start.27 = (bf16[1024,2048]{1,0:T(8,128)(2,1)S(1)}, bf16[1024,2048]{1,0:T(8,128)(2,1)}, u32[]{:S(2)}) copy-start(bf16[1024,2048]{1,0:T(8,128)(2,1)} %all-gather.4.cloned.1.call-done.down_w) | copy-start | bytes 12582916
  231.5 6.1 %copy-start.3 = (bf16[2,1,64,2048]{3,2,1,0:T(8,128)(2,1)S(1)}, bf16[2,1,64,2048]{3,2,1,0:T(8,128)(2,1)}, u32[]{:S(2)}) copy-start(bf16[2,1,64,2048]{3,2,1,0:T(8,128)(2,1)} %param.16) | copy-start | bytes 1572868
  231.5 6.1 %copy-start.11 = (f32[128,2048]{1,0:T(8,128)S(1)}, f32[128,2048]{1,0:T(8,128)}, u32[]{:S(2)}) copy-start(f32[128,2048]{1,0:T(8,128)} %copy-done.10) | copy-start | bytes 3145732
  237.6 70.6 %copy-start.2 = (bf16[1024,1024]{1,0:T(8,128)(2,1)S(1)}, bf16[1024,1024]{1,0:T(8,128)(2,1)}, u32[]{:S(2)}) copy-start(bf16[1024,1024]{1,0:T(8,128)(2,1)} %get-tuple-element.80.swish) | copy-start | bytes 6291460
  308.1 10.2 %copy-start.20 = (bf16[128,2048]{1,0:T(8,128)(2,1)}, bf16[128,2048]{1,0:T(8,128)(2,1)S(1)}, u32[]{:S(2)}) copy-start(bf16[128,2048]{1,0:T(8,128)(2,1)S(1)} %get-tuple-element.73) | copy-start | bytes 1572868
  308.2 10.2 %copy-start.32 = (bf16[8,128,2048]{2,1,0:T(8,128)(2,1)S(1)}, bf16[8,128,2048]{2,1,0:T(8,128)(2,1)}, u32[]{:S(2)}) copy-start(bf16[8,128,2048]{2,1,0:T(8,128)(2,1)} %get-tuple-element.68) | copy-start | bytes 12582916
  331.8 144.4 %reduce-scatter.7.cloned.1.call-start = ((), (), s32[]{:S(2)}) async-start(), calls=%async_computation.9 | async-start | bytes 5242880 | tf_op jit(solution)/shard_map/reduce_scatter | solution.py:919
  331.8 14.0 %copy-start.4 = (bf16[2,1,64,2048]{3,2,1,0:T(8,128)(2,1)S(1)}, bf16[2,1,64,2048]{3,2,1,0:T(8,128)(2,1)}, u32[]{:S(2)}) copy-start(bf16[2,1,64,2048]{3,2,1,0:T(8,128)(2,1)} %param.16) | copy-start | bytes 1572868
  331.8 14.0 %copy-start.13 = (f32[128,2048]{1,0:T(8,128)S(1)}, f32[128,2048]{1,0:T(8,128)}, u32[]{:S(2)}) copy-start(f32[128,2048]{1,0:T(8,128)} %copy-done.12) | copy-start | bytes 3145732
  419.8 1.0 copy-start.8
  420.8 1.2 copy-start.30
  420.8 118.7 %reduce-scatter.9.cloned.1.call-start = ((), (), s32[]{:S(2)}) async-start(), calls=%async_computation.10 | async-start | bytes 3932160 | tf_op jit(solution)/shard_map/reduce_scatter | solution.py:919
  422.0 3.6 copy-start.15
  422.0 3.6 copy-start.17
  422.0 3.6 copy-start.19
  425.6 8.0 %copy-start.26 = (f32[1024,768]{1,0:T(8,128)S(1)}, f32[1024,768]{1,0:T(8,128)}, u32[]{:S(2)}) copy-start(f32[1024,768]{1,0:T(8,128)} %copy-done.25) | copy-start | bytes 9437188
  432.8 0.8 copy-start.22
  433.6 1.5 copy-start.6
  439.8 15.5 %copy-start.23 = (bf16[8,2,64,256]{3,2,1,0:T(8,128)(2,1)S(1)}, bf16[8,2,64,256]{3,2,1,0:T(8,128)(2,1)}, u32[]{:S(2)}) copy-start(bf16[8,2,64,256]{3,2,1,0:T(8,128)(2,1)} %copy-done.22) | copy-start | bytes 1572868
  452.2 3.1 copy-start.31
  454.5 0.8 copy-start.28
  460.2 79.3 %all-to-all-start = ((bf16[8,64,2048]{2,1,0:T(8,128)(2,1)}), bf16[8,64,2048]{2,1,0:T(8,128)(2,1)S(1)}, u32[]{:S(2)}, u32[]{:S(2)}) async-start(bf16[8,64,2048]{2,1,0:T(8,128)(2,1)} %bitcast.127), calls=%async_computation.4 | async-start | bytes 4194304 | tf_op jit(solution)/shard_map/all_to_all | solution.py:1035
  465.5 102.9 %reduce-scatter.11.cloned.1.call-start = ((), (), s32[]{:S(2)}) async-start(), calls=%async_computation.11 | async-start | bytes 1310720 | tf_op jit(solution)/shard_map/reduce_scatter | solution.py:919
  476.2 1.2 copy-start.9
  541.8 28.3 %copy-start.21 = (bf16[128,2048]{1,0:T(8,128)(2,1)S(1)}, bf16[128,2048]{1,0:T(8,128)(2,1)}, u32[]{:S(2)}) copy-start(bf16[128,2048]{1,0:T(8,128)(2,1)} %copy-done.20) | copy-start | bytes 1572868
  562.6 1.1 copy-start
Sparse Core Ops, SparseCore 0:
  9.9 62.5 all-gather.3
  74.3 42.8 all-gather.5
  119.0 87.6 all-gather.7
  331.9 88.3 reduce-scatter.4
  423.3 52.7 reduce-scatter.6
  479.0 44.9 reduce-scatter.8
  539.7 25.4 reduce-scatter.10
